TPU v7x, 32 devices: a whole 2x2x4 slice. The times are simulated.
32 devices in a mesh: groups: 1, tensor: 16 (over z, y, core), replica: 2 (over x).
Axes of the slice: x: 2, y: 2, z: 4, core: 2. Of those that a mesh axis runs over, the one named last changes fastest.
Arguments:
- q_latent: bfloat16 [256, 1536], P(('groups', 'tensor', 'replica')), may hold values from -6 to 6
- q_gain: float32 [1536], replicated, may hold values from 0.25 to 1.75
- q_up: bfloat16 [1536, 12288], P(None, 'tensor'), may hold values from -0.15625 to 0.15625
- w_uk: bfloat16 [64, 128, 512], P('tensor'), may hold values from -0.5 to 0.5
- w_uv: bfloat16 [64, 512, 128], P('tensor'), may hold values from -1 to 1
- w_o: bfloat16 [8192, 7168], P('tensor', 'replica'), may hold values from -0.0625 to 0.0625
- new_kv: bfloat16 [256, 576], P(('groups', 'tensor', 'replica')), may hold values from -6 to 6
- latent_cache: bfloat16 [64, 1024, 576], P(('groups', 'tensor', 'replica')), may hold values from -64 to 64
- cache_len: int32 [64], P(('groups', 'tensor', 'replica')), may hold values from 128 to 1024, as said below
- draft_count: int32 [64], P(('groups', 'tensor', 'replica')), may hold values from 1 to 4, as said below
Outputs:
- attn_out: bfloat16 [256, 7168], P(('groups', 'tensor', 'replica'))
Inputs may be any that keep to these rules, and one draw needn't show every extreme that they name: `cache_len`: some request of every draw uses all 1024 slots. The first draft_count rows of a request are in use; some request of every draw uses all 4.
All inputs are finite; a program needn't handle non-finite values.
Results may differ from a plain program's by a relative error of at most 0.024.
The roundings to bfloat16 on the way count: a program that leaves them out, or rounds other values in their place, can miss the bound.
Values may be sent and summed in bfloat16 or wider, within the bound.
No kernel may reach another device: no remote copies, remote signals or barrier semaphores. Data moves between devices by JAX's collectives and lax.ppermute only.
A program may use at most 64 MiB of HBM per device.

v0:
```python
import functools

import jax
import jax.numpy as jnp
from jax import lax
from jax.experimental import pallas as pl
from jax.experimental.pallas import tpu as pltpu
from jax.sharding import PartitionSpec as P


LATENT = 512
ROPE = 64
NOPE = 128
VDIM = 128
QKD = NOPE + ROPE
LANES = 128

FETCH_VMEM = 53_700_000
HALVES_VMEM = 51_000_000

rms_eps = 1e-06
rope_base = 50000.0

VMEM = pltpu.MemorySpace.VMEM
SMEM = pltpu.MemorySpace.SMEM
bf16 = jnp.bfloat16
f32 = jnp.float32


def vmem_spec():
    return pl.BlockSpec(memory_space=VMEM)


def smem_spec():
    return pl.BlockSpec(memory_space=SMEM)


def over(x, n):
    return x >> (n.bit_length() - 1) if n & (n - 1) == 0 else x // n


def rest(x, n):
    return x & (n - 1) if n & (n - 1) == 0 else x % n


def mm(a, b):
    return jnp.dot(a, b, preferred_element_type=f32)


def mm_nt(a, b):
    return lax.dot_general(a, b, (((1,), (1,)), ((), ())), preferred_element_type=f32)


def fetch_kernel(*refs):
    count = len(refs) // 2
    copies = [pltpu.make_async_copy(refs[i], refs[count + i], refs[-1].at[i]) for i in range(count)]
    for copy in copies:
        copy.start()
    for copy in copies:
        copy.wait()


def fetch(arrays, limit):
    return pl.pallas_call(
        fetch_kernel,
        out_shape=[pltpu.VMEM(x.shape, x.dtype) for x in arrays],
        in_specs=[pl.BlockSpec(memory_space=pl.ANY)] * len(arrays),
        out_specs=[vmem_spec()] * len(arrays),
        scratch_shapes=[pltpu.SemaphoreType.DMA((len(arrays),))],
        compiler_params=pltpu.CompilerParams(vmem_limit_bytes=limit),
        cost_estimate=pl.CostEstimate(
            flops=0, bytes_accessed=sum(4 * x.size for x in arrays), transcendentals=0
        ),
    )(*arrays)


def halves_kernel(place_ref, *refs):
    *sources, first, second, sems = refs
    copies = []
    for i, target in enumerate((first, second)):
        source, width = sources[i], target.shape[1]
        if source.shape[1] != width:
            source = source.at[:, pl.ds(pl.multiple_of(place_ref[0] * width, LANES), width)]
        copies.append(pltpu.make_async_copy(source, target, sems.at[i]))
        copies[i].start()
    for copy in copies:
        copy.wait()


def fetch_halves(place, arrays, width):
    depth = arrays[0].shape[0]
    return pl.pallas_call(
        halves_kernel,
        out_shape=[pltpu.VMEM((depth, width), bf16)] * 2,
        in_specs=[smem_spec()] + [pl.BlockSpec(memory_space=pl.ANY)] * 2,
        out_specs=[vmem_spec()] * 2,
        scratch_shapes=[pltpu.SemaphoreType.DMA((2,))],
        compiler_params=pltpu.CompilerParams(vmem_limit_bytes=HALVES_VMEM),
        cost_estimate=pl.CostEstimate(flops=0, bytes_accessed=8 * depth * width, transcendentals=0),
        name="near_output",
    )(place, *arrays)


def regroup(pieces, groups, size):
    assert groups == 2 and len(pieces) % 2 == 0
    rows = lax.broadcasted_iota(jnp.int32, pieces[0].shape, 0)
    low = rest(over(rows, size), 2) == 0
    total = pieces[0].shape[0]
    width = pieces[0].shape[1]
    firsts, seconds = [], []
    for h in range(0, len(pieces), 2):
        a, b = pieces[h], pieces[h + 1]
        firsts.append(jnp.where(low, a, pltpu.roll(b, size, 0)))
        seconds.append(jnp.where(low, pltpu.roll(a, total - size, 0), b))

    def stack(parts):
        parts = [part.reshape(total // (2 * size), 2 * size, width) for part in parts]
        return jnp.concatenate(parts, axis=1).reshape(total * len(parts), width)

    return [stack(firsts), stack(seconds)]


def query_kernel(reqs, drafts, heads, place_ref, *refs):
    *x_refs, gain_ref, up_ref, uk_ref, out_ref = refs
    owners = out_ref.shape[0]
    hd = heads * drafts
    x = jnp.concatenate([x_ref[...] for x_ref in x_refs], axis=0).astype(f32)
    scaled = x * lax.rsqrt(jnp.mean(x * x, axis=-1, keepdims=True) + rms_eps)
    normed = (scaled * gain_ref[...][None, :]).astype(bf16)
    full = mm(normed, up_ref[...]).astype(bf16)
    absorbed = [mm(full[:, h * QKD : h * QKD + NOPE], uk_ref[h * NOPE : (h + 1) * NOPE]) for h in range(heads)]
    rope = [full[:, h * QKD + NOPE : (h + 1) * QKD].astype(f32) for h in range(heads)]
    absorbed = regroup(absorbed, reqs, drafts)
    rope = regroup(rope, reqs, drafts)
    chunks = LATENT // LANES
    per = LANES // ROPE
    absorbed = [x.reshape(owners, hd, LATENT).astype(bf16) for x in absorbed]
    rope = [
        jnp.concatenate(rope[b * per : (b + 1) * per], axis=-1).reshape(owners, hd, LANES).astype(bf16)
        for b in range(reqs // per)
    ]
    for k in range(owners):
        distance = int(format(k, f"0{owners.bit_length() - 1}b")[::-1], 2)
        target = place_ref[2] ^ distance
        for q in range(reqs):
            for c in range(chunks):
                at = (q * chunks + c) * hd
                out_ref[target, at : at + hd, :] = absorbed[q][k, :, c * LANES : (c + 1) * LANES]
        for b in range(reqs // per):
            at = (reqs * chunks + b) * hd
            out_ref[target, at : at + hd, :] = rope[b][k]


def attend_kernel(reqs, drafts, heads, len_ref, count_ref, q_ref, cos_ref, sin_ref, new_ref, cache_ref, out_ref):
    owners = q_ref.shape[0]
    hd = heads * drafts
    count = owners * hd
    chunks = LATENT // LANES
    per = LANES // ROPE
    slots = cache_ref.shape[2]
    scale = QKD ** (-0.5)
    rotated = []
    for b in range(reqs // per):
        at = (reqs * chunks + b) * hd
        x = q_ref[:, at : at + hd, :].astype(f32).reshape(count, LANES)
        lane = rest(lax.broadcasted_iota(jnp.int32, x.shape, 1), ROPE)
        half = ROPE // 2
        other = jnp.where(lane < half, pltpu.roll(x, LANES - half, 1), pltpu.roll(x, half, 1))
        x = x.reshape(owners, hd, LANES) * cos_ref[b] + other.reshape(owners, hd, LANES) * sin_ref[b]
        x = x.astype(bf16).reshape(count, LANES)
        rotated += [x[:, i * ROPE : (i + 1) * ROPE] for i in range(per)]
    draft = rest(lax.broadcasted_iota(jnp.int32, (count, 1), 0), drafts)
    new_at = lax.broadcasted_iota(jnp.int32, (count, new_ref.shape[0]), 1)
    slot = lax.broadcasted_iota(jnp.int32, (1, slots), 1)
    for q in range(reqs):
        absorbed = jnp.concatenate(
            [
                q_ref[:, (q * chunks + c) * hd : (q * chunks + c + 1) * hd, :].reshape(count, LANES)
                for c in range(chunks)
            ],
            axis=-1,
        )
        keys = cache_ref[q]
        rows = new_ref[...]
        score = (mm(absorbed, keys[:LATENT]) + mm(rotated[q], keys[LATENT:])) * scale
        fresh = (mm_nt(absorbed, rows[:, :LATENT]) + mm_nt(rotated[q], rows[:, LATENT:])) * scale
        score = jnp.where(slot < len_ref[q], score, -jnp.inf)
        seen = (new_at >= q * drafts) & (new_at - q * drafts <= draft)
        fresh = jnp.where(seen, fresh, -jnp.inf)
        peak = jnp.maximum(
            jnp.max(score, axis=1, keepdims=True), jnp.max(fresh, axis=1, keepdims=True)
        )
        score = jnp.exp(score - peak)
        fresh = jnp.exp(fresh - peak)
        total = jnp.sum(score, axis=1, keepdims=True) + jnp.sum(fresh, axis=1, keepdims=True)
        inverse = 1.0 / total
        mix = mm_nt((score * inverse).astype(bf16), keys[:LATENT])
        mix = mix + mm((fresh * inverse).astype(bf16), rows[:, :LATENT])
        mix = jnp.where(draft < count_ref[q], mix, 0.0).astype(bf16)
        out_ref[:, q * hd : (q + 1) * hd, :] = mix.reshape(owners, hd, LATENT)


def value_kernel(drafts, heads, latent_ref, uv_ref, out_ref):
    owners = latent_ref.shape[0]
    hd = heads * drafts
    pair = 2 * drafts
    rows = owners * pair
    low = rest(over(lax.broadcasted_iota(jnp.int32, (rows, LATENT), 0), drafts), 2) == 0
    for h in range(0, heads, 2):
        a = latent_ref[:, h * drafts : h * drafts + pair, :].astype(f32).reshape(rows, LATENT)
        b = latent_ref[:, hd + h * drafts : hd + h * drafts + pair, :].astype(f32).reshape(rows, LATENT)
        first = jnp.where(low, a, pltpu.roll(b, drafts, 0)).astype(bf16)
        second = jnp.where(low, pltpu.roll(a, rows - drafts, 0), b).astype(bf16)
        out_ref[:, h * VDIM : (h + 1) * VDIM] = mm(first, uv_ref[h]).astype(bf16)
        out_ref[:, (h + 1) * VDIM : (h + 2) * VDIM] = mm(second, uv_ref[h + 1]).astype(bf16)


def output_kernel(place_ref, *refs):
    *value_refs, w_own_ref, w_other_ref, out_ref = refs
    replicas, rows, half = out_ref.shape
    own = jnp.concatenate([ref[...] for ref in value_refs[:replicas]], axis=0)
    other = jnp.concatenate([ref[...] for ref in value_refs[replicas:]], axis=0)
    tile = 256 if half % 256 == 0 else half
    for at in range(0, half, tile):
        part = mm(own, w_own_ref[:, at : at + tile]) + mm(other, w_other_ref[:, at : at + tile])
        part = part.astype(bf16)
        for k in range(replicas):
            out_ref[place_ref[1] ^ k, :, at : at + tile] = part[k * rows : (k + 1) * rows]


def sum_kernel(replicas, pairs, x_ref, out_ref):
    width = x_ref.shape[-1]
    for r in range(replicas):
        for c in range(2):
            total = None
            for p in range(pairs):
                part = x_ref[(r * pairs + p) * 2 + c].astype(f32)
                total = part if total is None else total + part
            at = (r * 2 + c) * width
            out_ref[:, at : at + width] = total.astype(bf16)


def step(x, axis, size, k):
    return lax.ppermute(x, axis, [(i, i ^ k) for i in range(size)])


def local_step(q_latent, q_gain, q_up, w_uk, w_uv, w_o, new_kv, latent_cache, cache_len, draft_count):
    rows_dev, _ = q_latent.shape
    owners = lax.axis_size("tensor")
    replicas = lax.axis_size("replica")
    heads = w_uk.shape[0]
    reqs = cache_len.shape[0]
    drafts = rows_dev // reqs
    hd = heads * drafts
    me = lax.axis_index("tensor")
    core = me % 2

    place = jnp.stack([core, lax.axis_index("replica"), me]).astype(jnp.int32)
    w_uk = w_uk.reshape(heads * NOPE, LATENT)
    near = fetch((q_up, w_uk, q_gain, q_latent), FETCH_VMEM)

    frequency = rope_base ** (-(jnp.arange(ROPE // 2).astype(f32) * 2.0 / ROPE))
    positions = (cache_len[:, None] + jnp.arange(drafts)[None, :]).astype(f32)
    angles = positions[:, :, None] * frequency
    per = LANES // ROPE

    def table(first, second):
        lanes = jnp.concatenate([first, second], axis=-1)
        lanes = lanes.reshape(reqs // per, per, drafts, ROPE)
        lanes = jnp.swapaxes(lanes, 1, 2).reshape(reqs // per, 1, drafts, LANES)
        return jnp.broadcast_to(lanes, (reqs // per, heads, drafts, LANES)).reshape(reqs // per, hd, LANES)

    cosine = jnp.cos(angles)
    sine = jnp.sin(angles)
    tables = table(cosine, cosine), table(-sine, sine)

    first = step(q_latent, "tensor", owners, owners // 2)
    first, q_up, w_uk, gain, rows, *tables = lax.optimization_barrier((first, *near, *tables))
    rows = jnp.concatenate([rows, first], axis=0)
    bit = owners // 4
    while bit > 2:
        rows = jnp.concatenate([rows, step(rows, "tensor", owners, bit)], axis=0)
        bit //= 2
    parts = [rows]
    while bit:
        parts = parts + [step(part, "tensor", owners, bit) for part in parts]
        bit //= 2

    chunks = LATENT // LANES
    packed = (reqs * chunks + reqs * ROPE // LANES) * hd
    params = pltpu.CompilerParams(vmem_limit_bytes=24 * 1024 * 1024)
    queries = pl.pallas_call(
        functools.partial(query_kernel, reqs, drafts, heads),
        out_shape=jax.ShapeDtypeStruct((owners, packed, LANES), bf16),
        in_specs=[smem_spec()] + [vmem_spec()] * (len(parts) + 3),
        out_specs=vmem_spec(),
        compiler_params=params,
        name="query",
    )(place, *parts, gain, q_up, w_uk)
    arrived = lax.all_to_all(queries, "tensor", split_axis=0, concat_axis=0, tiled=True)

    arrived, w_late = lax.optimization_barrier((arrived, w_o))

    half = w_o.shape[1] // 2
    aligned = half % LANES == 0
    w_own = w_o if aligned else lax.dynamic_slice_in_dim(w_o, core * half, half, axis=1)
    w_away = w_late if aligned else lax.dynamic_slice_in_dim(w_late, (1 - core) * half, half, axis=1)
    w_other = step(w_away, "tensor", owners, 1)

    latent = pl.pallas_call(
        functools.partial(attend_kernel, reqs, drafts, heads),
        out_shape=jax.ShapeDtypeStruct((owners, reqs * hd, LATENT), bf16),
        in_specs=[smem_spec()] * 2 + [vmem_spec()] * 5,
        out_specs=vmem_spec(),
        compiler_params=params,
        name="attend",
    )(cache_len, draft_count, arrived, *tables, new_kv, jnp.swapaxes(latent_cache, 1, 2))
    returned = lax.all_to_all(latent, "tensor", split_axis=0, concat_axis=0, tiled=True)
    returned, w_other = lax.optimization_barrier((returned, w_other))

    values = pl.pallas_call(
        functools.partial(value_kernel, drafts, heads),
        out_shape=jax.ShapeDtypeStruct((owners * rows_dev, heads * VDIM), bf16),
        in_specs=[vmem_spec()] * 2,
        out_specs=vmem_spec(),
        compiler_params=params,
        name="values",
    )(returned, w_uv)
    nearest = step(values, "replica", replicas, 1)
    own = [values, nearest] + [step(values, "replica", replicas, k) for k in range(2, replicas)]
    w_own, w_other = fetch_halves(place, (w_own, w_other), half)
    other = [step(piece, "tensor", owners, 1) for piece in own]

    product = pl.pallas_call(
        output_kernel,
        out_shape=jax.ShapeDtypeStruct((replicas, owners * rows_dev, half), bf16),
        in_specs=[smem_spec()] + [vmem_spec()] * (2 * replicas + 2),
        out_specs=vmem_spec(),
        compiler_params=params,
        name="output",
    )(place, *own, *other, w_own, w_other)
    product = product.reshape(replicas * owners, rows_dev, half)
    placed = lax.all_to_all(product, ("replica", "tensor"), split_axis=0, concat_axis=0, tiled=True)
    return pl.pallas_call(
        functools.partial(sum_kernel, replicas, owners // 2),
        out_shape=jax.ShapeDtypeStruct((rows_dev, replicas * 2 * half), bf16),
        in_specs=[vmem_spec()],
        out_specs=vmem_spec(),
        compiler_params=params,
        name="combine",
    )(placed)


def solution(mesh):
    rows = ("groups", "tensor", "replica")
    return jax.shard_map(
        local_step,
        mesh=mesh,
        in_specs=(
            P(rows, None),
            P(),
            P(None, "tensor"),
            P("tensor", None, None),
            P("tensor", None, None),
            P("tensor", "replica"),
            P(rows, None),
            P(rows, None, None),
            P(rows),
            P(rows),
        ),
        out_specs=P(rows, None),
        check_vma=False,
    )
```

profile of v0, /device:TPU:0, one launch (start us, length us, event | category | flops | bytes accessed | tf_op | source)
XLA Modules:
  0.0 101.2 jit_solution(14414973885834010614)
XLA Ops:
  0.0 4.1 %collective-permute-start = (bf16[8,1536]{1,0:T(8,128)(2,1)}, bf16[8,1536]{1,0:T(8,128)(2,1)S(1)}, u32[]{:S(2)}, u32[]{:S(2)}) collective-permute-start(bf16[8,1536]{1,0:T(8,128)(2,1)} %refs_3_.1), channel_id=1, source_target_pairs={{0,16},{2,18},{4,20},{6,22},{8,24},{10,26},{12,28},{14,30},{16,0},... | collective-permute-start | bytes 73736 | tf_op jit(solution)/shard_map/ppermute | solution.py:244
  4.1 0.7 add_convert_fusion
  4.7 0.1 fusion
  4.9 0.1 maximum_bitcast_fusion
  5.0 0.1 broadcast_in_dim.22
  5.0 0.1 broadcast_in_dim.25
  5.1 1.8 %shard_map.100 = (bf16[1536,768]{1,0:T(8,128)(2,1)S(1)}, bf16[512,512]{1,0:T(8,128)(2,1)S(1)}, f32[1536]{0:T(1024)S(1)}, bf16[8,1536]{1,0:T(8,128)(2,1)S(1)}) custom-call(bf16[1536,768]{1,0:T(8,128)(2,1)} %refs_0_.2, bf16[512,512]{1,0:T(8,128)(2,1)} %bitcast.20, f32[1536]{0:T(1024)} %refs_2_.1, bf16[8,1536]{1,0:T(8,128)(2,1)} %refs_3_.1), custom_call_target="tpu_custom_call" | custom-call | bytes 5822464 | tf_op jit(solution)/shard_map/pallas_call | solution.py:64
  6.9 0.0 collective-permute-done
  7.0 1.6 %collective-permute-start.1 = (bf16[16,1536]{1,0:T(8,128)(2,1)S(1)}, bf16[16,1536]{1,0:T(8,128)(2,1)S(1)}, u32[]{:S(2)}, u32[]{:S(2)}) collective-permute-start(bf16[16,1536]{1,0:T(8,128)(2,1)S(1)} %pad_maximum_fusion), channel_id=1, source_target_pairs={{0,8},{2,10},{4,12},{6,14},{8,0},{10,2},{12,4},{14,6},{16,24},{18,... | collective-permute-start | bytes 147464 | tf_op jit(solution)/shard_map/ppermute | solution.py:244
  8.6 2.5 %collective-permute-done.1 = bf16[16,1536]{1,0:T(8,128)(2,1)S(1)} collective-permute-done((bf16[16,1536]{1,0:T(8,128)(2,1)S(1)}, bf16[16,1536]{1,0:T(8,128)(2,1)S(1)}, u32[]{:S(2)}, u32[]{:S(2)}) %collective-permute-start.1) | collective-permute-done | bytes 49184 | tf_op jit(solution)/shard_map/ppermute | solution.py:244
  11.2 1.5 %collective-permute-start.2 = (bf16[32,1536]{1,0:T(8,128)(2,1)S(1)}, bf16[32,1536]{1,0:T(8,128)(2,1)S(1)}, u32[]{:S(2)}, u32[]{:S(2)}) collective-permute-start(bf16[32,1536]{1,0:T(8,128)(2,1)S(1)} %constant_dynamic-update-slice_fusion.refs_0_), channel_id=1, source_target_pairs={{0,4},{2,6},{4,0},{6,2},{8,12},{10,14},{12,8},{14,10},{16,20},{18,... | collective-permute-start | bytes 294920 | tf_op jit(solution)/shard_map/ppermute | solution.py:244
  12.7 0.0 collective-permute-start.3
  12.7 3.1 %collective-permute-done.2.refs_1_ = bf16[32,1536]{1,0:T(8,128)(2,1)S(1)} collective-permute-done((bf16[32,1536]{1,0:T(8,128)(2,1)S(1)}, bf16[32,1536]{1,0:T(8,128)(2,1)S(1)}, u32[]{:S(2)}, u32[]{:S(2)}) %collective-permute-start.2) | collective-permute-done | bytes 98336 | tf_op jit(solution)/shard_map/ppermute | solution.py:244
  15.8 0.0 collective-permute-start.4
  15.8 0.1 pad_add_fusion.place_ref
  15.9 0.0 collective-permute-done.3.refs_2_
  15.9 1.2 %collective-permute-done.4.refs_3_ = bf16[32,1536]{1,0:T(8,128)(2,1)S(1)} collective-permute-done((bf16[32,1536]{1,0:T(8,128)(2,1)S(1)}, bf16[32,1536]{1,0:T(8,128)(2,1)S(1)}, u32[]{:S(2)}, u32[]{:S(2)}) %collective-permute-start.4) | collective-permute-done | bytes 98336 | tf_op jit(solution)/shard_map/ppermute | solution.py:244
  17.1 1.5 %query.1 = bf16[16,144,128]{2,1,0:T(8,128)(2,1)S(1)} custom-call(s32[3]{0:T(128)S(1)} %pad_add_fusion.place_ref, bf16[32,1536]{1,0:T(8,128)(2,1)S(1)} %constant_dynamic-update-slice_fusion.refs_0_, bf16[32,1536]{1,0:T(8,128)(2,1)S(1)} %collective-permute-done.2.refs_1_, bf16[32,1536]{1,0:T(8,128)(2,1)S(1)} %collective-permute-done.3.refs_2_, ...), custom_call_target="tpu_custom_call" | custom-call | tf_op jit(solution)/shard_map/query/pallas_call | solution.py:292
  18.6 22.6 %all_to_all.15.q_ref = bf16[16,144,128]{2,1,0:T(8,128)(2,1)S(1)} all-to-all(bf16[16,144,128]{2,1,0:T(8,128)(2,1)S(1)} %query.1), channel_id=1, replica_groups=mesh['groups'=1,'tensor'=16,'replica'=2] {'tensor'}, dimensions={0} | all-to-all | bytes 1179648 | tf_op jit(solution)/shard_map/all_to_all | solution.py:300
  41.2 0.1 collective-permute-start.5
  41.3 3.2 %attend.1 = bf16[16,32,512]{2,1,0:T(8,128)(2,1)S(1)} custom-call(s32[2]{0:T(128)S(1)} %copy-done.3, s32[2]{0:T(128)S(1)} %copy-done.4, bf16[16,144,128]{2,1,0:T(8,128)(2,1)S(1)} %all_to_all.15.q_ref, f32[1,16,128]{2,1,0:T(8,128)S(1)} %bitcast.19, f32[1,16,128]{2,1,0:T(8,128)S(1)} %bitcast.18, bf16[8,576]{1,0:T(8,128)(2,1)S(1)} %copy-done.2, ...), custom_call_target="tpu_custom_call" | custom-call | tf_op jit(solution)/shard_map/attend/pallas_call | solution.py:310
  44.5 17.1 %all_to_all.16.latent_ref = bf16[16,32,512]{2,1,0:T(8,128)(2,1)S(1)} all-to-all(bf16[16,32,512]{2,1,0:T(8,128)(2,1)S(1)} %attend.1), channel_id=1, replica_groups=mesh['groups'=1,'tensor'=16,'replica'=2] {'tensor'}, dimensions={0} | all-to-all | bytes 1048576 | tf_op jit(solution)/shard_map/all_to_all | solution.py:318
  61.6 0.0 collective-permute-done.5.refs_1_
  61.6 0.3 values.1.refs_0_
  61.9 1.6 %collective-permute-start.6 = (bf16[128,512]{1,0:T(8,128)(2,1)S(1)}, bf16[128,512]{1,0:T(8,128)(2,1)S(1)}, u32[]{:S(2)}, u32[]{:S(2)}) collective-permute-start(bf16[128,512]{1,0:T(8,128)(2,1)S(1)} %values.1.refs_0_), channel_id=1, source_target_pairs={{0,1},{1,0},{2,3},{3,2},{4,5},{5,4},{6,7},{7,6},{8,9},{9,8},{10,11... | collective-permute-start | bytes 393224 | tf_op jit(solution)/shard_map/ppermute | solution.py:244
  63.5 4.0 %collective-permute-done.6.refs_1_ = bf16[128,512]{1,0:T(8,128)(2,1)S(1)} collective-permute-done((bf16[128,512]{1,0:T(8,128)(2,1)S(1)}, bf16[128,512]{1,0:T(8,128)(2,1)S(1)}, u32[]{:S(2)}, u32[]{:S(2)}) %collective-permute-start.6) | collective-permute-done | bytes 131104 | tf_op jit(solution)/shard_map/ppermute | solution.py:244
  67.5 0.0 collective-permute-start.8
  67.5 2.6 %near_output.1 = (bf16[512,1792]{1,0:T(8,128)(2,1)S(1)}, bf16[512,1792]{1,0:T(8,128)(2,1)S(1)}) custom-call(s32[3]{0:T(128)S(1)} %pad_add_fusion.place_ref, bf16[512,3584]{1,0:T(8,128)(2,1)} %refs_0_.3, bf16[512,3584]{1,0:T(8,128)(2,1)} %copy-done.5), custom_call_target="tpu_custom_call" | custom-call | bytes 7340032 | tf_op jit(solution)/shard_map/near_output/pallas_call | solution.py:92
  70.2 0.0 collective-permute-done.8.refs_3_
  70.2 1.7 %output.1 = bf16[2,128,1792]{2,1,0:T(8,128)(2,1)S(1)} custom-call(s32[3]{0:T(128)S(1)} %pad_add_fusion.place_ref, bf16[128,512]{1,0:T(8,128)(2,1)S(1)} %values.1.refs_0_, bf16[128,512]{1,0:T(8,128)(2,1)S(1)} %collective-permute-done.6.refs_1_, bf16[128,512]{1,0:T(8,128)(2,1)S(1)} %collective-permute-done.7.refs_2_, ...), custom_call_target="tpu_custom_call" | custom-call | tf_op jit(solution)/shard_map/output/pallas_call | solution.py:334
  71.8 28.6 %all_to_all.17.x_ref = bf16[32,8,1792]{2,1,0:T(8,128)(2,1)S(1)} all-to-all(bf16[32,8,1792]{2,1,0:T(8,128)(2,1)S(1)} %bitcast.16), channel_id=1, replica_groups=mesh['groups'=1,'tensor'=16,'replica'=2] {'replica','tensor'}, dimensions={0} | all-to-all | bytes 1835008 | tf_op jit(solution)/shard_map/all_to_all | solution.py:343
  100.4 0.8 combine.1
  (21 shorter events, 0.1 us)
Async XLA Ops:
  0.0 6.9 %collective-permute-start = (bf16[8,1536]{1,0:T(8,128)(2,1)}, bf16[8,1536]{1,0:T(8,128)(2,1)S(1)}, u32[]{:S(2)}, u32[]{:S(2)}) collective-permute-start(bf16[8,1536]{1,0:T(8,128)(2,1)} %refs_3_.1), channel_id=1, source_target_pairs={{0,16},{2,18},{4,20},{6,22},{8,24},{10,26},{12,28},{14,30},{16,0},... | collective-permute-start | bytes 73736 | tf_op jit(solution)/shard_map/ppermute | solution.py:244
  7.0 4.2 %collective-permute-start.1 = (bf16[16,1536]{1,0:T(8,128)(2,1)S(1)}, bf16[16,1536]{1,0:T(8,128)(2,1)S(1)}, u32[]{:S(2)}, u32[]{:S(2)}) collective-permute-start(bf16[16,1536]{1,0:T(8,128)(2,1)S(1)} %pad_maximum_fusion), channel_id=1, source_target_pairs={{0,8},{2,10},{4,12},{6,14},{8,0},{10,2},{12,4},{14,6},{16,24},{18,... | collective-permute-start | bytes 147464 | tf_op jit(solution)/shard_map/ppermute | solution.py:244
  11.2 4.6 %collective-permute-start.2 = (bf16[32,1536]{1,0:T(8,128)(2,1)S(1)}, bf16[32,1536]{1,0:T(8,128)(2,1)S(1)}, u32[]{:S(2)}, u32[]{:S(2)}) collective-permute-start(bf16[32,1536]{1,0:T(8,128)(2,1)S(1)} %constant_dynamic-update-slice_fusion.refs_0_), channel_id=1, source_target_pairs={{0,4},{2,6},{4,0},{6,2},{8,12},{10,14},{12,8},{14,10},{16,20},{18,... | collective-permute-start | bytes 294920 | tf_op jit(solution)/shard_map/ppermute | solution.py:244
  12.7 3.2 %collective-permute-start.3 = (bf16[32,1536]{1,0:T(8,128)(2,1)S(1)}, bf16[32,1536]{1,0:T(8,128)(2,1)S(1)}, u32[]{:S(2)}, u32[]{:S(2)}) collective-permute-start(bf16[32,1536]{1,0:T(8,128)(2,1)S(1)} %constant_dynamic-update-slice_fusion.refs_0_), channel_id=1, source_target_pairs={{0,2},{2,0},{4,6},{6,4},{8,10},{10,8},{12,14},{14,12},{16,18},{18,... | collective-permute-start | bytes 294920 | tf_op jit(solution)/shard_map/ppermute | solution.py:244
  15.8 1.3 %collective-permute-start.4 = (bf16[32,1536]{1,0:T(8,128)(2,1)S(1)}, bf16[32,1536]{1,0:T(8,128)(2,1)S(1)}, u32[]{:S(2)}, u32[]{:S(2)}) collective-permute-start(bf16[32,1536]{1,0:T(8,128)(2,1)S(1)} %collective-permute-done.2.refs_1_), channel_id=1, source_target_pairs={{0,2},{2,0},{4,6},{6,4},{8,10},{10,8},{12,14},{14,12},{16,18},{18,... | collective-permute-start | bytes 294920 | tf_op jit(solution)/shard_map/ppermute | solution.py:244
  15.8 25.4 %copy-start = (bf16[2,1024,576]{1,2,0:T(8,128)(2,1)S(1)}, bf16[2,1024,576]{1,2,0:T(8,128)(2,1)}, u32[]{:S(2)}) copy-start(bf16[2,1024,576]{1,2,0:T(8,128)(2,1)} %param.17) | copy-start | bytes 7077892
  15.9 25.4 %copy-start.2 = (bf16[8,576]{1,0:T(8,128)(2,1)S(1)}, bf16[8,576]{1,0:T(8,128)(2,1)}, u32[]{:S(2)}) copy-start(bf16[8,576]{1,0:T(8,128)(2,1)} %new_ref.1) | copy-start | bytes 27652
  15.9 25.4 %copy-start.3 = (s32[2]{0:T(128)S(1)}, s32[2]{0:T(128)}, u32[]{:S(2)}) copy-start(s32[2]{0:T(128)} %len_ref.1) | copy-start | bytes 28
  15.9 25.4 %copy-start.4 = (s32[2]{0:T(128)S(1)}, s32[2]{0:T(128)}, u32[]{:S(2)}) copy-start(s32[2]{0:T(128)} %count_ref.1) | copy-start | bytes 28
  41.2 20.4 %copy-start.1 = (bf16[4,512,128]{2,1,0:T(8,128)(2,1)S(1)}, bf16[4,512,128]{2,1,0:T(8,128)(2,1)}, u32[]{:S(2)}) copy-start(bf16[4,512,128]{2,1,0:T(8,128)(2,1)} %uv_ref.1) | copy-start | bytes 1572868
  41.2 20.4 %collective-permute-start.5 = (bf16[512,3584]{1,0:T(8,128)(2,1)}, bf16[512,3584]{1,0:T(8,128)(2,1)S(1)}, u32[]{:S(2)}, u32[]{:S(2)}) collective-permute-start(bf16[512,3584]{1,0:T(8,128)(2,1)} %refs_0_.3), channel_id=1, source_target_pairs={{0,2},{2,0},{4,6},{6,4},{8,10},{10,8},{12,14},{14,12},{16,18},{18,... | collective-permute-start | bytes 11010056 | tf_op jit(solution)/shard_map/ppermute | solution.py:244
  61.6 6.0 %copy-start.5 = (bf16[512,3584]{1,0:T(8,128)(2,1)}, bf16[512,3584]{1,0:T(8,128)(2,1)S(1)}, u32[]{:S(2)}) copy-start(bf16[512,3584]{1,0:T(8,128)(2,1)S(1)} %collective-permute-done.5.refs_1_) | copy-start | bytes 11010052
  61.9 5.6 %collective-permute-start.6 = (bf16[128,512]{1,0:T(8,128)(2,1)S(1)}, bf16[128,512]{1,0:T(8,128)(2,1)S(1)}, u32[]{:S(2)}, u32[]{:S(2)}) collective-permute-start(bf16[128,512]{1,0:T(8,128)(2,1)S(1)} %values.1.refs_0_), channel_id=1, source_target_pairs={{0,1},{1,0},{2,3},{3,2},{4,5},{5,4},{6,7},{7,6},{8,9},{9,8},{10,11... | collective-permute-start | bytes 393224 | tf_op jit(solution)/shard_map/ppermute | solution.py:244
  63.5 6.7 %collective-permute-start.7 = (bf16[128,512]{1,0:T(8,128)(2,1)S(1)}, bf16[128,512]{1,0:T(8,128)(2,1)S(1)}, u32[]{:S(2)}, u32[]{:S(2)}) collective-permute-start(bf16[128,512]{1,0:T(8,128)(2,1)S(1)} %values.1.refs_0_), channel_id=1, source_target_pairs={{0,2},{2,0},{4,6},{6,4},{8,10},{10,8},{12,14},{14,12},{16,18},{18,... | collective-permute-start | bytes 393224 | tf_op jit(solution)/shard_map/ppermute | solution.py:244
  67.5 2.6 %collective-permute-start.8 = (bf16[128,512]{1,0:T(8,128)(2,1)S(1)}, bf16[128,512]{1,0:T(8,128)(2,1)S(1)}, u32[]{:S(2)}, u32[]{:S(2)}) collective-permute-start(bf16[128,512]{1,0:T(8,128)(2,1)S(1)} %collective-permute-done.6.refs_1_), channel_id=1, source_target_pairs={{0,2},{2,0},{4,6},{6,4},{8,10},{10,8},{12,14},{14,12},{16,18},{18,... | collective-permute-start | bytes 393224 | tf_op jit(solution)/shard_map/ppermute | solution.py:244
where the time goes:
time: 101 us
  blocking collectives  68.2 us (68%)
  Pallas kernels  11.9 us (12%)
  waiting for transfers between devices  10.9 us (11%)
  starting transfers between devices  8.91 us (9%)
    all_to_all x1, blocking collectives, local_step(): lax.all_to_all(product, ('replica', 'tensor'), split_axis=0, concat_axis=...  28.6 us
    all_to_all x1, blocking collectives, local_step(): lax.all_to_all(queries, 'tensor', split_axis=0, concat_axis=0, tiled=True)  22.6 us
    all_to_all x1, blocking collectives, local_step(): lax.all_to_all(latent, 'tensor', split_axis=0, concat_axis=0, tiled=True)  17.1 us
    ppermute x9, waiting for transfers between devices, step(): return lax.ppermute(x, axis, [(i, i ^ k) for i in range(size)])  10.9 us
    ppermute x9, starting transfers between devices, step(): return lax.ppermute(x, axis, [(i, i ^ k) for i in range(size)])  8.91 us
    pallas_call x1, Pallas kernels, local_step(): pl.pallas_call(functools.partial(attend_kernel, reqs, drafts, heads), out...  3.18 us
    pallas_call x1, Pallas kernels, fetch_halves(): pl.pallas_call(halves_kernel, out_shape=[pltpu.VMEM((depth, width), bf16)...  2.61 us
  transfers between devices with their start and end apart: 9, of which 4 were waited for; matrix products, arithmetic and copies ran while one was open for 1% of the time, Pallas kernels for 7%

commit v1 on v0

--- a/solution.py
+++ b/solution.py
@@ -151,7 +151,7 @@
             out_ref[target, at : at + hd, :] = rope[b][k]
 
 
-def attend_kernel(reqs, drafts, heads, len_ref, count_ref, q_ref, cos_ref, sin_ref, new_ref, cache_ref, out_ref):
+def attend_kernel(reqs, drafts, heads, len_ref, count_ref, q_ref, frequency_ref, new_ref, cache_ref, out_ref):
     owners = q_ref.shape[0]
     hd = heads * drafts
     count = owners * hd
@@ -163,10 +163,18 @@
     for b in range(reqs // per):
         at = (reqs * chunks + b) * hd
         x = q_ref[:, at : at + hd, :].astype(f32).reshape(count, LANES)
-        lane = rest(lax.broadcasted_iota(jnp.int32, x.shape, 1), ROPE)
         half = ROPE // 2
-        other = jnp.where(lane < half, pltpu.roll(x, LANES - half, 1), pltpu.roll(x, half, 1))
-        x = x.reshape(owners, hd, LANES) * cos_ref[b] + other.reshape(owners, hd, LANES) * sin_ref[b]
+        low = rest(lax.broadcasted_iota(jnp.int32, x.shape, 1), ROPE) < half
+        other = jnp.where(low, pltpu.roll(x, LANES - half, 1), pltpu.roll(x, half, 1))
+        lane = lax.broadcasted_iota(jnp.int32, (hd, LANES), 1)
+        length = jnp.zeros_like(lane)
+        for i in range(per):
+            length = jnp.where(over(lane, ROPE) == i, len_ref[b * per + i], length)
+        position = length + rest(lax.broadcasted_iota(jnp.int32, (hd, LANES), 0), drafts)
+        angle = position.astype(f32) * frequency_ref[...]
+        sine = jnp.sin(angle)
+        sine = jnp.where(rest(lane, ROPE) < half, -sine, sine)
+        x = x.reshape(owners, hd, LANES) * jnp.cos(angle) + other.reshape(owners, hd, LANES) * sine
         x = x.astype(bf16).reshape(count, LANES)
         rotated += [x[:, i * ROPE : (i + 1) * ROPE] for i in range(per)]
     draft = rest(lax.broadcasted_iota(jnp.int32, (count, 1), 0), drafts)
@@ -259,23 +267,11 @@
     w_uk = w_uk.reshape(heads * NOPE, LATENT)
     near = fetch((q_up, w_uk, q_gain, q_latent), FETCH_VMEM)
 
-    frequency = rope_base ** (-(jnp.arange(ROPE // 2).astype(f32) * 2.0 / ROPE))
-    positions = (cache_len[:, None] + jnp.arange(drafts)[None, :]).astype(f32)
-    angles = positions[:, :, None] * frequency
-    per = LANES // ROPE
-
-    def table(first, second):
-        lanes = jnp.concatenate([first, second], axis=-1)
-        lanes = lanes.reshape(reqs // per, per, drafts, ROPE)
-        lanes = jnp.swapaxes(lanes, 1, 2).reshape(reqs // per, 1, drafts, LANES)
-        return jnp.broadcast_to(lanes, (reqs // per, heads, drafts, LANES)).reshape(reqs // per, hd, LANES)
-
-    cosine = jnp.cos(angles)
-    sine = jnp.sin(angles)
-    tables = table(cosine, cosine), table(-sine, sine)
+    lane_pair = jnp.arange(LANES) % (ROPE // 2)
+    frequency = (rope_base ** (-(lane_pair.astype(f32) * 2.0 / ROPE)))[None, :]
 
     first = step(q_latent, "tensor", owners, owners // 2)
-    first, q_up, w_uk, gain, rows, *tables = lax.optimization_barrier((first, *near, *tables))
+    first, q_up, w_uk, gain, rows, frequency = lax.optimization_barrier((first, *near, frequency))
     rows = jnp.concatenate([rows, first], axis=0)
     bit = owners // 4
     while bit > 2:
@@ -310,11 +306,11 @@
     latent = pl.pallas_call(
         functools.partial(attend_kernel, reqs, drafts, heads),
         out_shape=jax.ShapeDtypeStruct((owners, reqs * hd, LATENT), bf16),
-        in_specs=[smem_spec()] * 2 + [vmem_spec()] * 5,
+        in_specs=[smem_spec()] * 2 + [vmem_spec()] * 4,
         out_specs=vmem_spec(),
         compiler_params=params,
         name="attend",
-    )(cache_len, draft_count, arrived, *tables, new_kv, jnp.swapaxes(latent_cache, 1, 2))
+    )(cache_len, draft_count, arrived, frequency, new_kv, jnp.swapaxes(latent_cache, 1, 2))
     returned = lax.all_to_all(latent, "tensor", split_axis=0, concat_axis=0, tiled=True)
     returned, w_other = lax.optimization_barrier((returned, w_other))
 

time: 101 us -> 101 us (level)
  transfers between devices with their start and end apart: 9 -> 9, of which waited for: 4 -> 5; matrix products, arithmetic and copies ran while one was open for 1% -> 0% of each run, Pallas kernels for 7% -> 8%
where the time goes in v1:
time: 101 us
  blocking collectives  69.1 us (68%)
  Pallas kernels  11.9 us (12%)
  waiting for transfers between devices  10.3 us (10%)
  starting transfers between devices  9.69 us (10%)
    all_to_all x1, blocking collectives, local_step(): lax.all_to_all(product, ('replica', 'tensor'), split_axis=0, concat_axis=...  28.6 us
    all_to_all x1, blocking collectives, local_step(): lax.all_to_all(queries, 'tensor', split_axis=0, concat_axis=0, tiled=True)  23.4 us
    all_to_all x1, blocking collectives, local_step(): lax.all_to_all(latent, 'tensor', split_axis=0, concat_axis=0, tiled=True)  17.1 us
    ppermute x9, waiting for transfers between devices, step(): return lax.ppermute(x, axis, [(i, i ^ k) for i in range(size)])  10.3 us
    ppermute x9, starting transfers between devices, step(): return lax.ppermute(x, axis, [(i, i ^ k) for i in range(size)])  9.69 us
    pallas_call x1, Pallas kernels, local_step(): pl.pallas_call(functools.partial(attend_kernel, reqs, drafts, heads), out...  3.19 us
    pallas_call x1, Pallas kernels, fetch_halves(): pl.pallas_call(halves_kernel, out_shape=[pltpu.VMEM((depth, width), bf16)...  2.61 us
  transfers between devices with their start and end apart: 9, of which 5 were waited for; matrix products, arithmetic and copies ran while one was open for 0% of the time, Pallas kernels for 8%

profile of v1, /device:TPU:0, one launch (start us, length us, event | category | flops | bytes accessed | tf_op | source)
XLA Modules:
  0.0 101.2 jit_solution(13613424260673965439)
XLA Ops:
  0.0 4.1 %collective-permute-start = (bf16[8,1536]{1,0:T(8,128)(2,1)}, bf16[8,1536]{1,0:T(8,128)(2,1)S(1)}, u32[]{:S(2)}, u32[]{:S(2)}) collective-permute-start(bf16[8,1536]{1,0:T(8,128)(2,1)} %refs_3_.1), channel_id=1, source_target_pairs={{0,16},{2,18},{4,20},{6,22},{8,24},{10,26},{12,28},{14,30},{16,0},... | collective-permute-start | bytes 73736 | tf_op jit(solution)/shard_map/ppermute | solution.py:252
  4.1 1.8 %shard_map.100 = (bf16[1536,768]{1,0:T(8,128)(2,1)S(1)}, bf16[512,512]{1,0:T(8,128)(2,1)S(1)}, f32[1536]{0:T(1024)S(1)}, bf16[8,1536]{1,0:T(8,128)(2,1)S(1)}) custom-call(bf16[1536,768]{1,0:T(8,128)(2,1)} %refs_0_.2, bf16[512,512]{1,0:T(8,128)(2,1)} %bitcast.8, f32[1536]{0:T(1024)} %refs_2_.1, bf16[8,1536]{1,0:T(8,128)(2,1)} %refs_3_.1), custom_call_target="tpu_custom_call" | custom-call | bytes 5822464 | tf_op jit(solution)/shard_map/pallas_call | solution.py:64
  5.9 0.2 collective-permute-done
  6.1 2.0 %collective-permute-start.1 = (bf16[16,1536]{1,0:T(8,128)(2,1)S(1)}, bf16[16,1536]{1,0:T(8,128)(2,1)S(1)}, u32[]{:S(2)}, u32[]{:S(2)}) collective-permute-start(bf16[16,1536]{1,0:T(8,128)(2,1)S(1)} %pad_maximum_fusion), channel_id=1, source_target_pairs={{0,8},{2,10},{4,12},{6,14},{8,0},{10,2},{12,4},{14,6},{16,24},{18,... | collective-permute-start | bytes 147464 | tf_op jit(solution)/shard_map/ppermute | solution.py:252
  8.1 2.2 %collective-permute-done.1 = bf16[16,1536]{1,0:T(8,128)(2,1)S(1)} collective-permute-done((bf16[16,1536]{1,0:T(8,128)(2,1)S(1)}, bf16[16,1536]{1,0:T(8,128)(2,1)S(1)}, u32[]{:S(2)}, u32[]{:S(2)}) %collective-permute-start.1) | collective-permute-done | bytes 49184 | tf_op jit(solution)/shard_map/ppermute | solution.py:252
  10.3 2.0 %collective-permute-start.2 = (bf16[32,1536]{1,0:T(8,128)(2,1)S(1)}, bf16[32,1536]{1,0:T(8,128)(2,1)S(1)}, u32[]{:S(2)}, u32[]{:S(2)}) collective-permute-start(bf16[32,1536]{1,0:T(8,128)(2,1)S(1)} %constant_dynamic-update-slice_fusion.refs_0_), channel_id=1, source_target_pairs={{0,4},{2,6},{4,0},{6,2},{8,12},{10,14},{12,8},{14,10},{16,20},{18,... | collective-permute-start | bytes 294920 | tf_op jit(solution)/shard_map/ppermute | solution.py:252
  12.2 0.0 collective-permute-start.3
  12.2 2.6 %collective-permute-done.2.refs_1_ = bf16[32,1536]{1,0:T(8,128)(2,1)S(1)} collective-permute-done((bf16[32,1536]{1,0:T(8,128)(2,1)S(1)}, bf16[32,1536]{1,0:T(8,128)(2,1)S(1)}, u32[]{:S(2)}, u32[]{:S(2)}) %collective-permute-start.2) | collective-permute-done | bytes 98336 | tf_op jit(solution)/shard_map/ppermute | solution.py:252
  14.9 0.0 collective-permute-start.4
  14.9 0.1 pad_add_fusion.place_ref
  15.0 0.0 collective-permute-done.3.refs_2_
  15.0 1.2 %collective-permute-done.4.refs_3_ = bf16[32,1536]{1,0:T(8,128)(2,1)S(1)} collective-permute-done((bf16[32,1536]{1,0:T(8,128)(2,1)S(1)}, bf16[32,1536]{1,0:T(8,128)(2,1)S(1)}, u32[]{:S(2)}, u32[]{:S(2)}) %collective-permute-start.4) | collective-permute-done | bytes 98336 | tf_op jit(solution)/shard_map/ppermute | solution.py:252
  16.2 1.5 %query.1 = bf16[16,144,128]{2,1,0:T(8,128)(2,1)S(1)} custom-call(s32[3]{0:T(128)S(1)} %pad_add_fusion.place_ref, bf16[32,1536]{1,0:T(8,128)(2,1)S(1)} %constant_dynamic-update-slice_fusion.refs_0_, bf16[32,1536]{1,0:T(8,128)(2,1)S(1)} %collective-permute-done.2.refs_1_, bf16[32,1536]{1,0:T(8,128)(2,1)S(1)} %collective-permute-done.3.refs_2_, ...), custom_call_target="tpu_custom_call" | custom-call | tf_op jit(solution)/shard_map/query/pallas_call | solution.py:288
  17.7 23.4 %all_to_all.15.q_ref = bf16[16,144,128]{2,1,0:T(8,128)(2,1)S(1)} all-to-all(bf16[16,144,128]{2,1,0:T(8,128)(2,1)S(1)} %query.1), channel_id=1, replica_groups=mesh['groups'=1,'tensor'=16,'replica'=2] {'tensor'}, dimensions={0} | all-to-all | bytes 1179648 | tf_op jit(solution)/shard_map/all_to_all | solution.py:296
  41.1 0.1 collective-permute-start.5
  41.3 0.0 copy-done
  41.3 0.0 copy-done.2
  41.3 0.0 copy-done.4
  41.3 3.2 %attend.1 = bf16[16,32,512]{2,1,0:T(8,128)(2,1)S(1)} custom-call(s32[2]{0:T(128)S(1)} %copy-done.3, s32[2]{0:T(128)S(1)} %copy-done.4, bf16[16,144,128]{2,1,0:T(8,128)(2,1)S(1)} %all_to_all.15.q_ref, f32[1,128]{1,0:T(1,128)S(1)} %fusion.3.frequency_ref, bf16[8,576]{1,0:T(8,128)(2,1)S(1)} %copy-done.2, bf16[2,576,1024]{2,1,0:T(8,128)(2,1)S(1)} %bitcast.7), custom_call_target="tpu_custom_call" | custom-call | tf_op jit(solution)/shard_map/attend/pallas_call | solution.py:306
  44.5 17.1 %all_to_all.16.latent_ref = bf16[16,32,512]{2,1,0:T(8,128)(2,1)S(1)} all-to-all(bf16[16,32,512]{2,1,0:T(8,128)(2,1)S(1)} %attend.1), channel_id=1, replica_groups=mesh['groups'=1,'tensor'=16,'replica'=2] {'tensor'}, dimensions={0} | all-to-all | bytes 1048576 | tf_op jit(solution)/shard_map/all_to_all | solution.py:314
  61.5 0.0 collective-permute-done.5.refs_1_
  61.6 0.3 values.1.refs_0_
  61.9 1.6 %collective-permute-start.6 = (bf16[128,512]{1,0:T(8,128)(2,1)S(1)}, bf16[128,512]{1,0:T(8,128)(2,1)S(1)}, u32[]{:S(2)}, u32[]{:S(2)}) collective-permute-start(bf16[128,512]{1,0:T(8,128)(2,1)S(1)} %values.1.refs_0_), channel_id=1, source_target_pairs={{0,1},{1,0},{2,3},{3,2},{4,5},{5,4},{6,7},{7,6},{8,9},{9,8},{10,11... | collective-permute-start | bytes 393224 | tf_op jit(solution)/shard_map/ppermute | solution.py:252
  63.5 0.0 collective-permute-start.7
  63.5 4.1 %collective-permute-done.6.refs_1_ = bf16[128,512]{1,0:T(8,128)(2,1)S(1)} collective-permute-done((bf16[128,512]{1,0:T(8,128)(2,1)S(1)}, bf16[128,512]{1,0:T(8,128)(2,1)S(1)}, u32[]{:S(2)}, u32[]{:S(2)}) %collective-permute-start.6) | collective-permute-done | bytes 131104 | tf_op jit(solution)/shard_map/ppermute | solution.py:252
  67.5 0.0 collective-permute-start.8
  67.5 2.6 %near_output.1 = (bf16[512,1792]{1,0:T(8,128)(2,1)S(1)}, bf16[512,1792]{1,0:T(8,128)(2,1)S(1)}) custom-call(s32[3]{0:T(128)S(1)} %pad_add_fusion.place_ref, bf16[512,3584]{1,0:T(8,128)(2,1)} %refs_0_.3, bf16[512,3584]{1,0:T(8,128)(2,1)} %copy-done.5), custom_call_target="tpu_custom_call" | custom-call | bytes 7340032 | tf_op jit(solution)/shard_map/near_output/pallas_call | solution.py:92
  70.1 0.0 collective-permute-done.7.refs_2_
  70.2 0.0 collective-permute-done.8.refs_3_
  70.2 1.7 %output.1 = bf16[2,128,1792]{2,1,0:T(8,128)(2,1)S(1)} custom-call(s32[3]{0:T(128)S(1)} %pad_add_fusion.place_ref, bf16[128,512]{1,0:T(8,128)(2,1)S(1)} %values.1.refs_0_, bf16[128,512]{1,0:T(8,128)(2,1)S(1)} %collective-permute-done.6.refs_1_, bf16[128,512]{1,0:T(8,128)(2,1)S(1)} %collective-permute-done.7.refs_2_, ...), custom_call_target="tpu_custom_call" | custom-call | tf_op jit(solution)/shard_map/output/pallas_call | solution.py:330
  71.8 28.6 %all_to_all.17.x_ref = bf16[32,8,1792]{2,1,0:T(8,128)(2,1)S(1)} all-to-all(bf16[32,8,1792]{2,1,0:T(8,128)(2,1)S(1)} %bitcast.6), channel_id=1, replica_groups=mesh['groups'=1,'tensor'=16,'replica'=2] {'replica','tensor'}, dimensions={0} | all-to-all | bytes 1835008 | tf_op jit(solution)/shard_map/all_to_all | solution.py:339
  100.4 0.8 combine.1
  (14 shorter events, 0.0 us)
Async XLA Ops:
  0.0 6.1 %collective-permute-start = (bf16[8,1536]{1,0:T(8,128)(2,1)}, bf16[8,1536]{1,0:T(8,128)(2,1)S(1)}, u32[]{:S(2)}, u32[]{:S(2)}) collective-permute-start(bf16[8,1536]{1,0:T(8,128)(2,1)} %refs_3_.1), channel_id=1, source_target_pairs={{0,16},{2,18},{4,20},{6,22},{8,24},{10,26},{12,28},{14,30},{16,0},... | collective-permute-start | bytes 73736 | tf_op jit(solution)/shard_map/ppermute | solution.py:252
  6.1 4.2 %collective-permute-start.1 = (bf16[16,1536]{1,0:T(8,128)(2,1)S(1)}, bf16[16,1536]{1,0:T(8,128)(2,1)S(1)}, u32[]{:S(2)}, u32[]{:S(2)}) collective-permute-start(bf16[16,1536]{1,0:T(8,128)(2,1)S(1)} %pad_maximum_fusion), channel_id=1, source_target_pairs={{0,8},{2,10},{4,12},{6,14},{8,0},{10,2},{12,4},{14,6},{16,24},{18,... | collective-permute-start | bytes 147464 | tf_op jit(solution)/shard_map/ppermute | solution.py:252
  10.3 4.6 %collective-permute-start.2 = (bf16[32,1536]{1,0:T(8,128)(2,1)S(1)}, bf16[32,1536]{1,0:T(8,128)(2,1)S(1)}, u32[]{:S(2)}, u32[]{:S(2)}) collective-permute-start(bf16[32,1536]{1,0:T(8,128)(2,1)S(1)} %constant_dynamic-update-slice_fusion.refs_0_), channel_id=1, source_target_pairs={{0,4},{2,6},{4,0},{6,2},{8,12},{10,14},{12,8},{14,10},{16,20},{18,... | collective-permute-start | bytes 294920 | tf_op jit(solution)/shard_map/ppermute | solution.py:252
  12.2 2.7 %collective-permute-start.3 = (bf16[32,1536]{1,0:T(8,128)(2,1)S(1)}, bf16[32,1536]{1,0:T(8,128)(2,1)S(1)}, u32[]{:S(2)}, u32[]{:S(2)}) collective-permute-start(bf16[32,1536]{1,0:T(8,128)(2,1)S(1)} %constant_dynamic-update-slice_fusion.refs_0_), channel_id=1, source_target_pairs={{0,2},{2,0},{4,6},{6,4},{8,10},{10,8},{12,14},{14,12},{16,18},{18,... | collective-permute-start | bytes 294920 | tf_op jit(solution)/shard_map/ppermute | solution.py:252
  14.9 1.3 %collective-permute-start.4 = (bf16[32,1536]{1,0:T(8,128)(2,1)S(1)}, bf16[32,1536]{1,0:T(8,128)(2,1)S(1)}, u32[]{:S(2)}, u32[]{:S(2)}) collective-permute-start(bf16[32,1536]{1,0:T(8,128)(2,1)S(1)} %collective-permute-done.2.refs_1_), channel_id=1, source_target_pairs={{0,2},{2,0},{4,6},{6,4},{8,10},{10,8},{12,14},{14,12},{16,18},{18,... | collective-permute-start | bytes 294920 | tf_op jit(solution)/shard_map/ppermute | solution.py:252
  15.0 26.3 %copy-start = (bf16[2,1024,576]{1,2,0:T(8,128)(2,1)S(1)}, bf16[2,1024,576]{1,2,0:T(8,128)(2,1)}, u32[]{:S(2)}) copy-start(bf16[2,1024,576]{1,2,0:T(8,128)(2,1)} %param.17) | copy-start | bytes 7077892
  15.0 26.3 %copy-start.2 = (bf16[8,576]{1,0:T(8,128)(2,1)S(1)}, bf16[8,576]{1,0:T(8,128)(2,1)}, u32[]{:S(2)}) copy-start(bf16[8,576]{1,0:T(8,128)(2,1)} %new_ref.1) | copy-start | bytes 27652
  15.0 26.3 %copy-start.3 = (s32[2]{0:T(128)S(1)}, s32[2]{0:T(128)}, u32[]{:S(2)}) copy-start(s32[2]{0:T(128)} %len_ref.1) | copy-start | bytes 28
  15.0 26.3 %copy-start.4 = (s32[2]{0:T(128)S(1)}, s32[2]{0:T(128)}, u32[]{:S(2)}) copy-start(s32[2]{0:T(128)} %count_ref.1) | copy-start | bytes 28
  41.1 20.4 %copy-start.1 = (bf16[4,512,128]{2,1,0:T(8,128)(2,1)S(1)}, bf16[4,512,128]{2,1,0:T(8,128)(2,1)}, u32[]{:S(2)}) copy-start(bf16[4,512,128]{2,1,0:T(8,128)(2,1)} %uv_ref.1) | copy-start | bytes 1572868
  41.1 20.4 %collective-permute-start.5 = (bf16[512,3584]{1,0:T(8,128)(2,1)}, bf16[512,3584]{1,0:T(8,128)(2,1)S(1)}, u32[]{:S(2)}, u32[]{:S(2)}) collective-permute-start(bf16[512,3584]{1,0:T(8,128)(2,1)} %refs_0_.3), channel_id=1, source_target_pairs={{0,2},{2,0},{4,6},{6,4},{8,10},{10,8},{12,14},{14,12},{16,18},{18,... | collective-permute-start | bytes 11010056 | tf_op jit(solution)/shard_map/ppermute | solution.py:252
  61.5 6.0 %copy-start.5 = (bf16[512,3584]{1,0:T(8,128)(2,1)}, bf16[512,3584]{1,0:T(8,128)(2,1)S(1)}, u32[]{:S(2)}) copy-start(bf16[512,3584]{1,0:T(8,128)(2,1)S(1)} %collective-permute-done.5.refs_1_) | copy-start | bytes 11010052
  61.9 5.6 %collective-permute-start.6 = (bf16[128,512]{1,0:T(8,128)(2,1)S(1)}, bf16[128,512]{1,0:T(8,128)(2,1)S(1)}, u32[]{:S(2)}, u32[]{:S(2)}) collective-permute-start(bf16[128,512]{1,0:T(8,128)(2,1)S(1)} %values.1.refs_0_), channel_id=1, source_target_pairs={{0,1},{1,0},{2,3},{3,2},{4,5},{5,4},{6,7},{7,6},{8,9},{9,8},{10,11... | collective-permute-start | bytes 393224 | tf_op jit(solution)/shard_map/ppermute | solution.py:252
  63.5 6.7 %collective-permute-start.7 = (bf16[128,512]{1,0:T(8,128)(2,1)S(1)}, bf16[128,512]{1,0:T(8,128)(2,1)S(1)}, u32[]{:S(2)}, u32[]{:S(2)}) collective-permute-start(bf16[128,512]{1,0:T(8,128)(2,1)S(1)} %values.1.refs_0_), channel_id=1, source_target_pairs={{0,2},{2,0},{4,6},{6,4},{8,10},{10,8},{12,14},{14,12},{16,18},{18,... | collective-permute-start | bytes 393224 | tf_op jit(solution)/shard_map/ppermute | solution.py:252
  67.5 2.6 %collective-permute-start.8 = (bf16[128,512]{1,0:T(8,128)(2,1)S(1)}, bf16[128,512]{1,0:T(8,128)(2,1)S(1)}, u32[]{:S(2)}, u32[]{:S(2)}) collective-permute-start(bf16[128,512]{1,0:T(8,128)(2,1)S(1)} %collective-permute-done.6.refs_1_), channel_id=1, source_target_pairs={{0,2},{2,0},{4,6},{6,4},{8,10},{10,8},{12,14},{14,12},{16,18},{18,... | collective-permute-start | bytes 393224 | tf_op jit(solution)/shard_map/ppermute | solution.py:252

commit v2 on v1

--- a/solution.py
+++ b/solution.py
@@ -274,10 +274,13 @@
     first, q_up, w_uk, gain, rows, frequency = lax.optimization_barrier((first, *near, frequency))
     rows = jnp.concatenate([rows, first], axis=0)
     bit = owners // 4
-    while bit > 2:
+    while bit > 4:
         rows = jnp.concatenate([rows, step(rows, "tensor", owners, bit)], axis=0)
         bit //= 2
     parts = [rows]
+    if bit == 4:
+        parts = parts + [step(rows, "tensor", owners, k) for k in (4, 2, 6)]
+        bit = 1
     while bit:
         parts = parts + [step(part, "tensor", owners, bit) for part in parts]
         bit //= 2

time: 101 us -> 98.7 us (0.977)
  blocking collectives: 69.1 us -> 67.7 us
    all_to_all x1, blocking collectives: 23.4 us -> 22.1 us  [local_step(): lax.all_to_all(queries, 'tensor', split_axis=0, concat_axis=0, tiled=True)]
    ppermute x9 -> x12, waiting for transfers between devices: 10.3 us -> 9.34 us  [step(): return lax.ppermute(x, axis, [(i, i ^ k) for i in range(size)])]
    ppermute x9 -> x12, starting transfers between devices: 9.69 us -> 9.24 us  [step(): return lax.ppermute(x, axis, [(i, i ^ k) for i in range(size)])]
  transfers between devices with their start and end apart: 9 -> 12, of which waited for: 5 -> 7; matrix products, arithmetic and copies ran while one was open for 0% -> 0% of each run, Pallas kernels for 8% -> 8%
where the time goes in v2:
time: 98.7 us; the launch traced here: 98.4 us
  blocking collectives  67.7 us (69%)
  Pallas kernels  11.9 us (12%)
  waiting for transfers between devices  9.34 us (9%)
  starting transfers between devices  9.24 us (9%)
    all_to_all x1, blocking collectives, local_step(): lax.all_to_all(product, ('replica', 'tensor'), split_axis=0, concat_axis=...  28.5 us
    all_to_all x1, blocking collectives, local_step(): lax.all_to_all(queries, 'tensor', split_axis=0, concat_axis=0, tiled=True)  22.1 us
    all_to_all x1, blocking collectives, local_step(): lax.all_to_all(latent, 'tensor', split_axis=0, concat_axis=0, tiled=True)  17.1 us
    ppermute x12, waiting for transfers between devices, step(): return lax.ppermute(x, axis, [(i, i ^ k) for i in range(size)])  9.34 us
    ppermute x12, starting transfers between devices, step(): return lax.ppermute(x, axis, [(i, i ^ k) for i in range(size)])  9.24 us
    pallas_call x1, Pallas kernels, local_step(): pl.pallas_call(functools.partial(attend_kernel, reqs, drafts, heads), out...  3.18 us
    pallas_call x1, Pallas kernels, fetch_halves(): pl.pallas_call(halves_kernel, out_shape=[pltpu.VMEM((depth, width), bf16)...  2.61 us
  transfers between devices with their start and end apart: 12, of which 7 were waited for; matrix products, arithmetic and copies ran while one was open for 0% of the time, Pallas kernels for 8%

profile of v2, /device:TPU:0, one launch (start us, length us, event | category | flops | bytes accessed | tf_op | source)
XLA Modules:
  0.0 98.4 jit_solution(1095984955002199736)
XLA Ops:
  0.0 4.1 %collective-permute-start = (bf16[8,1536]{1,0:T(8,128)(2,1)}, bf16[8,1536]{1,0:T(8,128)(2,1)S(1)}, u32[]{:S(2)}, u32[]{:S(2)}) collective-permute-start(bf16[8,1536]{1,0:T(8,128)(2,1)} %refs_3_.1), channel_id=1, source_target_pairs={{0,16},{2,18},{4,20},{6,22},{8,24},{10,26},{12,28},{14,30},{16,0},... | collective-permute-start | bytes 73736 | tf_op jit(solution)/shard_map/ppermute | solution.py:252
  4.1 1.8 %shard_map.100 = (bf16[1536,768]{1,0:T(8,128)(2,1)S(1)}, bf16[512,512]{1,0:T(8,128)(2,1)S(1)}, f32[1536]{0:T(1024)S(1)}, bf16[8,1536]{1,0:T(8,128)(2,1)S(1)}) custom-call(bf16[1536,768]{1,0:T(8,128)(2,1)} %refs_0_.2, bf16[512,512]{1,0:T(8,128)(2,1)} %bitcast.8, f32[1536]{0:T(1024)} %refs_2_.1, bf16[8,1536]{1,0:T(8,128)(2,1)} %refs_3_.1), custom_call_target="tpu_custom_call" | custom-call | bytes 5822464 | tf_op jit(solution)/shard_map/pallas_call | solution.py:64
  5.9 0.2 collective-permute-done
  6.1 2.9 %collective-permute-start.3 = (bf16[16,1536]{1,0:T(8,128)(2,1)S(1)}, bf16[16,1536]{1,0:T(8,128)(2,1)S(1)}, u32[]{:S(2)}, u32[]{:S(2)}) collective-permute-start(bf16[16,1536]{1,0:T(8,128)(2,1)S(1)} %constant_dynamic-update-slice_fusion.refs_0_), channel_id=1, source_target_pairs={{0,12},{2,14},{4,8},{6,10},{8,4},{10,6},{12,0},{14,2},{16,28},{18,... | collective-permute-start | bytes 147464 | tf_op jit(solution)/shard_map/ppermute | solution.py:252
  9.0 0.5 collective-permute-start.2
  9.5 0.1 collective-permute-start.1
  9.6 0.0 collective-permute-start.4
  9.6 1.6 %collective-permute-done.3.refs_3_ = bf16[16,1536]{1,0:T(8,128)(2,1)S(1)} collective-permute-done((bf16[16,1536]{1,0:T(8,128)(2,1)S(1)}, bf16[16,1536]{1,0:T(8,128)(2,1)S(1)}, u32[]{:S(2)}, u32[]{:S(2)}) %collective-permute-start.3) | collective-permute-done | bytes 49184 | tf_op jit(solution)/shard_map/ppermute | solution.py:252
  11.2 0.0 collective-permute-start.7
  11.2 1.9 %collective-permute-done.2.refs_2_ = bf16[16,1536]{1,0:T(8,128)(2,1)S(1)} collective-permute-done((bf16[16,1536]{1,0:T(8,128)(2,1)S(1)}, bf16[16,1536]{1,0:T(8,128)(2,1)S(1)}, u32[]{:S(2)}, u32[]{:S(2)}) %collective-permute-start.2) | collective-permute-done | bytes 49184 | tf_op jit(solution)/shard_map/ppermute | solution.py:252
  13.0 0.5 collective-permute-done.1.refs_1_
  13.6 0.0 collective-permute-start.5
  13.6 0.1 pad_add_fusion.place_ref
  13.6 0.0 collective-permute-done.4.refs_4_
  13.7 0.6 collective-permute-done.6.refs_6_
  14.3 0.5 collective-permute-done.5.refs_5_
  14.8 1.5 %query.1 = bf16[16,144,128]{2,1,0:T(8,128)(2,1)S(1)} custom-call(s32[3]{0:T(128)S(1)} %pad_add_fusion.place_ref, bf16[16,1536]{1,0:T(8,128)(2,1)S(1)} %constant_dynamic-update-slice_fusion.refs_0_, bf16[16,1536]{1,0:T(8,128)(2,1)S(1)} %collective-permute-done.1.refs_1_, bf16[16,1536]{1,0:T(8,128)(2,1)S(1)} %collective-permute-done.2.refs_2_, ...), custom_call_target="tpu_custom_call" | custom-call | tf_op jit(solution)/shard_map/query/pallas_call | solution.py:291
  16.3 22.1 %all_to_all.15.q_ref = bf16[16,144,128]{2,1,0:T(8,128)(2,1)S(1)} all-to-all(bf16[16,144,128]{2,1,0:T(8,128)(2,1)S(1)} %query.1), channel_id=1, replica_groups=mesh['groups'=1,'tensor'=16,'replica'=2] {'tensor'}, dimensions={0} | all-to-all | bytes 1179648 | tf_op jit(solution)/shard_map/all_to_all | solution.py:299
  38.4 0.1 collective-permute-start.8
  38.5 3.2 %attend.1 = bf16[16,32,512]{2,1,0:T(8,128)(2,1)S(1)} custom-call(s32[2]{0:T(128)S(1)} %copy-done.3, s32[2]{0:T(128)S(1)} %copy-done.4, bf16[16,144,128]{2,1,0:T(8,128)(2,1)S(1)} %all_to_all.15.q_ref, f32[1,128]{1,0:T(1,128)S(1)} %fusion.3.frequency_ref, bf16[8,576]{1,0:T(8,128)(2,1)S(1)} %copy-done.2, bf16[2,576,1024]{2,1,0:T(8,128)(2,1)S(1)} %bitcast.7), custom_call_target="tpu_custom_call" | custom-call | tf_op jit(solution)/shard_map/attend/pallas_call | solution.py:309
  41.7 17.1 %all_to_all.16.latent_ref = bf16[16,32,512]{2,1,0:T(8,128)(2,1)S(1)} all-to-all(bf16[16,32,512]{2,1,0:T(8,128)(2,1)S(1)} %attend.1), channel_id=1, replica_groups=mesh['groups'=1,'tensor'=16,'replica'=2] {'tensor'}, dimensions={0} | all-to-all | bytes 1048576 | tf_op jit(solution)/shard_map/all_to_all | solution.py:317
  58.8 0.0 collective-permute-done.8.refs_1_
  58.8 0.3 values.1.refs_0_
  59.2 1.6 %collective-permute-start.9 = (bf16[128,512]{1,0:T(8,128)(2,1)S(1)}, bf16[128,512]{1,0:T(8,128)(2,1)S(1)}, u32[]{:S(2)}, u32[]{:S(2)}) collective-permute-start(bf16[128,512]{1,0:T(8,128)(2,1)S(1)} %values.1.refs_0_), channel_id=1, source_target_pairs={{0,1},{1,0},{2,3},{3,2},{4,5},{5,4},{6,7},{7,6},{8,9},{9,8},{10,11... | collective-permute-start | bytes 393224 | tf_op jit(solution)/shard_map/ppermute | solution.py:252
  60.7 0.0 collective-permute-start.10
  60.7 4.1 %collective-permute-done.9.refs_1_ = bf16[128,512]{1,0:T(8,128)(2,1)S(1)} collective-permute-done((bf16[128,512]{1,0:T(8,128)(2,1)S(1)}, bf16[128,512]{1,0:T(8,128)(2,1)S(1)}, u32[]{:S(2)}, u32[]{:S(2)}) %collective-permute-start.9) | collective-permute-done | bytes 131104 | tf_op jit(solution)/shard_map/ppermute | solution.py:252
  64.8 0.0 collective-permute-start.11
  64.8 2.6 %near_output.1 = (bf16[512,1792]{1,0:T(8,128)(2,1)S(1)}, bf16[512,1792]{1,0:T(8,128)(2,1)S(1)}) custom-call(s32[3]{0:T(128)S(1)} %pad_add_fusion.place_ref, bf16[512,3584]{1,0:T(8,128)(2,1)} %refs_0_.3, bf16[512,3584]{1,0:T(8,128)(2,1)} %copy-done.5), custom_call_target="tpu_custom_call" | custom-call | bytes 7340032 | tf_op jit(solution)/shard_map/near_output/pallas_call | solution.py:92
  67.4 0.0 collective-permute-done.11.refs_3_
  67.4 1.7 %output.1 = bf16[2,128,1792]{2,1,0:T(8,128)(2,1)S(1)} custom-call(s32[3]{0:T(128)S(1)} %pad_add_fusion.place_ref, bf16[128,512]{1,0:T(8,128)(2,1)S(1)} %values.1.refs_0_, bf16[128,512]{1,0:T(8,128)(2,1)S(1)} %collective-permute-done.9.refs_1_, bf16[128,512]{1,0:T(8,128)(2,1)S(1)} %collective-permute-done.10.refs_2_, ...), custom_call_target="tpu_custom_call" | custom-call | tf_op jit(solution)/shard_map/output/pallas_call | solution.py:333
  69.1 28.5 %all_to_all.17.x_ref = bf16[32,8,1792]{2,1,0:T(8,128)(2,1)S(1)} all-to-all(bf16[32,8,1792]{2,1,0:T(8,128)(2,1)S(1)} %bitcast.6), channel_id=1, replica_groups=mesh['groups'=1,'tensor'=16,'replica'=2] {'replica','tensor'}, dimensions={0} | all-to-all | bytes 1835008 | tf_op jit(solution)/shard_map/all_to_all | solution.py:342
  97.7 0.8 combine.1
  (18 shorter events, 0.0 us)
Async XLA Ops:
  0.0 6.1 %collective-permute-start = (bf16[8,1536]{1,0:T(8,128)(2,1)}, bf16[8,1536]{1,0:T(8,128)(2,1)S(1)}, u32[]{:S(2)}, u32[]{:S(2)}) collective-permute-start(bf16[8,1536]{1,0:T(8,128)(2,1)} %refs_3_.1), channel_id=1, source_target_pairs={{0,16},{2,18},{4,20},{6,22},{8,24},{10,26},{12,28},{14,30},{16,0},... | collective-permute-start | bytes 73736 | tf_op jit(solution)/shard_map/ppermute | solution.py:252
  6.1 5.1 %collective-permute-start.3 = (bf16[16,1536]{1,0:T(8,128)(2,1)S(1)}, bf16[16,1536]{1,0:T(8,128)(2,1)S(1)}, u32[]{:S(2)}, u32[]{:S(2)}) collective-permute-start(bf16[16,1536]{1,0:T(8,128)(2,1)S(1)} %constant_dynamic-update-slice_fusion.refs_0_), channel_id=1, source_target_pairs={{0,12},{2,14},{4,8},{6,10},{8,4},{10,6},{12,0},{14,2},{16,28},{18,... | collective-permute-start | bytes 147464 | tf_op jit(solution)/shard_map/ppermute | solution.py:252
  9.0 4.1 %collective-permute-start.2 = (bf16[16,1536]{1,0:T(8,128)(2,1)S(1)}, bf16[16,1536]{1,0:T(8,128)(2,1)S(1)}, u32[]{:S(2)}, u32[]{:S(2)}) collective-permute-start(bf16[16,1536]{1,0:T(8,128)(2,1)S(1)} %constant_dynamic-update-slice_fusion.refs_0_), channel_id=1, source_target_pairs={{0,4},{2,6},{4,0},{6,2},{8,12},{10,14},{12,8},{14,10},{16,20},{18,... | collective-permute-start | bytes 147464 | tf_op jit(solution)/shard_map/ppermute | solution.py:252
  9.5 4.1 %collective-permute-start.1 = (bf16[16,1536]{1,0:T(8,128)(2,1)S(1)}, bf16[16,1536]{1,0:T(8,128)(2,1)S(1)}, u32[]{:S(2)}, u32[]{:S(2)}) collective-permute-start(bf16[16,1536]{1,0:T(8,128)(2,1)S(1)} %constant_dynamic-update-slice_fusion.refs_0_), channel_id=1, source_target_pairs={{0,8},{2,10},{4,12},{6,14},{8,0},{10,2},{12,4},{14,6},{16,24},{18,... | collective-permute-start | bytes 147464 | tf_op jit(solution)/shard_map/ppermute | solution.py:252
  9.6 4.1 %collective-permute-start.4 = (bf16[16,1536]{1,0:T(8,128)(2,1)S(1)}, bf16[16,1536]{1,0:T(8,128)(2,1)S(1)}, u32[]{:S(2)}, u32[]{:S(2)}) collective-permute-start(bf16[16,1536]{1,0:T(8,128)(2,1)S(1)} %constant_dynamic-update-slice_fusion.refs_0_), channel_id=1, source_target_pairs={{0,2},{2,0},{4,6},{6,4},{8,10},{10,8},{12,14},{14,12},{16,18},{18,... | collective-permute-start | bytes 147464 | tf_op jit(solution)/shard_map/ppermute | solution.py:252
  11.2 2.5 %collective-permute-start.7 = (bf16[16,1536]{1,0:T(8,128)(2,1)S(1)}, bf16[16,1536]{1,0:T(8,128)(2,1)S(1)}, u32[]{:S(2)}, u32[]{:S(2)}) collective-permute-start(bf16[16,1536]{1,0:T(8,128)(2,1)S(1)} %collective-permute-done.3.refs_3_), channel_id=1, source_target_pairs={{0,2},{2,0},{4,6},{6,4},{8,10},{10,8},{12,14},{14,12},{16,18},{18,... | collective-permute-start | bytes 147464 | tf_op jit(solution)/shard_map/ppermute | solution.py:252
  13.0 1.2 %collective-permute-start.6 = (bf16[16,1536]{1,0:T(8,128)(2,1)S(1)}, bf16[16,1536]{1,0:T(8,128)(2,1)S(1)}, u32[]{:S(2)}, u32[]{:S(2)}) collective-permute-start(bf16[16,1536]{1,0:T(8,128)(2,1)S(1)} %collective-permute-done.2.refs_2_), channel_id=1, source_target_pairs={{0,2},{2,0},{4,6},{6,4},{8,10},{10,8},{12,14},{14,12},{16,18},{18,... | collective-permute-start | bytes 147464 | tf_op jit(solution)/shard_map/ppermute | solution.py:252
  13.6 1.2 %collective-permute-start.5 = (bf16[16,1536]{1,0:T(8,128)(2,1)S(1)}, bf16[16,1536]{1,0:T(8,128)(2,1)S(1)}, u32[]{:S(2)}, u32[]{:S(2)}) collective-permute-start(bf16[16,1536]{1,0:T(8,128)(2,1)S(1)} %collective-permute-done.1.refs_1_), channel_id=1, source_target_pairs={{0,2},{2,0},{4,6},{6,4},{8,10},{10,8},{12,14},{14,12},{16,18},{18,... | collective-permute-start | bytes 147464 | tf_op jit(solution)/shard_map/ppermute | solution.py:252
  13.6 24.9 %copy-start = (bf16[2,1024,576]{1,2,0:T(8,128)(2,1)S(1)}, bf16[2,1024,576]{1,2,0:T(8,128)(2,1)}, u32[]{:S(2)}) copy-start(bf16[2,1024,576]{1,2,0:T(8,128)(2,1)} %param.17) | copy-start | bytes 7077892
  13.6 24.9 %copy-start.2 = (bf16[8,576]{1,0:T(8,128)(2,1)S(1)}, bf16[8,576]{1,0:T(8,128)(2,1)}, u32[]{:S(2)}) copy-start(bf16[8,576]{1,0:T(8,128)(2,1)} %new_ref.1) | copy-start | bytes 27652
  13.6 24.9 %copy-start.3 = (s32[2]{0:T(128)S(1)}, s32[2]{0:T(128)}, u32[]{:S(2)}) copy-start(s32[2]{0:T(128)} %len_ref.1) | copy-start | bytes 28
  13.6 24.9 %copy-start.4 = (s32[2]{0:T(128)S(1)}, s32[2]{0:T(128)}, u32[]{:S(2)}) copy-start(s32[2]{0:T(128)} %count_ref.1) | copy-start | bytes 28
  38.4 20.4 %copy-start.1 = (bf16[4,512,128]{2,1,0:T(8,128)(2,1)S(1)}, bf16[4,512,128]{2,1,0:T(8,128)(2,1)}, u32[]{:S(2)}) copy-start(bf16[4,512,128]{2,1,0:T(8,128)(2,1)} %uv_ref.1) | copy-start | bytes 1572868
  38.4 20.4 %collective-permute-start.8 = (bf16[512,3584]{1,0:T(8,128)(2,1)}, bf16[512,3584]{1,0:T(8,128)(2,1)S(1)}, u32[]{:S(2)}, u32[]{:S(2)}) collective-permute-start(bf16[512,3584]{1,0:T(8,128)(2,1)} %refs_0_.3), channel_id=1, source_target_pairs={{0,2},{2,0},{4,6},{6,4},{8,10},{10,8},{12,14},{14,12},{16,18},{18,... | collective-permute-start | bytes 11010056 | tf_op jit(solution)/shard_map/ppermute | solution.py:252
  58.8 6.0 %copy-start.5 = (bf16[512,3584]{1,0:T(8,128)(2,1)}, bf16[512,3584]{1,0:T(8,128)(2,1)S(1)}, u32[]{:S(2)}) copy-start(bf16[512,3584]{1,0:T(8,128)(2,1)S(1)} %collective-permute-done.8.refs_1_) | copy-start | bytes 11010052
  59.2 5.6 %collective-permute-start.9 = (bf16[128,512]{1,0:T(8,128)(2,1)S(1)}, bf16[128,512]{1,0:T(8,128)(2,1)S(1)}, u32[]{:S(2)}, u32[]{:S(2)}) collective-permute-start(bf16[128,512]{1,0:T(8,128)(2,1)S(1)} %values.1.refs_0_), channel_id=1, source_target_pairs={{0,1},{1,0},{2,3},{3,2},{4,5},{5,4},{6,7},{7,6},{8,9},{9,8},{10,11... | collective-permute-start | bytes 393224 | tf_op jit(solution)/shard_map/ppermute | solution.py:252
  60.7 6.7 %collective-permute-start.10 = (bf16[128,512]{1,0:T(8,128)(2,1)S(1)}, bf16[128,512]{1,0:T(8,128)(2,1)S(1)}, u32[]{:S(2)}, u32[]{:S(2)}) collective-permute-start(bf16[128,512]{1,0:T(8,128)(2,1)S(1)} %values.1.refs_0_), channel_id=1, source_target_pairs={{0,2},{2,0},{4,6},{6,4},{8,10},{10,8},{12,14},{14,12},{16,18},{18,... | collective-permute-start | bytes 393224 | tf_op jit(solution)/shard_map/ppermute | solution.py:252
  64.8 2.6 %collective-permute-start.11 = (bf16[128,512]{1,0:T(8,128)(2,1)S(1)}, bf16[128,512]{1,0:T(8,128)(2,1)S(1)}, u32[]{:S(2)}, u32[]{:S(2)}) collective-permute-start(bf16[128,512]{1,0:T(8,128)(2,1)S(1)} %collective-permute-done.9.refs_1_), channel_id=1, source_target_pairs={{0,2},{2,0},{4,6},{6,4},{8,10},{10,8},{12,14},{14,12},{16,18},{18,... | collective-permute-start | bytes 393224 | tf_op jit(solution)/shard_map/ppermute | solution.py:252

commit v3 on v2

--- a/solution.py
+++ b/solution.py
@@ -1,4 +1,5 @@
 import functools
+import math
 
 import jax
 import jax.numpy as jnp
@@ -158,7 +159,7 @@
     chunks = LATENT // LANES
     per = LANES // ROPE
     slots = cache_ref.shape[2]
-    scale = QKD ** (-0.5)
+    scale = QKD ** (-0.5) * math.log2(math.e)
     rotated = []
     for b in range(reqs // per):
         at = (reqs * chunks + b) * hd
@@ -190,21 +191,19 @@
         )
         keys = cache_ref[q]
         rows = new_ref[...]
-        score = (mm(absorbed, keys[:LATENT]) + mm(rotated[q], keys[LATENT:])) * scale
-        fresh = (mm_nt(absorbed, rows[:, :LATENT]) + mm_nt(rotated[q], rows[:, LATENT:])) * scale
+        score = mm(absorbed, keys[:LATENT]) + mm(rotated[q], keys[LATENT:])
+        fresh = mm_nt(absorbed, rows[:, :LATENT]) + mm_nt(rotated[q], rows[:, LATENT:])
         score = jnp.where(slot < len_ref[q], score, -jnp.inf)
         seen = (new_at >= q * drafts) & (new_at - q * drafts <= draft)
         fresh = jnp.where(seen, fresh, -jnp.inf)
         peak = jnp.maximum(
             jnp.max(score, axis=1, keepdims=True), jnp.max(fresh, axis=1, keepdims=True)
         )
-        score = jnp.exp(score - peak)
-        fresh = jnp.exp(fresh - peak)
+        score = jnp.exp2((score - peak) * scale)
+        fresh = jnp.exp2((fresh - peak) * scale)
         total = jnp.sum(score, axis=1, keepdims=True) + jnp.sum(fresh, axis=1, keepdims=True)
-        inverse = 1.0 / total
-        mix = mm_nt((score * inverse).astype(bf16), keys[:LATENT])
-        mix = mix + mm((fresh * inverse).astype(bf16), rows[:, :LATENT])
-        mix = jnp.where(draft < count_ref[q], mix, 0.0).astype(bf16)
+        mix = mm_nt(score.astype(bf16), keys[:LATENT]) + mm(fresh.astype(bf16), rows[:, :LATENT])
+        mix = jnp.where(draft < count_ref[q], mix * (1.0 / total), 0.0).astype(bf16)
         out_ref[:, q * hd : (q + 1) * hd, :] = mix.reshape(owners, hd, LATENT)
 
 

time: 98.7 us -> 98.4 us (level)
  transfers between devices with their start and end apart: 12 -> 12, of which waited for: 7 -> 7; matrix products, arithmetic and copies ran while one was open for 0% -> 0% of each run, Pallas kernels for 8% -> 7%
where the time goes in v3:
time: 98.4 us; the launch traced here: 98.2 us
  blocking collectives  67.7 us (69%)
  Pallas kernels  11.6 us (12%)
  waiting for transfers between devices  9.34 us (9%)
  starting transfers between devices  9.25 us (9%)
    all_to_all x1, blocking collectives, local_step(): lax.all_to_all(product, ('replica', 'tensor'), split_axis=0, concat_axis=...  28.6 us
    all_to_all x1, blocking collectives, local_step(): lax.all_to_all(queries, 'tensor', split_axis=0, concat_axis=0, tiled=True)  22.1 us
    all_to_all x1, blocking collectives, local_step(): lax.all_to_all(latent, 'tensor', split_axis=0, concat_axis=0, tiled=True)  17.1 us
    ppermute x12, waiting for transfers between devices, step(): return lax.ppermute(x, axis, [(i, i ^ k) for i in range(size)])  9.34 us
    ppermute x12, starting transfers between devices, step(): return lax.ppermute(x, axis, [(i, i ^ k) for i in range(size)])  9.25 us
    pallas_call x1, Pallas kernels, local_step(): pl.pallas_call(functools.partial(attend_kernel, reqs, drafts, heads), out...  2.95 us
    pallas_call x1, Pallas kernels, fetch_halves(): pl.pallas_call(halves_kernel, out_shape=[pltpu.VMEM((depth, width), bf16)...  2.61 us
  transfers between devices with their start and end apart: 12, of which 7 were waited for; matrix products, arithmetic and copies ran while one was open for 0% of the time, Pallas kernels for 7%

profile of v3, /device:TPU:0, one launch (start us, length us, event | category | flops | bytes accessed | tf_op | source)
XLA Modules:
  0.0 98.2 jit_solution(14231949730488035706)
XLA Ops:
  0.0 4.1 %collective-permute-start = (bf16[8,1536]{1,0:T(8,128)(2,1)}, bf16[8,1536]{1,0:T(8,128)(2,1)S(1)}, u32[]{:S(2)}, u32[]{:S(2)}) collective-permute-start(bf16[8,1536]{1,0:T(8,128)(2,1)} %refs_3_.1), channel_id=1, source_target_pairs={{0,16},{2,18},{4,20},{6,22},{8,24},{10,26},{12,28},{14,30},{16,0},... | collective-permute-start | bytes 73736 | tf_op jit(solution)/shard_map/ppermute | solution.py:251
  4.1 1.8 %shard_map.100 = (bf16[1536,768]{1,0:T(8,128)(2,1)S(1)}, bf16[512,512]{1,0:T(8,128)(2,1)S(1)}, f32[1536]{0:T(1024)S(1)}, bf16[8,1536]{1,0:T(8,128)(2,1)S(1)}) custom-call(bf16[1536,768]{1,0:T(8,128)(2,1)} %refs_0_.2, bf16[512,512]{1,0:T(8,128)(2,1)} %bitcast.8, f32[1536]{0:T(1024)} %refs_2_.1, bf16[8,1536]{1,0:T(8,128)(2,1)} %refs_3_.1), custom_call_target="tpu_custom_call" | custom-call | bytes 5822464 | tf_op jit(solution)/shard_map/pallas_call | solution.py:65
  5.9 0.2 collective-permute-done
  6.1 2.9 %collective-permute-start.3 = (bf16[16,1536]{1,0:T(8,128)(2,1)S(1)}, bf16[16,1536]{1,0:T(8,128)(2,1)S(1)}, u32[]{:S(2)}, u32[]{:S(2)}) collective-permute-start(bf16[16,1536]{1,0:T(8,128)(2,1)S(1)} %constant_dynamic-update-slice_fusion.refs_0_), channel_id=1, source_target_pairs={{0,12},{2,14},{4,8},{6,10},{8,4},{10,6},{12,0},{14,2},{16,28},{18,... | collective-permute-start | bytes 147464 | tf_op jit(solution)/shard_map/ppermute | solution.py:251
  9.0 0.5 collective-permute-start.2
  9.5 0.1 collective-permute-start.1
  9.6 0.0 collective-permute-start.4
  9.6 1.6 %collective-permute-done.3.refs_3_ = bf16[16,1536]{1,0:T(8,128)(2,1)S(1)} collective-permute-done((bf16[16,1536]{1,0:T(8,128)(2,1)S(1)}, bf16[16,1536]{1,0:T(8,128)(2,1)S(1)}, u32[]{:S(2)}, u32[]{:S(2)}) %collective-permute-start.3) | collective-permute-done | bytes 49184 | tf_op jit(solution)/shard_map/ppermute | solution.py:251
  11.2 0.0 collective-permute-start.7
  11.2 1.9 %collective-permute-done.2.refs_2_ = bf16[16,1536]{1,0:T(8,128)(2,1)S(1)} collective-permute-done((bf16[16,1536]{1,0:T(8,128)(2,1)S(1)}, bf16[16,1536]{1,0:T(8,128)(2,1)S(1)}, u32[]{:S(2)}, u32[]{:S(2)}) %collective-permute-start.2) | collective-permute-done | bytes 49184 | tf_op jit(solution)/shard_map/ppermute | solution.py:251
  13.0 0.0 collective-permute-start.6
  13.0 0.5 collective-permute-done.1.refs_1_
  13.6 0.0 collective-permute-start.5
  13.6 0.1 pad_add_fusion.place_ref
  13.6 0.0 collective-permute-done.4.refs_4_
  13.7 0.6 collective-permute-done.6.refs_6_
  14.3 0.5 collective-permute-done.5.refs_5_
  14.8 1.5 %query.1 = bf16[16,144,128]{2,1,0:T(8,128)(2,1)S(1)} custom-call(s32[3]{0:T(128)S(1)} %pad_add_fusion.place_ref, bf16[16,1536]{1,0:T(8,128)(2,1)S(1)} %constant_dynamic-update-slice_fusion.refs_0_, bf16[16,1536]{1,0:T(8,128)(2,1)S(1)} %collective-permute-done.1.refs_1_, bf16[16,1536]{1,0:T(8,128)(2,1)S(1)} %collective-permute-done.2.refs_2_, ...), custom_call_target="tpu_custom_call" | custom-call | tf_op jit(solution)/shard_map/query/pallas_call | solution.py:290
  16.3 22.1 %all_to_all.15.q_ref = bf16[16,144,128]{2,1,0:T(8,128)(2,1)S(1)} all-to-all(bf16[16,144,128]{2,1,0:T(8,128)(2,1)S(1)} %query.1), channel_id=1, replica_groups=mesh['groups'=1,'tensor'=16,'replica'=2] {'tensor'}, dimensions={0} | all-to-all | bytes 1179648 | tf_op jit(solution)/shard_map/all_to_all | solution.py:298
  38.4 0.1 collective-permute-start.8
  38.5 2.9 %attend.1 = bf16[16,32,512]{2,1,0:T(8,128)(2,1)S(1)} custom-call(s32[2]{0:T(128)S(1)} %copy-done.3, s32[2]{0:T(128)S(1)} %copy-done.4, bf16[16,144,128]{2,1,0:T(8,128)(2,1)S(1)} %all_to_all.15.q_ref, f32[1,128]{1,0:T(1,128)S(1)} %fusion.3.frequency_ref, bf16[8,576]{1,0:T(8,128)(2,1)S(1)} %copy-done.2, bf16[2,576,1024]{2,1,0:T(8,128)(2,1)S(1)} %bitcast.7), custom_call_target="tpu_custom_call" | custom-call | tf_op jit(solution)/shard_map/attend/pallas_call | solution.py:308
  41.5 17.1 %all_to_all.16.latent_ref = bf16[16,32,512]{2,1,0:T(8,128)(2,1)S(1)} all-to-all(bf16[16,32,512]{2,1,0:T(8,128)(2,1)S(1)} %attend.1), channel_id=1, replica_groups=mesh['groups'=1,'tensor'=16,'replica'=2] {'tensor'}, dimensions={0} | all-to-all | bytes 1048576 | tf_op jit(solution)/shard_map/all_to_all | solution.py:316
  58.6 0.3 values.1.refs_0_
  58.9 1.6 %collective-permute-start.9 = (bf16[128,512]{1,0:T(8,128)(2,1)S(1)}, bf16[128,512]{1,0:T(8,128)(2,1)S(1)}, u32[]{:S(2)}, u32[]{:S(2)}) collective-permute-start(bf16[128,512]{1,0:T(8,128)(2,1)S(1)} %values.1.refs_0_), channel_id=1, source_target_pairs={{0,1},{1,0},{2,3},{3,2},{4,5},{5,4},{6,7},{7,6},{8,9},{9,8},{10,11... | collective-permute-start | bytes 393224 | tf_op jit(solution)/shard_map/ppermute | solution.py:251
  60.5 4.0 %collective-permute-done.9.refs_1_ = bf16[128,512]{1,0:T(8,128)(2,1)S(1)} collective-permute-done((bf16[128,512]{1,0:T(8,128)(2,1)S(1)}, bf16[128,512]{1,0:T(8,128)(2,1)S(1)}, u32[]{:S(2)}, u32[]{:S(2)}) %collective-permute-start.9) | collective-permute-done | bytes 131104 | tf_op jit(solution)/shard_map/ppermute | solution.py:251
  64.5 0.0 collective-permute-start.11
  64.5 2.6 %near_output.1 = (bf16[512,1792]{1,0:T(8,128)(2,1)S(1)}, bf16[512,1792]{1,0:T(8,128)(2,1)S(1)}) custom-call(s32[3]{0:T(128)S(1)} %pad_add_fusion.place_ref, bf16[512,3584]{1,0:T(8,128)(2,1)} %refs_0_.3, bf16[512,3584]{1,0:T(8,128)(2,1)} %copy-done.5), custom_call_target="tpu_custom_call" | custom-call | bytes 7340032 | tf_op jit(solution)/shard_map/near_output/pallas_call | solution.py:93
  67.2 0.0 collective-permute-done.10.refs_2_
  67.2 0.0 collective-permute-done.11.refs_3_
  67.2 1.7 %output.1 = bf16[2,128,1792]{2,1,0:T(8,128)(2,1)S(1)} custom-call(s32[3]{0:T(128)S(1)} %pad_add_fusion.place_ref, bf16[128,512]{1,0:T(8,128)(2,1)S(1)} %values.1.refs_0_, bf16[128,512]{1,0:T(8,128)(2,1)S(1)} %collective-permute-done.9.refs_1_, bf16[128,512]{1,0:T(8,128)(2,1)S(1)} %collective-permute-done.10.refs_2_, ...), custom_call_target="tpu_custom_call" | custom-call | tf_op jit(solution)/shard_map/output/pallas_call | solution.py:332
  68.9 28.6 %all_to_all.17.x_ref = bf16[32,8,1792]{2,1,0:T(8,128)(2,1)S(1)} all-to-all(bf16[32,8,1792]{2,1,0:T(8,128)(2,1)S(1)} %bitcast.6), channel_id=1, replica_groups=mesh['groups'=1,'tensor'=16,'replica'=2] {'replica','tensor'}, dimensions={0} | all-to-all | bytes 1835008 | tf_op jit(solution)/shard_map/all_to_all | solution.py:341
  97.4 0.8 combine.1
  (18 shorter events, 0.0 us)
Async XLA Ops:
  0.0 6.1 %collective-permute-start = (bf16[8,1536]{1,0:T(8,128)(2,1)}, bf16[8,1536]{1,0:T(8,128)(2,1)S(1)}, u32[]{:S(2)}, u32[]{:S(2)}) collective-permute-start(bf16[8,1536]{1,0:T(8,128)(2,1)} %refs_3_.1), channel_id=1, source_target_pairs={{0,16},{2,18},{4,20},{6,22},{8,24},{10,26},{12,28},{14,30},{16,0},... | collective-permute-start | bytes 73736 | tf_op jit(solution)/shard_map/ppermute | solution.py:251
  6.1 5.1 %collective-permute-start.3 = (bf16[16,1536]{1,0:T(8,128)(2,1)S(1)}, bf16[16,1536]{1,0:T(8,128)(2,1)S(1)}, u32[]{:S(2)}, u32[]{:S(2)}) collective-permute-start(bf16[16,1536]{1,0:T(8,128)(2,1)S(1)} %constant_dynamic-update-slice_fusion.refs_0_), channel_id=1, source_target_pairs={{0,12},{2,14},{4,8},{6,10},{8,4},{10,6},{12,0},{14,2},{16,28},{18,... | collective-permute-start | bytes 147464 | tf_op jit(solution)/shard_map/ppermute | solution.py:251
  9.0 4.1 %collective-permute-start.2 = (bf16[16,1536]{1,0:T(8,128)(2,1)S(1)}, bf16[16,1536]{1,0:T(8,128)(2,1)S(1)}, u32[]{:S(2)}, u32[]{:S(2)}) collective-permute-start(bf16[16,1536]{1,0:T(8,128)(2,1)S(1)} %constant_dynamic-update-slice_fusion.refs_0_), channel_id=1, source_target_pairs={{0,4},{2,6},{4,0},{6,2},{8,12},{10,14},{12,8},{14,10},{16,20},{18,... | collective-permute-start | bytes 147464 | tf_op jit(solution)/shard_map/ppermute | solution.py:251
  9.5 4.1 %collective-permute-start.1 = (bf16[16,1536]{1,0:T(8,128)(2,1)S(1)}, bf16[16,1536]{1,0:T(8,128)(2,1)S(1)}, u32[]{:S(2)}, u32[]{:S(2)}) collective-permute-start(bf16[16,1536]{1,0:T(8,128)(2,1)S(1)} %constant_dynamic-update-slice_fusion.refs_0_), channel_id=1, source_target_pairs={{0,8},{2,10},{4,12},{6,14},{8,0},{10,2},{12,4},{14,6},{16,24},{18,... | collective-permute-start | bytes 147464 | tf_op jit(solution)/shard_map/ppermute | solution.py:251
  9.6 4.1 %collective-permute-start.4 = (bf16[16,1536]{1,0:T(8,128)(2,1)S(1)}, bf16[16,1536]{1,0:T(8,128)(2,1)S(1)}, u32[]{:S(2)}, u32[]{:S(2)}) collective-permute-start(bf16[16,1536]{1,0:T(8,128)(2,1)S(1)} %constant_dynamic-update-slice_fusion.refs_0_), channel_id=1, source_target_pairs={{0,2},{2,0},{4,6},{6,4},{8,10},{10,8},{12,14},{14,12},{16,18},{18,... | collective-permute-start | bytes 147464 | tf_op jit(solution)/shard_map/ppermute | solution.py:251
  11.2 2.5 %collective-permute-start.7 = (bf16[16,1536]{1,0:T(8,128)(2,1)S(1)}, bf16[16,1536]{1,0:T(8,128)(2,1)S(1)}, u32[]{:S(2)}, u32[]{:S(2)}) collective-permute-start(bf16[16,1536]{1,0:T(8,128)(2,1)S(1)} %collective-permute-done.3.refs_3_), channel_id=1, source_target_pairs={{0,2},{2,0},{4,6},{6,4},{8,10},{10,8},{12,14},{14,12},{16,18},{18,... | collective-permute-start | bytes 147464 | tf_op jit(solution)/shard_map/ppermute | solution.py:251
  13.0 1.2 %collective-permute-start.6 = (bf16[16,1536]{1,0:T(8,128)(2,1)S(1)}, bf16[16,1536]{1,0:T(8,128)(2,1)S(1)}, u32[]{:S(2)}, u32[]{:S(2)}) collective-permute-start(bf16[16,1536]{1,0:T(8,128)(2,1)S(1)} %collective-permute-done.2.refs_2_), channel_id=1, source_target_pairs={{0,2},{2,0},{4,6},{6,4},{8,10},{10,8},{12,14},{14,12},{16,18},{18,... | collective-permute-start | bytes 147464 | tf_op jit(solution)/shard_map/ppermute | solution.py:251
  13.6 1.2 %collective-permute-start.5 = (bf16[16,1536]{1,0:T(8,128)(2,1)S(1)}, bf16[16,1536]{1,0:T(8,128)(2,1)S(1)}, u32[]{:S(2)}, u32[]{:S(2)}) collective-permute-start(bf16[16,1536]{1,0:T(8,128)(2,1)S(1)} %collective-permute-done.1.refs_1_), channel_id=1, source_target_pairs={{0,2},{2,0},{4,6},{6,4},{8,10},{10,8},{12,14},{14,12},{16,18},{18,... | collective-permute-start | bytes 147464 | tf_op jit(solution)/shard_map/ppermute | solution.py:251
  13.6 24.9 %copy-start = (bf16[2,1024,576]{1,2,0:T(8,128)(2,1)S(1)}, bf16[2,1024,576]{1,2,0:T(8,128)(2,1)}, u32[]{:S(2)}) copy-start(bf16[2,1024,576]{1,2,0:T(8,128)(2,1)} %param.17) | copy-start | bytes 7077892
  13.6 24.9 %copy-start.2 = (bf16[8,576]{1,0:T(8,128)(2,1)S(1)}, bf16[8,576]{1,0:T(8,128)(2,1)}, u32[]{:S(2)}) copy-start(bf16[8,576]{1,0:T(8,128)(2,1)} %new_ref.1) | copy-start | bytes 27652
  13.6 24.9 %copy-start.3 = (s32[2]{0:T(128)S(1)}, s32[2]{0:T(128)}, u32[]{:S(2)}) copy-start(s32[2]{0:T(128)} %len_ref.1) | copy-start | bytes 28
  13.6 24.9 %copy-start.4 = (s32[2]{0:T(128)S(1)}, s32[2]{0:T(128)}, u32[]{:S(2)}) copy-start(s32[2]{0:T(128)} %count_ref.1) | copy-start | bytes 28
  38.4 20.2 %copy-start.1 = (bf16[4,512,128]{2,1,0:T(8,128)(2,1)S(1)}, bf16[4,512,128]{2,1,0:T(8,128)(2,1)}, u32[]{:S(2)}) copy-start(bf16[4,512,128]{2,1,0:T(8,128)(2,1)} %uv_ref.1) | copy-start | bytes 1572868
  38.4 20.2 %collective-permute-start.8 = (bf16[512,3584]{1,0:T(8,128)(2,1)}, bf16[512,3584]{1,0:T(8,128)(2,1)S(1)}, u32[]{:S(2)}, u32[]{:S(2)}) collective-permute-start(bf16[512,3584]{1,0:T(8,128)(2,1)} %refs_0_.3), channel_id=1, source_target_pairs={{0,2},{2,0},{4,6},{6,4},{8,10},{10,8},{12,14},{14,12},{16,18},{18,... | collective-permute-start | bytes 11010056 | tf_op jit(solution)/shard_map/ppermute | solution.py:251
  58.6 6.0 %copy-start.5 = (bf16[512,3584]{1,0:T(8,128)(2,1)}, bf16[512,3584]{1,0:T(8,128)(2,1)S(1)}, u32[]{:S(2)}) copy-start(bf16[512,3584]{1,0:T(8,128)(2,1)S(1)} %collective-permute-done.8.refs_1_) | copy-start | bytes 11010052
  58.9 5.6 %collective-permute-start.9 = (bf16[128,512]{1,0:T(8,128)(2,1)S(1)}, bf16[128,512]{1,0:T(8,128)(2,1)S(1)}, u32[]{:S(2)}, u32[]{:S(2)}) collective-permute-start(bf16[128,512]{1,0:T(8,128)(2,1)S(1)} %values.1.refs_0_), channel_id=1, source_target_pairs={{0,1},{1,0},{2,3},{3,2},{4,5},{5,4},{6,7},{7,6},{8,9},{9,8},{10,11... | collective-permute-start | bytes 393224 | tf_op jit(solution)/shard_map/ppermute | solution.py:251
  60.5 6.7 %collective-permute-start.10 = (bf16[128,512]{1,0:T(8,128)(2,1)S(1)}, bf16[128,512]{1,0:T(8,128)(2,1)S(1)}, u32[]{:S(2)}, u32[]{:S(2)}) collective-permute-start(bf16[128,512]{1,0:T(8,128)(2,1)S(1)} %values.1.refs_0_), channel_id=1, source_target_pairs={{0,2},{2,0},{4,6},{6,4},{8,10},{10,8},{12,14},{14,12},{16,18},{18,... | collective-permute-start | bytes 393224 | tf_op jit(solution)/shard_map/ppermute | solution.py:251
  64.5 2.6 %collective-permute-start.11 = (bf16[128,512]{1,0:T(8,128)(2,1)S(1)}, bf16[128,512]{1,0:T(8,128)(2,1)S(1)}, u32[]{:S(2)}, u32[]{:S(2)}) collective-permute-start(bf16[128,512]{1,0:T(8,128)(2,1)S(1)} %collective-permute-done.9.refs_1_), channel_id=1, source_target_pairs={{0,2},{2,0},{4,6},{6,4},{8,10},{10,8},{12,14},{14,12},{16,18},{18,... | collective-permute-start | bytes 393224 | tf_op jit(solution)/shard_map/ppermute | solution.py:251

commit v4 on v3

--- a/solution.py
+++ b/solution.py
@@ -222,17 +222,34 @@
         out_ref[:, (h + 1) * VDIM : (h + 2) * VDIM] = mm(second, uv_ref[h + 1]).astype(bf16)
 
 
-def output_kernel(place_ref, *refs):
-    *value_refs, w_own_ref, w_other_ref, out_ref = refs
-    replicas, rows, half = out_ref.shape
-    own = jnp.concatenate([ref[...] for ref in value_refs[:replicas]], axis=0)
-    other = jnp.concatenate([ref[...] for ref in value_refs[replicas:]], axis=0)
+def output_kernel(done, place_ref, w_own_ref, w_other_ref, *refs):
+    ready_refs, value_refs, out_ref = refs[:done], refs[done:-1], refs[-1]
+    rows, half = out_ref.shape[1:]
+    count = len(value_refs) // 2
+    own = jnp.concatenate([ref[...] for ref in value_refs[:count]], axis=0)
+    other = jnp.concatenate([ref[...] for ref in value_refs[count:]], axis=0)
+    base = place_ref[1] if done else 0
+    for k in range(done):
+        out_ref[base ^ k] = ready_refs[k][0]
     tile = 256 if half % 256 == 0 else half
     for at in range(0, half, tile):
         part = mm(own, w_own_ref[:, at : at + tile]) + mm(other, w_other_ref[:, at : at + tile])
         part = part.astype(bf16)
-        for k in range(replicas):
-            out_ref[place_ref[1] ^ k, :, at : at + tile] = part[k * rows : (k + 1) * rows]
+        for k in range(count):
+            out_ref[base ^ (done + k), :, at : at + tile] = part[k * rows : (k + 1) * rows]
+
+
+def output_rows(ready, blocks, place, weights, own, other, params):
+    operands = [place, *weights, *ready, *own, *other]
+    shape = (blocks, own[0].shape[0], weights[0].shape[1])
+    return pl.pallas_call(
+        functools.partial(output_kernel, len(ready)),
+        out_shape=jax.ShapeDtypeStruct(shape, bf16),
+        in_specs=[smem_spec()] + [vmem_spec()] * (len(operands) - 1),
+        out_specs=vmem_spec(),
+        compiler_params=params,
+        name="output",
+    )(*operands)
 
 
 def sum_kernel(replicas, pairs, x_ref, out_ref):
@@ -329,14 +346,10 @@
     w_own, w_other = fetch_halves(place, (w_own, w_other), half)
     other = [step(piece, "tensor", owners, 1) for piece in own]
 
-    product = pl.pallas_call(
-        output_kernel,
-        out_shape=jax.ShapeDtypeStruct((replicas, owners * rows_dev, half), bf16),
-        in_specs=[smem_spec()] + [vmem_spec()] * (2 * replicas + 2),
-        out_specs=vmem_spec(),
-        compiler_params=params,
-        name="output",
-    )(place, *own, *other, w_own, w_other)
+    weights = (w_own, w_other)
+    product = output_rows((), 1, place, weights, own[:1], other[:1], params)
+    if replicas > 1:
+        product = output_rows((product,), replicas, place, weights, own[1:], other[1:], params)
     product = product.reshape(replicas * owners, rows_dev, half)
     placed = lax.all_to_all(product, ("replica", "tensor"), split_axis=0, concat_axis=0, tiled=True)
     return pl.pallas_call(

time: 98.4 us -> 99.2 us (level)
    pallas_call x1 -> x2, Pallas kernels: 1.67 us -> 2.38 us  [output_rows(): pl.pallas_call(functools.partial(output_kernel, len(ready)), out_shape=ja...]
  transfers between devices with their start and end apart: 12 -> 12, of which waited for: 7 -> 7; matrix products, arithmetic and copies ran while one was open for 0% -> 0% of each run, Pallas kernels for 7% -> 9%
where the time goes in v4:
time: 99.2 us; the launch traced here: 98.9 us
  blocking collectives  67.7 us (68%)
  Pallas kernels  12.4 us (12%)
  waiting for transfers between devices  9.34 us (9%)
  starting transfers between devices  9.25 us (9%)
    all_to_all x1, blocking collectives, local_step(): lax.all_to_all(product, ('replica', 'tensor'), split_axis=0, concat_axis=...  28.6 us
    all_to_all x1, blocking collectives, local_step(): lax.all_to_all(queries, 'tensor', split_axis=0, concat_axis=0, tiled=True)  22.1 us
    all_to_all x1, blocking collectives, local_step(): lax.all_to_all(latent, 'tensor', split_axis=0, concat_axis=0, tiled=True)  17.1 us
    ppermute x12, waiting for transfers between devices, step(): return lax.ppermute(x, axis, [(i, i ^ k) for i in range(size)])  9.34 us
    ppermute x12, starting transfers between devices, step(): return lax.ppermute(x, axis, [(i, i ^ k) for i in range(size)])  9.25 us
    pallas_call x1, Pallas kernels, local_step(): pl.pallas_call(functools.partial(attend_kernel, reqs, drafts, heads), out...  2.95 us
    pallas_call x1, Pallas kernels, fetch_halves(): pl.pallas_call(halves_kernel, out_shape=[pltpu.VMEM((depth, width), bf16)...  2.61 us
    pallas_call x2, Pallas kernels, output_rows(): pl.pallas_call(functools.partial(output_kernel, len(ready)), out_shape=ja...  2.38 us
  transfers between devices with their start and end apart: 12, of which 7 were waited for; matrix products, arithmetic and copies ran while one was open for 0% of the time, Pallas kernels for 9%

profile of v4, /device:TPU:0, one launch (start us, length us, event | category | flops | bytes accessed | tf_op | source)
XLA Modules:
  0.0 98.9 jit_solution(1888601736116161829)
XLA Ops:
  0.0 4.1 %collective-permute-start = (bf16[8,1536]{1,0:T(8,128)(2,1)}, bf16[8,1536]{1,0:T(8,128)(2,1)S(1)}, u32[]{:S(2)}, u32[]{:S(2)}) collective-permute-start(bf16[8,1536]{1,0:T(8,128)(2,1)} %refs_3_.1), channel_id=1, source_target_pairs={{0,16},{2,18},{4,20},{6,22},{8,24},{10,26},{12,28},{14,30},{16,0},... | collective-permute-start | bytes 73736 | tf_op jit(solution)/shard_map/ppermute | solution.py:268
  4.1 1.8 %shard_map.100 = (bf16[1536,768]{1,0:T(8,128)(2,1)S(1)}, bf16[512,512]{1,0:T(8,128)(2,1)S(1)}, f32[1536]{0:T(1024)S(1)}, bf16[8,1536]{1,0:T(8,128)(2,1)S(1)}) custom-call(bf16[1536,768]{1,0:T(8,128)(2,1)} %refs_0_.2, bf16[512,512]{1,0:T(8,128)(2,1)} %bitcast.8, f32[1536]{0:T(1024)} %refs_2_.1, bf16[8,1536]{1,0:T(8,128)(2,1)} %refs_3_.1), custom_call_target="tpu_custom_call" | custom-call | bytes 5822464 | tf_op jit(solution)/shard_map/pallas_call | solution.py:65
  5.9 0.2 collective-permute-done
  6.1 2.9 %collective-permute-start.3 = (bf16[16,1536]{1,0:T(8,128)(2,1)S(1)}, bf16[16,1536]{1,0:T(8,128)(2,1)S(1)}, u32[]{:S(2)}, u32[]{:S(2)}) collective-permute-start(bf16[16,1536]{1,0:T(8,128)(2,1)S(1)} %constant_dynamic-update-slice_fusion.refs_0_), channel_id=1, source_target_pairs={{0,12},{2,14},{4,8},{6,10},{8,4},{10,6},{12,0},{14,2},{16,28},{18,... | collective-permute-start | bytes 147464 | tf_op jit(solution)/shard_map/ppermute | solution.py:268
  9.0 0.5 collective-permute-start.2
  9.5 0.1 collective-permute-start.1
  9.6 0.0 collective-permute-start.4
  9.6 1.6 %collective-permute-done.3.refs_3_ = bf16[16,1536]{1,0:T(8,128)(2,1)S(1)} collective-permute-done((bf16[16,1536]{1,0:T(8,128)(2,1)S(1)}, bf16[16,1536]{1,0:T(8,128)(2,1)S(1)}, u32[]{:S(2)}, u32[]{:S(2)}) %collective-permute-start.3) | collective-permute-done | bytes 49184 | tf_op jit(solution)/shard_map/ppermute | solution.py:268
  11.2 0.0 collective-permute-start.7
  11.2 1.9 %collective-permute-done.2.refs_2_ = bf16[16,1536]{1,0:T(8,128)(2,1)S(1)} collective-permute-done((bf16[16,1536]{1,0:T(8,128)(2,1)S(1)}, bf16[16,1536]{1,0:T(8,128)(2,1)S(1)}, u32[]{:S(2)}, u32[]{:S(2)}) %collective-permute-start.2) | collective-permute-done | bytes 49184 | tf_op jit(solution)/shard_map/ppermute | solution.py:268
  13.0 0.5 collective-permute-done.1.refs_1_
  13.6 0.0 collective-permute-start.5
  13.6 0.1 pad_add_fusion.place_ref
  13.6 0.0 collective-permute-done.4.refs_4_
  13.7 0.6 collective-permute-done.6.refs_6_
  14.3 0.5 collective-permute-done.5.refs_5_
  14.8 1.5 %query.1 = bf16[16,144,128]{2,1,0:T(8,128)(2,1)S(1)} custom-call(s32[3]{0:T(128)S(1)} %pad_add_fusion.place_ref, bf16[16,1536]{1,0:T(8,128)(2,1)S(1)} %constant_dynamic-update-slice_fusion.refs_0_, bf16[16,1536]{1,0:T(8,128)(2,1)S(1)} %collective-permute-done.1.refs_1_, bf16[16,1536]{1,0:T(8,128)(2,1)S(1)} %collective-permute-done.2.refs_2_, ...), custom_call_target="tpu_custom_call" | custom-call | tf_op jit(solution)/shard_map/query/pallas_call | solution.py:307
  16.3 22.1 %all_to_all.15.q_ref = bf16[16,144,128]{2,1,0:T(8,128)(2,1)S(1)} all-to-all(bf16[16,144,128]{2,1,0:T(8,128)(2,1)S(1)} %query.1), channel_id=1, replica_groups=mesh['groups'=1,'tensor'=16,'replica'=2] {'tensor'}, dimensions={0} | all-to-all | bytes 1179648 | tf_op jit(solution)/shard_map/all_to_all | solution.py:315
  38.4 0.1 collective-permute-start.8
  38.5 2.9 %attend.1 = bf16[16,32,512]{2,1,0:T(8,128)(2,1)S(1)} custom-call(s32[2]{0:T(128)S(1)} %copy-done.3, s32[2]{0:T(128)S(1)} %copy-done.4, bf16[16,144,128]{2,1,0:T(8,128)(2,1)S(1)} %all_to_all.15.q_ref, f32[1,128]{1,0:T(1,128)S(1)} %fusion.3.frequency_ref, bf16[8,576]{1,0:T(8,128)(2,1)S(1)} %copy-done.2, bf16[2,576,1024]{2,1,0:T(8,128)(2,1)S(1)} %bitcast.7), custom_call_target="tpu_custom_call" | custom-call | tf_op jit(solution)/shard_map/attend/pallas_call | solution.py:325
  41.5 17.1 %all_to_all.16.latent_ref = bf16[16,32,512]{2,1,0:T(8,128)(2,1)S(1)} all-to-all(bf16[16,32,512]{2,1,0:T(8,128)(2,1)S(1)} %attend.1), channel_id=1, replica_groups=mesh['groups'=1,'tensor'=16,'replica'=2] {'tensor'}, dimensions={0} | all-to-all | bytes 1048576 | tf_op jit(solution)/shard_map/all_to_all | solution.py:333
  58.6 0.4 values.1.refs_0_
  58.9 1.6 %collective-permute-start.10 = (bf16[128,512]{1,0:T(8,128)(2,1)S(1)}, bf16[128,512]{1,0:T(8,128)(2,1)S(1)}, u32[]{:S(2)}, u32[]{:S(2)}) collective-permute-start(bf16[128,512]{1,0:T(8,128)(2,1)S(1)} %values.1.refs_0_), channel_id=1, source_target_pairs={{0,1},{1,0},{2,3},{3,2},{4,5},{5,4},{6,7},{7,6},{8,9},{9,8},{10,11... | collective-permute-start | bytes 393224 | tf_op jit(solution)/shard_map/ppermute | solution.py:268
  60.5 4.0 %collective-permute-done.10.refs_1_ = bf16[128,512]{1,0:T(8,128)(2,1)S(1)} collective-permute-done((bf16[128,512]{1,0:T(8,128)(2,1)S(1)}, bf16[128,512]{1,0:T(8,128)(2,1)S(1)}, u32[]{:S(2)}, u32[]{:S(2)}) %collective-permute-start.10) | collective-permute-done | bytes 131104 | tf_op jit(solution)/shard_map/ppermute | solution.py:268
  64.5 0.0 collective-permute-start.11
  64.6 2.6 %near_output.1 = (bf16[512,1792]{1,0:T(8,128)(2,1)S(1)}, bf16[512,1792]{1,0:T(8,128)(2,1)S(1)}) custom-call(s32[3]{0:T(128)S(1)} %pad_add_fusion.place_ref, bf16[512,3584]{1,0:T(8,128)(2,1)} %refs_0_.3, bf16[512,3584]{1,0:T(8,128)(2,1)} %copy-done.5), custom_call_target="tpu_custom_call" | custom-call | bytes 7340032 | tf_op jit(solution)/shard_map/near_output/pallas_call | solution.py:93
  67.2 0.0 collective-permute-done.9.refs_1_
  67.2 1.2 %output.2.refs_0_ = bf16[1,128,1792]{2,1,0:T(8,128)(2,1)S(1)} custom-call(s32[3]{0:T(128)S(1)} %pad_add_fusion.place_ref, bf16[512,1792]{1,0:T(8,128)(2,1)S(1)} %get-tuple-element.34.w_own_ref, bf16[512,1792]{1,0:T(8,128)(2,1)S(1)} %get-tuple-element.35.w_other_ref, bf16[128,512]{1,0:T(8,128)(2,1)S(1)} %values.1.refs_0_, ...), custom_call_target="tpu_custom_call" | custom-call | tf_op jit(solution)/shard_map/output/pallas_call | solution.py:245
  68.4 0.0 collective-permute-done.11.refs_2_
  68.4 1.2 %output.3 = bf16[2,128,1792]{2,1,0:T(8,128)(2,1)S(1)} custom-call(s32[3]{0:T(128)S(1)} %pad_add_fusion.place_ref, bf16[512,1792]{1,0:T(8,128)(2,1)S(1)} %get-tuple-element.34.w_own_ref, bf16[512,1792]{1,0:T(8,128)(2,1)S(1)} %get-tuple-element.35.w_other_ref, bf16[1,128,1792]{2,1,0:T(8,128)(2,1)S(1)} %output.2.refs_0_, ...), custom_call_target="tpu_custom_call" | custom-call | tf_op jit(solution)/shard_map/output/pallas_call | solution.py:245
  69.6 28.6 %all_to_all.17.x_ref = bf16[32,8,1792]{2,1,0:T(8,128)(2,1)S(1)} all-to-all(bf16[32,8,1792]{2,1,0:T(8,128)(2,1)S(1)} %bitcast.6), channel_id=1, replica_groups=mesh['groups'=1,'tensor'=16,'replica'=2] {'replica','tensor'}, dimensions={0} | all-to-all | bytes 1835008 | tf_op jit(solution)/shard_map/all_to_all | solution.py:354
  98.1 0.8 combine.1
  (19 shorter events, 0.0 us)
Async XLA Ops:
  0.0 6.1 %collective-permute-start = (bf16[8,1536]{1,0:T(8,128)(2,1)}, bf16[8,1536]{1,0:T(8,128)(2,1)S(1)}, u32[]{:S(2)}, u32[]{:S(2)}) collective-permute-start(bf16[8,1536]{1,0:T(8,128)(2,1)} %refs_3_.1), channel_id=1, source_target_pairs={{0,16},{2,18},{4,20},{6,22},{8,24},{10,26},{12,28},{14,30},{16,0},... | collective-permute-start | bytes 73736 | tf_op jit(solution)/shard_map/ppermute | solution.py:268
  6.1 5.1 %collective-permute-start.3 = (bf16[16,1536]{1,0:T(8,128)(2,1)S(1)}, bf16[16,1536]{1,0:T(8,128)(2,1)S(1)}, u32[]{:S(2)}, u32[]{:S(2)}) collective-permute-start(bf16[16,1536]{1,0:T(8,128)(2,1)S(1)} %constant_dynamic-update-slice_fusion.refs_0_), channel_id=1, source_target_pairs={{0,12},{2,14},{4,8},{6,10},{8,4},{10,6},{12,0},{14,2},{16,28},{18,... | collective-permute-start | bytes 147464 | tf_op jit(solution)/shard_map/ppermute | solution.py:268
  9.0 4.1 %collective-permute-start.2 = (bf16[16,1536]{1,0:T(8,128)(2,1)S(1)}, bf16[16,1536]{1,0:T(8,128)(2,1)S(1)}, u32[]{:S(2)}, u32[]{:S(2)}) collective-permute-start(bf16[16,1536]{1,0:T(8,128)(2,1)S(1)} %constant_dynamic-update-slice_fusion.refs_0_), channel_id=1, source_target_pairs={{0,4},{2,6},{4,0},{6,2},{8,12},{10,14},{12,8},{14,10},{16,20},{18,... | collective-permute-start | bytes 147464 | tf_op jit(solution)/shard_map/ppermute | solution.py:268
  9.5 4.1 %collective-permute-start.1 = (bf16[16,1536]{1,0:T(8,128)(2,1)S(1)}, bf16[16,1536]{1,0:T(8,128)(2,1)S(1)}, u32[]{:S(2)}, u32[]{:S(2)}) collective-permute-start(bf16[16,1536]{1,0:T(8,128)(2,1)S(1)} %constant_dynamic-update-slice_fusion.refs_0_), channel_id=1, source_target_pairs={{0,8},{2,10},{4,12},{6,14},{8,0},{10,2},{12,4},{14,6},{16,24},{18,... | collective-permute-start | bytes 147464 | tf_op jit(solution)/shard_map/ppermute | solution.py:268
  9.6 4.1 %collective-permute-start.4 = (bf16[16,1536]{1,0:T(8,128)(2,1)S(1)}, bf16[16,1536]{1,0:T(8,128)(2,1)S(1)}, u32[]{:S(2)}, u32[]{:S(2)}) collective-permute-start(bf16[16,1536]{1,0:T(8,128)(2,1)S(1)} %constant_dynamic-update-slice_fusion.refs_0_), channel_id=1, source_target_pairs={{0,2},{2,0},{4,6},{6,4},{8,10},{10,8},{12,14},{14,12},{16,18},{18,... | collective-permute-start | bytes 147464 | tf_op jit(solution)/shard_map/ppermute | solution.py:268
  11.2 2.5 %collective-permute-start.7 = (bf16[16,1536]{1,0:T(8,128)(2,1)S(1)}, bf16[16,1536]{1,0:T(8,128)(2,1)S(1)}, u32[]{:S(2)}, u32[]{:S(2)}) collective-permute-start(bf16[16,1536]{1,0:T(8,128)(2,1)S(1)} %collective-permute-done.3.refs_3_), channel_id=1, source_target_pairs={{0,2},{2,0},{4,6},{6,4},{8,10},{10,8},{12,14},{14,12},{16,18},{18,... | collective-permute-start | bytes 147464 | tf_op jit(solution)/shard_map/ppermute | solution.py:268
  13.0 1.2 %collective-permute-start.6 = (bf16[16,1536]{1,0:T(8,128)(2,1)S(1)}, bf16[16,1536]{1,0:T(8,128)(2,1)S(1)}, u32[]{:S(2)}, u32[]{:S(2)}) collective-permute-start(bf16[16,1536]{1,0:T(8,128)(2,1)S(1)} %collective-permute-done.2.refs_2_), channel_id=1, source_target_pairs={{0,2},{2,0},{4,6},{6,4},{8,10},{10,8},{12,14},{14,12},{16,18},{18,... | collective-permute-start | bytes 147464 | tf_op jit(solution)/shard_map/ppermute | solution.py:268
  13.6 1.2 %collective-permute-start.5 = (bf16[16,1536]{1,0:T(8,128)(2,1)S(1)}, bf16[16,1536]{1,0:T(8,128)(2,1)S(1)}, u32[]{:S(2)}, u32[]{:S(2)}) collective-permute-start(bf16[16,1536]{1,0:T(8,128)(2,1)S(1)} %collective-permute-done.1.refs_1_), channel_id=1, source_target_pairs={{0,2},{2,0},{4,6},{6,4},{8,10},{10,8},{12,14},{14,12},{16,18},{18,... | collective-permute-start | bytes 147464 | tf_op jit(solution)/shard_map/ppermute | solution.py:268
  13.6 24.9 %copy-start = (bf16[2,1024,576]{1,2,0:T(8,128)(2,1)S(1)}, bf16[2,1024,576]{1,2,0:T(8,128)(2,1)}, u32[]{:S(2)}) copy-start(bf16[2,1024,576]{1,2,0:T(8,128)(2,1)} %param.17) | copy-start | bytes 7077892
  13.6 24.9 %copy-start.2 = (bf16[8,576]{1,0:T(8,128)(2,1)S(1)}, bf16[8,576]{1,0:T(8,128)(2,1)}, u32[]{:S(2)}) copy-start(bf16[8,576]{1,0:T(8,128)(2,1)} %new_ref.1) | copy-start | bytes 27652
  13.6 24.9 %copy-start.3 = (s32[2]{0:T(128)S(1)}, s32[2]{0:T(128)}, u32[]{:S(2)}) copy-start(s32[2]{0:T(128)} %len_ref.1) | copy-start | bytes 28
  13.6 24.9 %copy-start.4 = (s32[2]{0:T(128)S(1)}, s32[2]{0:T(128)}, u32[]{:S(2)}) copy-start(s32[2]{0:T(128)} %count_ref.1) | copy-start | bytes 28
  38.4 20.2 %copy-start.1 = (bf16[4,512,128]{2,1,0:T(8,128)(2,1)S(1)}, bf16[4,512,128]{2,1,0:T(8,128)(2,1)}, u32[]{:S(2)}) copy-start(bf16[4,512,128]{2,1,0:T(8,128)(2,1)} %uv_ref.1) | copy-start | bytes 1572868
  38.4 20.2 %collective-permute-start.8 = (bf16[512,3584]{1,0:T(8,128)(2,1)}, bf16[512,3584]{1,0:T(8,128)(2,1)S(1)}, u32[]{:S(2)}, u32[]{:S(2)}) collective-permute-start(bf16[512,3584]{1,0:T(8,128)(2,1)} %refs_0_.3), channel_id=1, source_target_pairs={{0,2},{2,0},{4,6},{6,4},{8,10},{10,8},{12,14},{14,12},{16,18},{18,... | collective-permute-start | bytes 11010056 | tf_op jit(solution)/shard_map/ppermute | solution.py:268
  58.6 6.0 %copy-start.5 = (bf16[512,3584]{1,0:T(8,128)(2,1)}, bf16[512,3584]{1,0:T(8,128)(2,1)S(1)}, u32[]{:S(2)}) copy-start(bf16[512,3584]{1,0:T(8,128)(2,1)S(1)} %collective-permute-done.8.refs_1_) | copy-start | bytes 11010052
  58.9 5.6 %collective-permute-start.10 = (bf16[128,512]{1,0:T(8,128)(2,1)S(1)}, bf16[128,512]{1,0:T(8,128)(2,1)S(1)}, u32[]{:S(2)}, u32[]{:S(2)}) collective-permute-start(bf16[128,512]{1,0:T(8,128)(2,1)S(1)} %values.1.refs_0_), channel_id=1, source_target_pairs={{0,1},{1,0},{2,3},{3,2},{4,5},{5,4},{6,7},{7,6},{8,9},{9,8},{10,11... | collective-permute-start | bytes 393224 | tf_op jit(solution)/shard_map/ppermute | solution.py:268
  60.5 6.7 %collective-permute-start.9 = (bf16[128,512]{1,0:T(8,128)(2,1)S(1)}, bf16[128,512]{1,0:T(8,128)(2,1)S(1)}, u32[]{:S(2)}, u32[]{:S(2)}) collective-permute-start(bf16[128,512]{1,0:T(8,128)(2,1)S(1)} %values.1.refs_0_), channel_id=1, source_target_pairs={{0,2},{2,0},{4,6},{6,4},{8,10},{10,8},{12,14},{14,12},{16,18},{18,... | collective-permute-start | bytes 393224 | tf_op jit(solution)/shard_map/ppermute | solution.py:268
  64.5 3.8 %collective-permute-start.11 = (bf16[128,512]{1,0:T(8,128)(2,1)S(1)}, bf16[128,512]{1,0:T(8,128)(2,1)S(1)}, u32[]{:S(2)}, u32[]{:S(2)}) collective-permute-start(bf16[128,512]{1,0:T(8,128)(2,1)S(1)} %collective-permute-done.10.refs_1_), channel_id=1, source_target_pairs={{0,2},{2,0},{4,6},{6,4},{8,10},{10,8},{12,14},{14,12},{16,18},{18,... | collective-permute-start | bytes 393224 | tf_op jit(solution)/shard_map/ppermute | solution.py:268

commit v5 on v4

--- a/solution.py
+++ b/solution.py
@@ -222,26 +222,47 @@
         out_ref[:, (h + 1) * VDIM : (h + 2) * VDIM] = mm(second, uv_ref[h + 1]).astype(bf16)
 
 
-def output_kernel(done, place_ref, w_own_ref, w_other_ref, *refs):
+def tile_of(width):
+    return 256 if width % 256 == 0 else width
+
+
+def half_product_kernel(count, *refs):
+    w_ref, *value_refs, out_ref = refs
+    rows = jnp.concatenate([ref[...] for ref in value_refs[:count]], axis=0)
+    tile = tile_of(w_ref.shape[1])
+    for at in range(0, w_ref.shape[1], tile):
+        out_ref[:, at : at + tile] = mm(rows, w_ref[:, at : at + tile])
+
+
+def half_product(weights, pieces, params):
+    return pl.pallas_call(
+        functools.partial(half_product_kernel, len(pieces)),
+        out_shape=jax.ShapeDtypeStruct((len(pieces) * pieces[0].shape[0], weights.shape[1]), f32),
+        in_specs=[vmem_spec()] * (1 + len(pieces)),
+        out_specs=vmem_spec(),
+        compiler_params=params,
+        name="half_product",
+    )(weights, *pieces)
+
+
+def output_kernel(done, place_ref, w_ref, partial_ref, *refs):
     ready_refs, value_refs, out_ref = refs[:done], refs[done:-1], refs[-1]
     rows, half = out_ref.shape[1:]
-    count = len(value_refs) // 2
-    own = jnp.concatenate([ref[...] for ref in value_refs[:count]], axis=0)
-    other = jnp.concatenate([ref[...] for ref in value_refs[count:]], axis=0)
+    other = jnp.concatenate([ref[...] for ref in value_refs], axis=0)
     base = place_ref[1] if done else 0
     for k in range(done):
         out_ref[base ^ k] = ready_refs[k][0]
-    tile = 256 if half % 256 == 0 else half
+    tile = tile_of(half)
     for at in range(0, half, tile):
-        part = mm(own, w_own_ref[:, at : at + tile]) + mm(other, w_other_ref[:, at : at + tile])
+        part = partial_ref[:, at : at + tile] + mm(other, w_ref[:, at : at + tile])
         part = part.astype(bf16)
-        for k in range(count):
+        for k in range(len(value_refs)):
             out_ref[base ^ (done + k), :, at : at + tile] = part[k * rows : (k + 1) * rows]
 
 
-def output_rows(ready, blocks, place, weights, own, other, params):
-    operands = [place, *weights, *ready, *own, *other]
-    shape = (blocks, own[0].shape[0], weights[0].shape[1])
+def output_rows(ready, blocks, place, weights, partial, other, params):
+    operands = [place, weights, partial, *ready, *other]
+    shape = (blocks, other[0].shape[0], weights.shape[1])
     return pl.pallas_call(
         functools.partial(output_kernel, len(ready)),
         out_shape=jax.ShapeDtypeStruct(shape, bf16),
@@ -344,12 +365,14 @@
     nearest = step(values, "replica", replicas, 1)
     own = [values, nearest] + [step(values, "replica", replicas, k) for k in range(2, replicas)]
     w_own, w_other = fetch_halves(place, (w_own, w_other), half)
-    other = [step(piece, "tensor", owners, 1) for piece in own]
-
-    weights = (w_own, w_other)
-    product = output_rows((), 1, place, weights, own[:1], other[:1], params)
+    other = [step(own[0], "tensor", owners, 1)]
+    product = half_product(w_own, own[:1], params)
+    product = output_rows((), 1, place, w_other, product, other, params)
     if replicas > 1:
-        product = output_rows((product,), replicas, place, weights, own[1:], other[1:], params)
+        other = [step(own[1], "tensor", owners, 1)]
+        other = other + [step(piece, "tensor", owners, 1) for piece in own[2:]]
+        partial = half_product(w_own, own[1:], params)
+        product = output_rows((product,), replicas, place, w_other, partial, other, params)
     product = product.reshape(replicas * owners, rows_dev, half)
     placed = lax.all_to_all(product, ("replica", "tensor"), split_axis=0, concat_axis=0, tiled=True)
     return pl.pallas_call(

time: 99.2 us -> 99.5 us (level)
  no operation moved by 1% of the time
where the time goes in v5:
time: 99.5 us; the launch traced here: 99.3 us
  blocking collectives  67.7 us (68%)
  Pallas kernels  12.7 us (13%)
  waiting for transfers between devices  9.34 us (9%)
  starting transfers between devices  9.25 us (9%)
    all_to_all x1, blocking collectives, local_step(): lax.all_to_all(product, ('replica', 'tensor'), split_axis=0, concat_axis=...  28.6 us
    all_to_all x1, blocking collectives, local_step(): lax.all_to_all(queries, 'tensor', split_axis=0, concat_axis=0, tiled=True)  22.1 us
    all_to_all x1, blocking collectives, local_step(): lax.all_to_all(latent, 'tensor', split_axis=0, concat_axis=0, tiled=True)  17.1 us
    ppermute x12, waiting for transfers between devices, step(): return lax.ppermute(x, axis, [(i, i ^ k) for i in range(size)])  9.34 us
    ppermute x12, starting transfers between devices, step(): return lax.ppermute(x, axis, [(i, i ^ k) for i in range(size)])  9.25 us
    pallas_call x1, Pallas kernels, local_step(): pl.pallas_call(functools.partial(attend_kernel, reqs, drafts, heads), out...  2.95 us
    pallas_call x1, Pallas kernels, fetch_halves(): pl.pallas_call(halves_kernel, out_shape=[pltpu.VMEM((depth, width), bf16)...  2.61 us
  transfers between devices with their start and end apart: 12, of which 7 were waited for; matrix products, arithmetic and copies ran while one was open for 0% of the time, Pallas kernels for 9%

profile of v5, /device:TPU:0, one launch (start us, length us, event | category | flops | bytes accessed | tf_op | source)
XLA Modules:
  0.0 99.3 jit_solution(1091281860462267764)
XLA Ops:
  0.0 4.1 %collective-permute-start = (bf16[8,1536]{1,0:T(8,128)(2,1)}, bf16[8,1536]{1,0:T(8,128)(2,1)S(1)}, u32[]{:S(2)}, u32[]{:S(2)}) collective-permute-start(bf16[8,1536]{1,0:T(8,128)(2,1)} %refs_3_.1), channel_id=1, source_target_pairs={{0,16},{2,18},{4,20},{6,22},{8,24},{10,26},{12,28},{14,30},{16,0},... | collective-permute-start | bytes 73736 | tf_op jit(solution)/shard_map/ppermute | solution.py:289
  4.1 1.8 %shard_map.100 = (bf16[1536,768]{1,0:T(8,128)(2,1)S(1)}, bf16[512,512]{1,0:T(8,128)(2,1)S(1)}, f32[1536]{0:T(1024)S(1)}, bf16[8,1536]{1,0:T(8,128)(2,1)S(1)}) custom-call(bf16[1536,768]{1,0:T(8,128)(2,1)} %refs_0_.2, bf16[512,512]{1,0:T(8,128)(2,1)} %bitcast.8, f32[1536]{0:T(1024)} %refs_2_.1, bf16[8,1536]{1,0:T(8,128)(2,1)} %refs_3_.1), custom_call_target="tpu_custom_call" | custom-call | bytes 5822464 | tf_op jit(solution)/shard_map/pallas_call | solution.py:65
  5.9 0.2 collective-permute-done
  6.1 2.9 %collective-permute-start.3 = (bf16[16,1536]{1,0:T(8,128)(2,1)S(1)}, bf16[16,1536]{1,0:T(8,128)(2,1)S(1)}, u32[]{:S(2)}, u32[]{:S(2)}) collective-permute-start(bf16[16,1536]{1,0:T(8,128)(2,1)S(1)} %constant_dynamic-update-slice_fusion.refs_0_), channel_id=1, source_target_pairs={{0,12},{2,14},{4,8},{6,10},{8,4},{10,6},{12,0},{14,2},{16,28},{18,... | collective-permute-start | bytes 147464 | tf_op jit(solution)/shard_map/ppermute | solution.py:289
  9.0 0.5 collective-permute-start.2
  9.5 0.1 collective-permute-start.1
  9.6 1.6 %collective-permute-done.3.refs_3_ = bf16[16,1536]{1,0:T(8,128)(2,1)S(1)} collective-permute-done((bf16[16,1536]{1,0:T(8,128)(2,1)S(1)}, bf16[16,1536]{1,0:T(8,128)(2,1)S(1)}, u32[]{:S(2)}, u32[]{:S(2)}) %collective-permute-start.3) | collective-permute-done | bytes 49184 | tf_op jit(solution)/shard_map/ppermute | solution.py:289
  11.2 1.9 %collective-permute-done.2.refs_2_ = bf16[16,1536]{1,0:T(8,128)(2,1)S(1)} collective-permute-done((bf16[16,1536]{1,0:T(8,128)(2,1)S(1)}, bf16[16,1536]{1,0:T(8,128)(2,1)S(1)}, u32[]{:S(2)}, u32[]{:S(2)}) %collective-permute-start.2) | collective-permute-done | bytes 49184 | tf_op jit(solution)/shard_map/ppermute | solution.py:289
  13.0 0.5 collective-permute-done.1.refs_1_
  13.6 0.0 collective-permute-start.5
  13.6 0.1 pad_add_fusion.place_ref
  13.6 0.0 collective-permute-done.4.refs_4_
  13.7 0.6 collective-permute-done.6.refs_6_
  14.3 0.5 collective-permute-done.5.refs_5_
  14.8 1.5 %query.1 = bf16[16,144,128]{2,1,0:T(8,128)(2,1)S(1)} custom-call(s32[3]{0:T(128)S(1)} %pad_add_fusion.place_ref, bf16[16,1536]{1,0:T(8,128)(2,1)S(1)} %constant_dynamic-update-slice_fusion.refs_0_, bf16[16,1536]{1,0:T(8,128)(2,1)S(1)} %collective-permute-done.1.refs_1_, bf16[16,1536]{1,0:T(8,128)(2,1)S(1)} %collective-permute-done.2.refs_2_, ...), custom_call_target="tpu_custom_call" | custom-call | tf_op jit(solution)/shard_map/query/pallas_call | solution.py:328
  16.3 22.1 %all_to_all.15.q_ref = bf16[16,144,128]{2,1,0:T(8,128)(2,1)S(1)} all-to-all(bf16[16,144,128]{2,1,0:T(8,128)(2,1)S(1)} %query.1), channel_id=1, replica_groups=mesh['groups'=1,'tensor'=16,'replica'=2] {'tensor'}, dimensions={0} | all-to-all | bytes 1179648 | tf_op jit(solution)/shard_map/all_to_all | solution.py:336
  38.4 0.1 collective-permute-start.8
  38.5 2.9 %attend.1 = bf16[16,32,512]{2,1,0:T(8,128)(2,1)S(1)} custom-call(s32[2]{0:T(128)S(1)} %copy-done.3, s32[2]{0:T(128)S(1)} %copy-done.4, bf16[16,144,128]{2,1,0:T(8,128)(2,1)S(1)} %all_to_all.15.q_ref, f32[1,128]{1,0:T(1,128)S(1)} %fusion.3.frequency_ref, bf16[8,576]{1,0:T(8,128)(2,1)S(1)} %copy-done.2, bf16[2,576,1024]{2,1,0:T(8,128)(2,1)S(1)} %bitcast.7), custom_call_target="tpu_custom_call" | custom-call | tf_op jit(solution)/shard_map/attend/pallas_call | solution.py:346
  41.5 17.1 %all_to_all.16.latent_ref = bf16[16,32,512]{2,1,0:T(8,128)(2,1)S(1)} all-to-all(bf16[16,32,512]{2,1,0:T(8,128)(2,1)S(1)} %attend.1), channel_id=1, replica_groups=mesh['groups'=1,'tensor'=16,'replica'=2] {'tensor'}, dimensions={0} | all-to-all | bytes 1048576 | tf_op jit(solution)/shard_map/all_to_all | solution.py:354
  58.6 0.4 values.1.refs_1_
  58.9 1.6 %collective-permute-start.9 = (bf16[128,512]{1,0:T(8,128)(2,1)S(1)}, bf16[128,512]{1,0:T(8,128)(2,1)S(1)}, u32[]{:S(2)}, u32[]{:S(2)}) collective-permute-start(bf16[128,512]{1,0:T(8,128)(2,1)S(1)} %values.1.refs_1_), channel_id=1, source_target_pairs={{0,1},{1,0},{2,3},{3,2},{4,5},{5,4},{6,7},{7,6},{8,9},{9,8},{10,11... | collective-permute-start | bytes 393224 | tf_op jit(solution)/shard_map/ppermute | solution.py:289
  60.5 4.0 %collective-permute-done.9.refs_1_ = bf16[128,512]{1,0:T(8,128)(2,1)S(1)} collective-permute-done((bf16[128,512]{1,0:T(8,128)(2,1)S(1)}, bf16[128,512]{1,0:T(8,128)(2,1)S(1)}, u32[]{:S(2)}, u32[]{:S(2)}) %collective-permute-start.9) | collective-permute-done | bytes 131104 | tf_op jit(solution)/shard_map/ppermute | solution.py:289
  64.5 0.0 collective-permute-start.11
  64.6 2.6 %near_output.1 = (bf16[512,1792]{1,0:T(8,128)(2,1)S(1)}, bf16[512,1792]{1,0:T(8,128)(2,1)S(1)}) custom-call(s32[3]{0:T(128)S(1)} %pad_add_fusion.place_ref, bf16[512,3584]{1,0:T(8,128)(2,1)} %refs_0_.3, bf16[512,3584]{1,0:T(8,128)(2,1)} %copy-done.5), custom_call_target="tpu_custom_call" | custom-call | bytes 7340032 | tf_op jit(solution)/shard_map/near_output/pallas_call | solution.py:93
  67.2 0.4 half_product.3.partial_ref
  67.6 0.4 half_product.2.partial_ref
  68.0 0.0 collective-permute-done.10.refs_0_
  68.0 1.0 output.2.refs_0_
  69.0 0.0 collective-permute-done.11.refs_1_
  69.0 1.0 output.3
  69.9 28.6 %all_to_all.17.x_ref = bf16[32,8,1792]{2,1,0:T(8,128)(2,1)S(1)} all-to-all(bf16[32,8,1792]{2,1,0:T(8,128)(2,1)S(1)} %bitcast.6), channel_id=1, replica_groups=mesh['groups'=1,'tensor'=16,'replica'=2] {'replica','tensor'}, dimensions={0} | all-to-all | bytes 1835008 | tf_op jit(solution)/shard_map/all_to_all | solution.py:377
  98.5 0.8 combine.1
  (21 shorter events, 0.1 us)
Async XLA Ops:
  0.0 6.1 %collective-permute-start = (bf16[8,1536]{1,0:T(8,128)(2,1)}, bf16[8,1536]{1,0:T(8,128)(2,1)S(1)}, u32[]{:S(2)}, u32[]{:S(2)}) collective-permute-start(bf16[8,1536]{1,0:T(8,128)(2,1)} %refs_3_.1), channel_id=1, source_target_pairs={{0,16},{2,18},{4,20},{6,22},{8,24},{10,26},{12,28},{14,30},{16,0},... | collective-permute-start | bytes 73736 | tf_op jit(solution)/shard_map/ppermute | solution.py:289
  6.1 5.1 %collective-permute-start.3 = (bf16[16,1536]{1,0:T(8,128)(2,1)S(1)}, bf16[16,1536]{1,0:T(8,128)(2,1)S(1)}, u32[]{:S(2)}, u32[]{:S(2)}) collective-permute-start(bf16[16,1536]{1,0:T(8,128)(2,1)S(1)} %constant_dynamic-update-slice_fusion.refs_0_), channel_id=1, source_target_pairs={{0,12},{2,14},{4,8},{6,10},{8,4},{10,6},{12,0},{14,2},{16,28},{18,... | collective-permute-start | bytes 147464 | tf_op jit(solution)/shard_map/ppermute | solution.py:289
  9.0 4.1 %collective-permute-start.2 = (bf16[16,1536]{1,0:T(8,128)(2,1)S(1)}, bf16[16,1536]{1,0:T(8,128)(2,1)S(1)}, u32[]{:S(2)}, u32[]{:S(2)}) collective-permute-start(bf16[16,1536]{1,0:T(8,128)(2,1)S(1)} %constant_dynamic-update-slice_fusion.refs_0_), channel_id=1, source_target_pairs={{0,4},{2,6},{4,0},{6,2},{8,12},{10,14},{12,8},{14,10},{16,20},{18,... | collective-permute-start | bytes 147464 | tf_op jit(solution)/shard_map/ppermute | solution.py:289
  9.5 4.1 %collective-permute-start.1 = (bf16[16,1536]{1,0:T(8,128)(2,1)S(1)}, bf16[16,1536]{1,0:T(8,128)(2,1)S(1)}, u32[]{:S(2)}, u32[]{:S(2)}) collective-permute-start(bf16[16,1536]{1,0:T(8,128)(2,1)S(1)} %constant_dynamic-update-slice_fusion.refs_0_), channel_id=1, source_target_pairs={{0,8},{2,10},{4,12},{6,14},{8,0},{10,2},{12,4},{14,6},{16,24},{18,... | collective-permute-start | bytes 147464 | tf_op jit(solution)/shard_map/ppermute | solution.py:289
  9.6 4.1 %collective-permute-start.4 = (bf16[16,1536]{1,0:T(8,128)(2,1)S(1)}, bf16[16,1536]{1,0:T(8,128)(2,1)S(1)}, u32[]{:S(2)}, u32[]{:S(2)}) collective-permute-start(bf16[16,1536]{1,0:T(8,128)(2,1)S(1)} %constant_dynamic-update-slice_fusion.refs_0_), channel_id=1, source_target_pairs={{0,2},{2,0},{4,6},{6,4},{8,10},{10,8},{12,14},{14,12},{16,18},{18,... | collective-permute-start | bytes 147464 | tf_op jit(solution)/shard_map/ppermute | solution.py:289
  11.2 2.5 %collective-permute-start.7 = (bf16[16,1536]{1,0:T(8,128)(2,1)S(1)}, bf16[16,1536]{1,0:T(8,128)(2,1)S(1)}, u32[]{:S(2)}, u32[]{:S(2)}) collective-permute-start(bf16[16,1536]{1,0:T(8,128)(2,1)S(1)} %collective-permute-done.3.refs_3_), channel_id=1, source_target_pairs={{0,2},{2,0},{4,6},{6,4},{8,10},{10,8},{12,14},{14,12},{16,18},{18,... | collective-permute-start | bytes 147464 | tf_op jit(solution)/shard_map/ppermute | solution.py:289
  13.0 1.2 %collective-permute-start.6 = (bf16[16,1536]{1,0:T(8,128)(2,1)S(1)}, bf16[16,1536]{1,0:T(8,128)(2,1)S(1)}, u32[]{:S(2)}, u32[]{:S(2)}) collective-permute-start(bf16[16,1536]{1,0:T(8,128)(2,1)S(1)} %collective-permute-done.2.refs_2_), channel_id=1, source_target_pairs={{0,2},{2,0},{4,6},{6,4},{8,10},{10,8},{12,14},{14,12},{16,18},{18,... | collective-permute-start | bytes 147464 | tf_op jit(solution)/shard_map/ppermute | solution.py:289
  13.6 1.2 %collective-permute-start.5 = (bf16[16,1536]{1,0:T(8,128)(2,1)S(1)}, bf16[16,1536]{1,0:T(8,128)(2,1)S(1)}, u32[]{:S(2)}, u32[]{:S(2)}) collective-permute-start(bf16[16,1536]{1,0:T(8,128)(2,1)S(1)} %collective-permute-done.1.refs_1_), channel_id=1, source_target_pairs={{0,2},{2,0},{4,6},{6,4},{8,10},{10,8},{12,14},{14,12},{16,18},{18,... | collective-permute-start | bytes 147464 | tf_op jit(solution)/shard_map/ppermute | solution.py:289
  13.6 24.9 %copy-start = (bf16[2,1024,576]{1,2,0:T(8,128)(2,1)S(1)}, bf16[2,1024,576]{1,2,0:T(8,128)(2,1)}, u32[]{:S(2)}) copy-start(bf16[2,1024,576]{1,2,0:T(8,128)(2,1)} %param.17) | copy-start | bytes 7077892
  13.6 24.9 %copy-start.2 = (bf16[8,576]{1,0:T(8,128)(2,1)S(1)}, bf16[8,576]{1,0:T(8,128)(2,1)}, u32[]{:S(2)}) copy-start(bf16[8,576]{1,0:T(8,128)(2,1)} %new_ref.1) | copy-start | bytes 27652
  13.6 24.9 %copy-start.3 = (s32[2]{0:T(128)S(1)}, s32[2]{0:T(128)}, u32[]{:S(2)}) copy-start(s32[2]{0:T(128)} %len_ref.1) | copy-start | bytes 28
  13.6 24.9 %copy-start.4 = (s32[2]{0:T(128)S(1)}, s32[2]{0:T(128)}, u32[]{:S(2)}) copy-start(s32[2]{0:T(128)} %count_ref.1) | copy-start | bytes 28
  38.4 20.2 %copy-start.1 = (bf16[4,512,128]{2,1,0:T(8,128)(2,1)S(1)}, bf16[4,512,128]{2,1,0:T(8,128)(2,1)}, u32[]{:S(2)}) copy-start(bf16[4,512,128]{2,1,0:T(8,128)(2,1)} %uv_ref.1) | copy-start | bytes 1572868
  38.4 20.2 %collective-permute-start.8 = (bf16[512,3584]{1,0:T(8,128)(2,1)}, bf16[512,3584]{1,0:T(8,128)(2,1)S(1)}, u32[]{:S(2)}, u32[]{:S(2)}) collective-permute-start(bf16[512,3584]{1,0:T(8,128)(2,1)} %refs_0_.3), channel_id=1, source_target_pairs={{0,2},{2,0},{4,6},{6,4},{8,10},{10,8},{12,14},{14,12},{16,18},{18,... | collective-permute-start | bytes 11010056 | tf_op jit(solution)/shard_map/ppermute | solution.py:289
  58.6 6.0 %copy-start.5 = (bf16[512,3584]{1,0:T(8,128)(2,1)}, bf16[512,3584]{1,0:T(8,128)(2,1)S(1)}, u32[]{:S(2)}) copy-start(bf16[512,3584]{1,0:T(8,128)(2,1)S(1)} %collective-permute-done.8.refs_1_) | copy-start | bytes 11010052
  58.9 5.6 %collective-permute-start.9 = (bf16[128,512]{1,0:T(8,128)(2,1)S(1)}, bf16[128,512]{1,0:T(8,128)(2,1)S(1)}, u32[]{:S(2)}, u32[]{:S(2)}) collective-permute-start(bf16[128,512]{1,0:T(8,128)(2,1)S(1)} %values.1.refs_1_), channel_id=1, source_target_pairs={{0,1},{1,0},{2,3},{3,2},{4,5},{5,4},{6,7},{7,6},{8,9},{9,8},{10,11... | collective-permute-start | bytes 393224 | tf_op jit(solution)/shard_map/ppermute | solution.py:289
  60.5 7.5 %collective-permute-start.10 = (bf16[128,512]{1,0:T(8,128)(2,1)S(1)}, bf16[128,512]{1,0:T(8,128)(2,1)S(1)}, u32[]{:S(2)}, u32[]{:S(2)}) collective-permute-start(bf16[128,512]{1,0:T(8,128)(2,1)S(1)} %values.1.refs_1_), channel_id=1, source_target_pairs={{0,2},{2,0},{4,6},{6,4},{8,10},{10,8},{12,14},{14,12},{16,18},{18,... | collective-permute-start | bytes 393224 | tf_op jit(solution)/shard_map/ppermute | solution.py:289
  64.5 4.4 %collective-permute-start.11 = (bf16[128,512]{1,0:T(8,128)(2,1)S(1)}, bf16[128,512]{1,0:T(8,128)(2,1)S(1)}, u32[]{:S(2)}, u32[]{:S(2)}) collective-permute-start(bf16[128,512]{1,0:T(8,128)(2,1)S(1)} %collective-permute-done.9.refs_1_), channel_id=1, source_target_pairs={{0,2},{2,0},{4,6},{6,4},{8,10},{10,8},{12,14},{14,12},{16,18},{18,... | collective-permute-start | bytes 393224 | tf_op jit(solution)/shard_map/ppermute | solution.py:289

commit v6 on v5

--- a/solution.py
+++ b/solution.py
@@ -247,17 +247,14 @@
 
 def output_kernel(done, place_ref, w_ref, partial_ref, *refs):
     ready_refs, value_refs, out_ref = refs[:done], refs[done:-1], refs[-1]
-    rows, half = out_ref.shape[1:]
+    rows = out_ref.shape[1]
     other = jnp.concatenate([ref[...] for ref in value_refs], axis=0)
     base = place_ref[1] if done else 0
     for k in range(done):
         out_ref[base ^ k] = ready_refs[k][0]
-    tile = tile_of(half)
-    for at in range(0, half, tile):
-        part = partial_ref[:, at : at + tile] + mm(other, w_ref[:, at : at + tile])
-        part = part.astype(bf16)
-        for k in range(len(value_refs)):
-            out_ref[base ^ (done + k), :, at : at + tile] = part[k * rows : (k + 1) * rows]
+    part = (partial_ref[...] + mm(other, w_ref[...])).astype(bf16)
+    for k in range(len(value_refs)):
+        out_ref[base ^ (done + k)] = part[k * rows : (k + 1) * rows]
 
 
 def output_rows(ready, blocks, place, weights, partial, other, params):

time: 99.5 us -> 99.5 us (level)
  no operation moved by 1% of the time
where the time goes in v6:
time: 99.5 us; the launch traced here: 99.3 us
  blocking collectives  67.7 us (68%)
  Pallas kernels  12.7 us (13%)
  waiting for transfers between devices  9.34 us (9%)
  starting transfers between devices  9.25 us (9%)
    all_to_all x1, blocking collectives, local_step(): lax.all_to_all(product, ('replica', 'tensor'), split_axis=0, concat_axis=...  28.6 us
    all_to_all x1, blocking collectives, local_step(): lax.all_to_all(queries, 'tensor', split_axis=0, concat_axis=0, tiled=True)  22.1 us
    all_to_all x1, blocking collectives, local_step(): lax.all_to_all(latent, 'tensor', split_axis=0, concat_axis=0, tiled=True)  17.1 us
    ppermute x12, waiting for transfers between devices, step(): return lax.ppermute(x, axis, [(i, i ^ k) for i in range(size)])  9.34 us
    ppermute x12, starting transfers between devices, step(): return lax.ppermute(x, axis, [(i, i ^ k) for i in range(size)])  9.25 us
    pallas_call x1, Pallas kernels, local_step(): pl.pallas_call(functools.partial(attend_kernel, reqs, drafts, heads), out...  2.95 us
    pallas_call x1, Pallas kernels, fetch_halves(): pl.pallas_call(halves_kernel, out_shape=[pltpu.VMEM((depth, width), bf16)...  2.61 us
  transfers between devices with their start and end apart: 12, of which 7 were waited for; matrix products, arithmetic and copies ran while one was open for 0% of the time, Pallas kernels for 9%

profile of v6, /device:TPU:0, one launch (start us, length us, event | category | flops | bytes accessed | tf_op | source)
XLA Modules:
  0.0 99.3 jit_solution(1091281860462267764)
XLA Ops:
  0.0 4.1 %collective-permute-start = (bf16[8,1536]{1,0:T(8,128)(2,1)}, bf16[8,1536]{1,0:T(8,128)(2,1)S(1)}, u32[]{:S(2)}, u32[]{:S(2)}) collective-permute-start(bf16[8,1536]{1,0:T(8,128)(2,1)} %refs_3_.1), channel_id=1, source_target_pairs={{0,16},{2,18},{4,20},{6,22},{8,24},{10,26},{12,28},{14,30},{16,0},... | collective-permute-start | bytes 73736 | tf_op jit(solution)/shard_map/ppermute | solution.py:286
  4.1 1.8 %shard_map.100 = (bf16[1536,768]{1,0:T(8,128)(2,1)S(1)}, bf16[512,512]{1,0:T(8,128)(2,1)S(1)}, f32[1536]{0:T(1024)S(1)}, bf16[8,1536]{1,0:T(8,128)(2,1)S(1)}) custom-call(bf16[1536,768]{1,0:T(8,128)(2,1)} %refs_0_.2, bf16[512,512]{1,0:T(8,128)(2,1)} %bitcast.8, f32[1536]{0:T(1024)} %refs_2_.1, bf16[8,1536]{1,0:T(8,128)(2,1)} %refs_3_.1), custom_call_target="tpu_custom_call" | custom-call | bytes 5822464 | tf_op jit(solution)/shard_map/pallas_call | solution.py:65
  5.9 0.2 collective-permute-done
  6.1 2.9 %collective-permute-start.3 = (bf16[16,1536]{1,0:T(8,128)(2,1)S(1)}, bf16[16,1536]{1,0:T(8,128)(2,1)S(1)}, u32[]{:S(2)}, u32[]{:S(2)}) collective-permute-start(bf16[16,1536]{1,0:T(8,128)(2,1)S(1)} %constant_dynamic-update-slice_fusion.refs_0_), channel_id=1, source_target_pairs={{0,12},{2,14},{4,8},{6,10},{8,4},{10,6},{12,0},{14,2},{16,28},{18,... | collective-permute-start | bytes 147464 | tf_op jit(solution)/shard_map/ppermute | solution.py:286
  9.0 0.5 collective-permute-start.2
  9.5 0.1 collective-permute-start.1
  9.6 1.6 %collective-permute-done.3.refs_3_ = bf16[16,1536]{1,0:T(8,128)(2,1)S(1)} collective-permute-done((bf16[16,1536]{1,0:T(8,128)(2,1)S(1)}, bf16[16,1536]{1,0:T(8,128)(2,1)S(1)}, u32[]{:S(2)}, u32[]{:S(2)}) %collective-permute-start.3) | collective-permute-done | bytes 49184 | tf_op jit(solution)/shard_map/ppermute | solution.py:286
  11.2 1.9 %collective-permute-done.2.refs_2_ = bf16[16,1536]{1,0:T(8,128)(2,1)S(1)} collective-permute-done((bf16[16,1536]{1,0:T(8,128)(2,1)S(1)}, bf16[16,1536]{1,0:T(8,128)(2,1)S(1)}, u32[]{:S(2)}, u32[]{:S(2)}) %collective-permute-start.2) | collective-permute-done | bytes 49184 | tf_op jit(solution)/shard_map/ppermute | solution.py:286
  13.0 0.5 collective-permute-done.1.refs_1_
  13.6 0.0 collective-permute-start.5
  13.6 0.1 pad_add_fusion.place_ref
  13.6 0.0 collective-permute-done.4.refs_4_
  13.7 0.6 collective-permute-done.6.refs_6_
  14.3 0.5 collective-permute-done.5.refs_5_
  14.8 1.5 %query.1 = bf16[16,144,128]{2,1,0:T(8,128)(2,1)S(1)} custom-call(s32[3]{0:T(128)S(1)} %pad_add_fusion.place_ref, bf16[16,1536]{1,0:T(8,128)(2,1)S(1)} %constant_dynamic-update-slice_fusion.refs_0_, bf16[16,1536]{1,0:T(8,128)(2,1)S(1)} %collective-permute-done.1.refs_1_, bf16[16,1536]{1,0:T(8,128)(2,1)S(1)} %collective-permute-done.2.refs_2_, ...), custom_call_target="tpu_custom_call" | custom-call | tf_op jit(solution)/shard_map/query/pallas_call | solution.py:325
  16.3 22.1 %all_to_all.15.q_ref = bf16[16,144,128]{2,1,0:T(8,128)(2,1)S(1)} all-to-all(bf16[16,144,128]{2,1,0:T(8,128)(2,1)S(1)} %query.1), channel_id=1, replica_groups=mesh['groups'=1,'tensor'=16,'replica'=2] {'tensor'}, dimensions={0} | all-to-all | bytes 1179648 | tf_op jit(solution)/shard_map/all_to_all | solution.py:333
  38.4 0.1 collective-permute-start.8
  38.5 2.9 %attend.1 = bf16[16,32,512]{2,1,0:T(8,128)(2,1)S(1)} custom-call(s32[2]{0:T(128)S(1)} %copy-done.3, s32[2]{0:T(128)S(1)} %copy-done.4, bf16[16,144,128]{2,1,0:T(8,128)(2,1)S(1)} %all_to_all.15.q_ref, f32[1,128]{1,0:T(1,128)S(1)} %fusion.3.frequency_ref, bf16[8,576]{1,0:T(8,128)(2,1)S(1)} %copy-done.2, bf16[2,576,1024]{2,1,0:T(8,128)(2,1)S(1)} %bitcast.7), custom_call_target="tpu_custom_call" | custom-call | tf_op jit(solution)/shard_map/attend/pallas_call | solution.py:343
  41.5 17.1 %all_to_all.16.latent_ref = bf16[16,32,512]{2,1,0:T(8,128)(2,1)S(1)} all-to-all(bf16[16,32,512]{2,1,0:T(8,128)(2,1)S(1)} %attend.1), channel_id=1, replica_groups=mesh['groups'=1,'tensor'=16,'replica'=2] {'tensor'}, dimensions={0} | all-to-all | bytes 1048576 | tf_op jit(solution)/shard_map/all_to_all | solution.py:351
  58.6 0.4 values.1.refs_1_
  58.9 1.6 %collective-permute-start.9 = (bf16[128,512]{1,0:T(8,128)(2,1)S(1)}, bf16[128,512]{1,0:T(8,128)(2,1)S(1)}, u32[]{:S(2)}, u32[]{:S(2)}) collective-permute-start(bf16[128,512]{1,0:T(8,128)(2,1)S(1)} %values.1.refs_1_), channel_id=1, source_target_pairs={{0,1},{1,0},{2,3},{3,2},{4,5},{5,4},{6,7},{7,6},{8,9},{9,8},{10,11... | collective-permute-start | bytes 393224 | tf_op jit(solution)/shard_map/ppermute | solution.py:286
  60.5 4.0 %collective-permute-done.9.refs_1_ = bf16[128,512]{1,0:T(8,128)(2,1)S(1)} collective-permute-done((bf16[128,512]{1,0:T(8,128)(2,1)S(1)}, bf16[128,512]{1,0:T(8,128)(2,1)S(1)}, u32[]{:S(2)}, u32[]{:S(2)}) %collective-permute-start.9) | collective-permute-done | bytes 131104 | tf_op jit(solution)/shard_map/ppermute | solution.py:286
  64.5 0.0 collective-permute-start.11
  64.6 2.6 %near_output.1 = (bf16[512,1792]{1,0:T(8,128)(2,1)S(1)}, bf16[512,1792]{1,0:T(8,128)(2,1)S(1)}) custom-call(s32[3]{0:T(128)S(1)} %pad_add_fusion.place_ref, bf16[512,3584]{1,0:T(8,128)(2,1)} %refs_0_.3, bf16[512,3584]{1,0:T(8,128)(2,1)} %copy-done.5), custom_call_target="tpu_custom_call" | custom-call | bytes 7340032 | tf_op jit(solution)/shard_map/near_output/pallas_call | solution.py:93
  67.2 0.4 half_product.3.partial_ref
  67.6 0.4 half_product.2.partial_ref
  68.0 0.0 collective-permute-done.10.refs_0_
  68.0 1.0 output.2.refs_0_
  69.0 0.0 collective-permute-done.11.refs_1_
  69.0 1.0 output.3
  69.9 28.6 %all_to_all.17.x_ref = bf16[32,8,1792]{2,1,0:T(8,128)(2,1)S(1)} all-to-all(bf16[32,8,1792]{2,1,0:T(8,128)(2,1)S(1)} %bitcast.6), channel_id=1, replica_groups=mesh['groups'=1,'tensor'=16,'replica'=2] {'replica','tensor'}, dimensions={0} | all-to-all | bytes 1835008 | tf_op jit(solution)/shard_map/all_to_all | solution.py:374
  98.5 0.8 combine.1
  (21 shorter events, 0.1 us)
Async XLA Ops:
  0.0 6.1 %collective-permute-start = (bf16[8,1536]{1,0:T(8,128)(2,1)}, bf16[8,1536]{1,0:T(8,128)(2,1)S(1)}, u32[]{:S(2)}, u32[]{:S(2)}) collective-permute-start(bf16[8,1536]{1,0:T(8,128)(2,1)} %refs_3_.1), channel_id=1, source_target_pairs={{0,16},{2,18},{4,20},{6,22},{8,24},{10,26},{12,28},{14,30},{16,0},... | collective-permute-start | bytes 73736 | tf_op jit(solution)/shard_map/ppermute | solution.py:286
  6.1 5.1 %collective-permute-start.3 = (bf16[16,1536]{1,0:T(8,128)(2,1)S(1)}, bf16[16,1536]{1,0:T(8,128)(2,1)S(1)}, u32[]{:S(2)}, u32[]{:S(2)}) collective-permute-start(bf16[16,1536]{1,0:T(8,128)(2,1)S(1)} %constant_dynamic-update-slice_fusion.refs_0_), channel_id=1, source_target_pairs={{0,12},{2,14},{4,8},{6,10},{8,4},{10,6},{12,0},{14,2},{16,28},{18,... | collective-permute-start | bytes 147464 | tf_op jit(solution)/shard_map/ppermute | solution.py:286
  9.0 4.1 %collective-permute-start.2 = (bf16[16,1536]{1,0:T(8,128)(2,1)S(1)}, bf16[16,1536]{1,0:T(8,128)(2,1)S(1)}, u32[]{:S(2)}, u32[]{:S(2)}) collective-permute-start(bf16[16,1536]{1,0:T(8,128)(2,1)S(1)} %constant_dynamic-update-slice_fusion.refs_0_), channel_id=1, source_target_pairs={{0,4},{2,6},{4,0},{6,2},{8,12},{10,14},{12,8},{14,10},{16,20},{18,... | collective-permute-start | bytes 147464 | tf_op jit(solution)/shard_map/ppermute | solution.py:286
  9.5 4.1 %collective-permute-start.1 = (bf16[16,1536]{1,0:T(8,128)(2,1)S(1)}, bf16[16,1536]{1,0:T(8,128)(2,1)S(1)}, u32[]{:S(2)}, u32[]{:S(2)}) collective-permute-start(bf16[16,1536]{1,0:T(8,128)(2,1)S(1)} %constant_dynamic-update-slice_fusion.refs_0_), channel_id=1, source_target_pairs={{0,8},{2,10},{4,12},{6,14},{8,0},{10,2},{12,4},{14,6},{16,24},{18,... | collective-permute-start | bytes 147464 | tf_op jit(solution)/shard_map/ppermute | solution.py:286
  9.6 4.1 %collective-permute-start.4 = (bf16[16,1536]{1,0:T(8,128)(2,1)S(1)}, bf16[16,1536]{1,0:T(8,128)(2,1)S(1)}, u32[]{:S(2)}, u32[]{:S(2)}) collective-permute-start(bf16[16,1536]{1,0:T(8,128)(2,1)S(1)} %constant_dynamic-update-slice_fusion.refs_0_), channel_id=1, source_target_pairs={{0,2},{2,0},{4,6},{6,4},{8,10},{10,8},{12,14},{14,12},{16,18},{18,... | collective-permute-start | bytes 147464 | tf_op jit(solution)/shard_map/ppermute | solution.py:286
  11.2 2.5 %collective-permute-start.7 = (bf16[16,1536]{1,0:T(8,128)(2,1)S(1)}, bf16[16,1536]{1,0:T(8,128)(2,1)S(1)}, u32[]{:S(2)}, u32[]{:S(2)}) collective-permute-start(bf16[16,1536]{1,0:T(8,128)(2,1)S(1)} %collective-permute-done.3.refs_3_), channel_id=1, source_target_pairs={{0,2},{2,0},{4,6},{6,4},{8,10},{10,8},{12,14},{14,12},{16,18},{18,... | collective-permute-start | bytes 147464 | tf_op jit(solution)/shard_map/ppermute | solution.py:286
  13.0 1.2 %collective-permute-start.6 = (bf16[16,1536]{1,0:T(8,128)(2,1)S(1)}, bf16[16,1536]{1,0:T(8,128)(2,1)S(1)}, u32[]{:S(2)}, u32[]{:S(2)}) collective-permute-start(bf16[16,1536]{1,0:T(8,128)(2,1)S(1)} %collective-permute-done.2.refs_2_), channel_id=1, source_target_pairs={{0,2},{2,0},{4,6},{6,4},{8,10},{10,8},{12,14},{14,12},{16,18},{18,... | collective-permute-start | bytes 147464 | tf_op jit(solution)/shard_map/ppermute | solution.py:286
  13.6 1.2 %collective-permute-start.5 = (bf16[16,1536]{1,0:T(8,128)(2,1)S(1)}, bf16[16,1536]{1,0:T(8,128)(2,1)S(1)}, u32[]{:S(2)}, u32[]{:S(2)}) collective-permute-start(bf16[16,1536]{1,0:T(8,128)(2,1)S(1)} %collective-permute-done.1.refs_1_), channel_id=1, source_target_pairs={{0,2},{2,0},{4,6},{6,4},{8,10},{10,8},{12,14},{14,12},{16,18},{18,... | collective-permute-start | bytes 147464 | tf_op jit(solution)/shard_map/ppermute | solution.py:286
  13.6 24.9 %copy-start = (bf16[2,1024,576]{1,2,0:T(8,128)(2,1)S(1)}, bf16[2,1024,576]{1,2,0:T(8,128)(2,1)}, u32[]{:S(2)}) copy-start(bf16[2,1024,576]{1,2,0:T(8,128)(2,1)} %param.17) | copy-start | bytes 7077892
  13.6 24.9 %copy-start.2 = (bf16[8,576]{1,0:T(8,128)(2,1)S(1)}, bf16[8,576]{1,0:T(8,128)(2,1)}, u32[]{:S(2)}) copy-start(bf16[8,576]{1,0:T(8,128)(2,1)} %new_ref.1) | copy-start | bytes 27652
  13.6 24.9 %copy-start.3 = (s32[2]{0:T(128)S(1)}, s32[2]{0:T(128)}, u32[]{:S(2)}) copy-start(s32[2]{0:T(128)} %len_ref.1) | copy-start | bytes 28
  13.6 24.9 %copy-start.4 = (s32[2]{0:T(128)S(1)}, s32[2]{0:T(128)}, u32[]{:S(2)}) copy-start(s32[2]{0:T(128)} %count_ref.1) | copy-start | bytes 28
  38.4 20.2 %copy-start.1 = (bf16[4,512,128]{2,1,0:T(8,128)(2,1)S(1)}, bf16[4,512,128]{2,1,0:T(8,128)(2,1)}, u32[]{:S(2)}) copy-start(bf16[4,512,128]{2,1,0:T(8,128)(2,1)} %uv_ref.1) | copy-start | bytes 1572868
  38.4 20.2 %collective-permute-start.8 = (bf16[512,3584]{1,0:T(8,128)(2,1)}, bf16[512,3584]{1,0:T(8,128)(2,1)S(1)}, u32[]{:S(2)}, u32[]{:S(2)}) collective-permute-start(bf16[512,3584]{1,0:T(8,128)(2,1)} %refs_0_.3), channel_id=1, source_target_pairs={{0,2},{2,0},{4,6},{6,4},{8,10},{10,8},{12,14},{14,12},{16,18},{18,... | collective-permute-start | bytes 11010056 | tf_op jit(solution)/shard_map/ppermute | solution.py:286
  58.6 6.0 %copy-start.5 = (bf16[512,3584]{1,0:T(8,128)(2,1)}, bf16[512,3584]{1,0:T(8,128)(2,1)S(1)}, u32[]{:S(2)}) copy-start(bf16[512,3584]{1,0:T(8,128)(2,1)S(1)} %collective-permute-done.8.refs_1_) | copy-start | bytes 11010052
  58.9 5.6 %collective-permute-start.9 = (bf16[128,512]{1,0:T(8,128)(2,1)S(1)}, bf16[128,512]{1,0:T(8,128)(2,1)S(1)}, u32[]{:S(2)}, u32[]{:S(2)}) collective-permute-start(bf16[128,512]{1,0:T(8,128)(2,1)S(1)} %values.1.refs_1_), channel_id=1, source_target_pairs={{0,1},{1,0},{2,3},{3,2},{4,5},{5,4},{6,7},{7,6},{8,9},{9,8},{10,11... | collective-permute-start | bytes 393224 | tf_op jit(solution)/shard_map/ppermute | solution.py:286
  60.5 7.5 %collective-permute-start.10 = (bf16[128,512]{1,0:T(8,128)(2,1)S(1)}, bf16[128,512]{1,0:T(8,128)(2,1)S(1)}, u32[]{:S(2)}, u32[]{:S(2)}) collective-permute-start(bf16[128,512]{1,0:T(8,128)(2,1)S(1)} %values.1.refs_1_), channel_id=1, source_target_pairs={{0,2},{2,0},{4,6},{6,4},{8,10},{10,8},{12,14},{14,12},{16,18},{18,... | collective-permute-start | bytes 393224 | tf_op jit(solution)/shard_map/ppermute | solution.py:286
  64.5 4.4 %collective-permute-start.11 = (bf16[128,512]{1,0:T(8,128)(2,1)S(1)}, bf16[128,512]{1,0:T(8,128)(2,1)S(1)}, u32[]{:S(2)}, u32[]{:S(2)}) collective-permute-start(bf16[128,512]{1,0:T(8,128)(2,1)S(1)} %collective-permute-done.9.refs_1_), channel_id=1, source_target_pairs={{0,2},{2,0},{4,6},{6,4},{8,10},{10,8},{12,14},{14,12},{16,18},{18,... | collective-permute-start | bytes 393224 | tf_op jit(solution)/shard_map/ppermute | solution.py:286

commit v7 on v6

--- a/solution.py
+++ b/solution.py
@@ -121,9 +121,10 @@
     return [stack(firsts), stack(seconds)]
 
 
-def query_kernel(reqs, drafts, heads, place_ref, *refs):
+def query_kernel(reqs, drafts, heads, *refs):
     *x_refs, gain_ref, up_ref, uk_ref, out_ref = refs
     owners = out_ref.shape[0]
+    me = lax.axis_index("tensor")
     hd = heads * drafts
     x = jnp.concatenate([x_ref[...] for x_ref in x_refs], axis=0).astype(f32)
     scaled = x * lax.rsqrt(jnp.mean(x * x, axis=-1, keepdims=True) + rms_eps)
@@ -142,7 +143,7 @@
     ]
     for k in range(owners):
         distance = int(format(k, f"0{owners.bit_length() - 1}b")[::-1], 2)
-        target = place_ref[2] ^ distance
+        target = me ^ distance
         for q in range(reqs):
             for c in range(chunks):
                 at = (q * chunks + c) * hd
@@ -245,11 +246,11 @@
     )(weights, *pieces)
 
 
-def output_kernel(done, place_ref, w_ref, partial_ref, *refs):
+def output_kernel(done, w_ref, partial_ref, *refs):
     ready_refs, value_refs, out_ref = refs[:done], refs[done:-1], refs[-1]
     rows = out_ref.shape[1]
     other = jnp.concatenate([ref[...] for ref in value_refs], axis=0)
-    base = place_ref[1] if done else 0
+    base = lax.axis_index("replica") if done else 0
     for k in range(done):
         out_ref[base ^ k] = ready_refs[k][0]
     part = (partial_ref[...] + mm(other, w_ref[...])).astype(bf16)
@@ -257,13 +258,13 @@
         out_ref[base ^ (done + k)] = part[k * rows : (k + 1) * rows]
 
 
-def output_rows(ready, blocks, place, weights, partial, other, params):
-    operands = [place, weights, partial, *ready, *other]
+def output_rows(ready, blocks, weights, partial, other, params):
+    operands = [weights, partial, *ready, *other]
     shape = (blocks, other[0].shape[0], weights.shape[1])
     return pl.pallas_call(
         functools.partial(output_kernel, len(ready)),
         out_shape=jax.ShapeDtypeStruct(shape, bf16),
-        in_specs=[smem_spec()] + [vmem_spec()] * (len(operands) - 1),
+        in_specs=[vmem_spec()] * len(operands),
         out_specs=vmem_spec(),
         compiler_params=params,
         name="output",
@@ -297,7 +298,7 @@
     me = lax.axis_index("tensor")
     core = me % 2
 
-    place = jnp.stack([core, lax.axis_index("replica"), me]).astype(jnp.int32)
+    place = core[None].astype(jnp.int32)
     w_uk = w_uk.reshape(heads * NOPE, LATENT)
     near = fetch((q_up, w_uk, q_gain, q_latent), FETCH_VMEM)
 
@@ -325,11 +326,11 @@
     queries = pl.pallas_call(
         functools.partial(query_kernel, reqs, drafts, heads),
         out_shape=jax.ShapeDtypeStruct((owners, packed, LANES), bf16),
-        in_specs=[smem_spec()] + [vmem_spec()] * (len(parts) + 3),
+        in_specs=[vmem_spec()] * (len(parts) + 3),
         out_specs=vmem_spec(),
         compiler_params=params,
         name="query",
-    )(place, *parts, gain, q_up, w_uk)
+    )(*parts, gain, q_up, w_uk)
     arrived = lax.all_to_all(queries, "tensor", split_axis=0, concat_axis=0, tiled=True)
 
     arrived, w_late = lax.optimization_barrier((arrived, w_o))
@@ -364,12 +365,12 @@
     w_own, w_other = fetch_halves(place, (w_own, w_other), half)
     other = [step(own[0], "tensor", owners, 1)]
     product = half_product(w_own, own[:1], params)
-    product = output_rows((), 1, place, w_other, product, other, params)
+    product = output_rows((), 1, w_other, product, other, params)
     if replicas > 1:
         other = [step(own[1], "tensor", owners, 1)]
         other = other + [step(piece, "tensor", owners, 1) for piece in own[2:]]
         partial = half_product(w_own, own[1:], params)
-        product = output_rows((product,), replicas, place, w_other, partial, other, params)
+        product = output_rows((product,), replicas, w_other, partial, other, params)
     product = product.reshape(replicas * owners, rows_dev, half)
     placed = lax.all_to_all(product, ("replica", "tensor"), split_axis=0, concat_axis=0, tiled=True)
     return pl.pallas_call(

time: 99.5 us -> 97.4 us (0.979)
  Pallas kernels: 12.7 us -> 10.7 us
    pallas_call x2, Pallas kernels: 1.9 us -> 0.85 us  [output_rows(): pl.pallas_call(functools.partial(output_kernel, len(ready)), out_shape=ja...]
  transfers between devices with their start and end apart: 12 -> 12, of which waited for: 7 -> 7; matrix products, arithmetic and copies ran while one was open for 0% -> 0% of each run, Pallas kernels for 9% -> 8%
where the time goes in v7:
time: 97.4 us; the launch traced here: 97.2 us
  blocking collectives  67.7 us (70%)
  Pallas kernels  10.7 us (11%)
  starting transfers between devices  9.32 us (10%)
  waiting for transfers between devices  9.29 us (10%)
    all_to_all x1, blocking collectives, local_step(): lax.all_to_all(product, ('replica', 'tensor'), split_axis=0, concat_axis=...  28.6 us
    all_to_all x1, blocking collectives, local_step(): lax.all_to_all(queries, 'tensor', split_axis=0, concat_axis=0, tiled=True)  22.1 us
    all_to_all x1, blocking collectives, local_step(): lax.all_to_all(latent, 'tensor', split_axis=0, concat_axis=0, tiled=True)  17.1 us
    ppermute x12, starting transfers between devices, step(): return lax.ppermute(x, axis, [(i, i ^ k) for i in range(size)])  9.32 us
    ppermute x12, waiting for transfers between devices, step(): return lax.ppermute(x, axis, [(i, i ^ k) for i in range(size)])  9.29 us
    pallas_call x1, Pallas kernels, local_step(): pl.pallas_call(functools.partial(attend_kernel, reqs, drafts, heads), out...  2.93 us
    pallas_call x1, Pallas kernels, fetch_halves(): pl.pallas_call(halves_kernel, out_shape=[pltpu.VMEM((depth, width), bf16)...  2.07 us
  transfers between devices with their start and end apart: 12, of which 7 were waited for; matrix products, arithmetic and copies ran while one was open for 0% of the time, Pallas kernels for 8%

profile of v7, /device:TPU:0, one launch (start us, length us, event | category | flops | bytes accessed | tf_op | source)
XLA Modules:
  0.0 97.2 jit_solution(548734433284354671)
XLA Ops:
  0.0 4.1 %collective-permute-start = (bf16[8,1536]{1,0:T(8,128)(2,1)}, bf16[8,1536]{1,0:T(8,128)(2,1)S(1)}, u32[]{:S(2)}, u32[]{:S(2)}) collective-permute-start(bf16[8,1536]{1,0:T(8,128)(2,1)} %refs_3_.1), channel_id=1, source_target_pairs={{0,16},{2,18},{4,20},{6,22},{8,24},{10,26},{12,28},{14,30},{16,0},... | collective-permute-start | bytes 73736 | tf_op jit(solution)/shard_map/ppermute | solution.py:287
  4.1 1.9 %shard_map.100 = (bf16[1536,768]{1,0:T(8,128)(2,1)S(1)}, bf16[512,512]{1,0:T(8,128)(2,1)S(1)}, f32[1536]{0:T(1024)S(1)}, bf16[8,1536]{1,0:T(8,128)(2,1)S(1)}) custom-call(bf16[1536,768]{1,0:T(8,128)(2,1)} %refs_0_.2, bf16[512,512]{1,0:T(8,128)(2,1)} %bitcast.6, f32[1536]{0:T(1024)} %refs_2_.1, bf16[8,1536]{1,0:T(8,128)(2,1)} %refs_3_.1), custom_call_target="tpu_custom_call" | custom-call | bytes 5822464 | tf_op jit(solution)/shard_map/pallas_call | solution.py:65
  6.0 0.1 collective-permute-done
  6.1 0.0 copy-start.2
  6.1 0.0 copy-start.3
  6.1 0.0 copy-start.4
  6.1 2.9 %collective-permute-start.3 = (bf16[16,1536]{1,0:T(8,128)(2,1)S(1)}, bf16[16,1536]{1,0:T(8,128)(2,1)S(1)}, u32[]{:S(2)}, u32[]{:S(2)}) collective-permute-start(bf16[16,1536]{1,0:T(8,128)(2,1)S(1)} %constant_dynamic-update-slice_fusion.refs_0_), channel_id=1, source_target_pairs={{0,12},{2,14},{4,8},{6,10},{8,4},{10,6},{12,0},{14,2},{16,28},{18,... | collective-permute-start | bytes 147464 | tf_op jit(solution)/shard_map/ppermute | solution.py:287
  9.1 0.5 collective-permute-start.2
  9.6 0.1 collective-permute-start.1
  9.7 0.0 collective-permute-start.4
  9.7 1.6 %collective-permute-done.3.refs_3_ = bf16[16,1536]{1,0:T(8,128)(2,1)S(1)} collective-permute-done((bf16[16,1536]{1,0:T(8,128)(2,1)S(1)}, bf16[16,1536]{1,0:T(8,128)(2,1)S(1)}, u32[]{:S(2)}, u32[]{:S(2)}) %collective-permute-start.3) | collective-permute-done | bytes 49184 | tf_op jit(solution)/shard_map/ppermute | solution.py:287
  11.3 1.8 %collective-permute-done.2.refs_2_ = bf16[16,1536]{1,0:T(8,128)(2,1)S(1)} collective-permute-done((bf16[16,1536]{1,0:T(8,128)(2,1)S(1)}, bf16[16,1536]{1,0:T(8,128)(2,1)S(1)}, u32[]{:S(2)}, u32[]{:S(2)}) %collective-permute-start.2) | collective-permute-done | bytes 49184 | tf_op jit(solution)/shard_map/ppermute | solution.py:287
  13.2 0.5 collective-permute-done.1.refs_1_
  13.7 0.0 collective-permute-start.5
  13.7 0.0 collective-permute-done.4.refs_4_
  13.7 0.7 collective-permute-done.6.refs_6_
  14.4 0.5 collective-permute-done.5.refs_5_
  14.9 1.0 query.1
  15.9 22.1 %all_to_all.15.q_ref = bf16[16,144,128]{2,1,0:T(8,128)(2,1)S(1)} all-to-all(bf16[16,144,128]{2,1,0:T(8,128)(2,1)S(1)} %query.1), channel_id=1, replica_groups=mesh['groups'=1,'tensor'=16,'replica'=2] {'tensor'}, dimensions={0} | all-to-all | bytes 1179648 | tf_op jit(solution)/shard_map/all_to_all | solution.py:334
  38.0 0.1 collective-permute-start.8
  38.1 2.9 %attend.1 = bf16[16,32,512]{2,1,0:T(8,128)(2,1)S(1)} custom-call(s32[2]{0:T(128)S(1)} %copy-done.3, s32[2]{0:T(128)S(1)} %copy-done.4, bf16[16,144,128]{2,1,0:T(8,128)(2,1)S(1)} %all_to_all.15.q_ref, f32[1,128]{1,0:T(1,128)S(1)} %fusion.3.frequency_ref, bf16[8,576]{1,0:T(8,128)(2,1)S(1)} %copy-done.2, bf16[2,576,1024]{2,1,0:T(8,128)(2,1)S(1)} %bitcast.5), custom_call_target="tpu_custom_call" | custom-call | tf_op jit(solution)/shard_map/attend/pallas_call | solution.py:344
  41.0 17.1 %all_to_all.16.latent_ref = bf16[16,32,512]{2,1,0:T(8,128)(2,1)S(1)} all-to-all(bf16[16,32,512]{2,1,0:T(8,128)(2,1)S(1)} %attend.1), channel_id=1, replica_groups=mesh['groups'=1,'tensor'=16,'replica'=2] {'tensor'}, dimensions={0} | all-to-all | bytes 1048576 | tf_op jit(solution)/shard_map/all_to_all | solution.py:352
  58.1 0.4 values.1.refs_1_
  58.5 1.6 %collective-permute-start.9 = (bf16[128,512]{1,0:T(8,128)(2,1)S(1)}, bf16[128,512]{1,0:T(8,128)(2,1)S(1)}, u32[]{:S(2)}, u32[]{:S(2)}) collective-permute-start(bf16[128,512]{1,0:T(8,128)(2,1)S(1)} %values.1.refs_1_), channel_id=1, source_target_pairs={{0,1},{1,0},{2,3},{3,2},{4,5},{5,4},{6,7},{7,6},{8,9},{9,8},{10,11... | collective-permute-start | bytes 393224 | tf_op jit(solution)/shard_map/ppermute | solution.py:287
  60.1 4.1 %collective-permute-done.9.refs_1_ = bf16[128,512]{1,0:T(8,128)(2,1)S(1)} collective-permute-done((bf16[128,512]{1,0:T(8,128)(2,1)S(1)}, bf16[128,512]{1,0:T(8,128)(2,1)S(1)}, u32[]{:S(2)}, u32[]{:S(2)}) %collective-permute-start.9) | collective-permute-done | bytes 131104 | tf_op jit(solution)/shard_map/ppermute | solution.py:287
  64.1 2.1 %near_output.1 = (bf16[512,1792]{1,0:T(8,128)(2,1)S(1)}, bf16[512,1792]{1,0:T(8,128)(2,1)S(1)}) custom-call(s32[1]{0:T(128)} %bitcast.place_ref, bf16[512,3584]{1,0:T(8,128)(2,1)} %refs_0_.3, bf16[512,3584]{1,0:T(8,128)(2,1)} %copy-done.6), custom_call_target="tpu_custom_call" | custom-call | bytes 7340032 | tf_op jit(solution)/shard_map/near_output/pallas_call | solution.py:93
  66.2 0.4 half_product.3.partial_ref
  66.6 0.4 half_product.2.partial_ref
  67.0 0.4 output.2.refs_0_
  67.5 0.4 output.3
  67.9 28.6 %all_to_all.17.x_ref = bf16[32,8,1792]{2,1,0:T(8,128)(2,1)S(1)} all-to-all(bf16[32,8,1792]{2,1,0:T(8,128)(2,1)S(1)} %bitcast.4), channel_id=1, replica_groups=mesh['groups'=1,'tensor'=16,'replica'=2] {'replica','tensor'}, dimensions={0} | all-to-all | bytes 1835008 | tf_op jit(solution)/shard_map/all_to_all | solution.py:375
  96.5 0.8 combine.1
  (22 shorter events, 0.1 us)
Async XLA Ops:
  0.0 6.1 %collective-permute-start = (bf16[8,1536]{1,0:T(8,128)(2,1)}, bf16[8,1536]{1,0:T(8,128)(2,1)S(1)}, u32[]{:S(2)}, u32[]{:S(2)}) collective-permute-start(bf16[8,1536]{1,0:T(8,128)(2,1)} %refs_3_.1), channel_id=1, source_target_pairs={{0,16},{2,18},{4,20},{6,22},{8,24},{10,26},{12,28},{14,30},{16,0},... | collective-permute-start | bytes 73736 | tf_op jit(solution)/shard_map/ppermute | solution.py:287
  4.1 33.9 %copy-start.5 = (bf16[512,3584]{1,0:T(8,128)(2,1)S(1)}, bf16[512,3584]{1,0:T(8,128)(2,1)}, u32[]{:S(2)}) copy-start(bf16[512,3584]{1,0:T(8,128)(2,1)} %refs_0_.3) | copy-start | bytes 11010052
  6.1 32.0 %copy-start = (bf16[2,1024,576]{1,2,0:T(8,128)(2,1)S(1)}, bf16[2,1024,576]{1,2,0:T(8,128)(2,1)}, u32[]{:S(2)}) copy-start(bf16[2,1024,576]{1,2,0:T(8,128)(2,1)} %param.17) | copy-start | bytes 7077892
  6.1 32.0 %copy-start.2 = (bf16[8,576]{1,0:T(8,128)(2,1)S(1)}, bf16[8,576]{1,0:T(8,128)(2,1)}, u32[]{:S(2)}) copy-start(bf16[8,576]{1,0:T(8,128)(2,1)} %new_ref.1) | copy-start | bytes 27652
  6.1 32.0 %copy-start.3 = (s32[2]{0:T(128)S(1)}, s32[2]{0:T(128)}, u32[]{:S(2)}) copy-start(s32[2]{0:T(128)} %len_ref.1) | copy-start | bytes 28
  6.1 32.0 %copy-start.4 = (s32[2]{0:T(128)S(1)}, s32[2]{0:T(128)}, u32[]{:S(2)}) copy-start(s32[2]{0:T(128)} %count_ref.1) | copy-start | bytes 28
  6.1 5.2 %collective-permute-start.3 = (bf16[16,1536]{1,0:T(8,128)(2,1)S(1)}, bf16[16,1536]{1,0:T(8,128)(2,1)S(1)}, u32[]{:S(2)}, u32[]{:S(2)}) collective-permute-start(bf16[16,1536]{1,0:T(8,128)(2,1)S(1)} %constant_dynamic-update-slice_fusion.refs_0_), channel_id=1, source_target_pairs={{0,12},{2,14},{4,8},{6,10},{8,4},{10,6},{12,0},{14,2},{16,28},{18,... | collective-permute-start | bytes 147464 | tf_op jit(solution)/shard_map/ppermute | solution.py:287
  9.1 4.1 %collective-permute-start.2 = (bf16[16,1536]{1,0:T(8,128)(2,1)S(1)}, bf16[16,1536]{1,0:T(8,128)(2,1)S(1)}, u32[]{:S(2)}, u32[]{:S(2)}) collective-permute-start(bf16[16,1536]{1,0:T(8,128)(2,1)S(1)} %constant_dynamic-update-slice_fusion.refs_0_), channel_id=1, source_target_pairs={{0,4},{2,6},{4,0},{6,2},{8,12},{10,14},{12,8},{14,10},{16,20},{18,... | collective-permute-start | bytes 147464 | tf_op jit(solution)/shard_map/ppermute | solution.py:287
  9.6 4.1 %collective-permute-start.1 = (bf16[16,1536]{1,0:T(8,128)(2,1)S(1)}, bf16[16,1536]{1,0:T(8,128)(2,1)S(1)}, u32[]{:S(2)}, u32[]{:S(2)}) collective-permute-start(bf16[16,1536]{1,0:T(8,128)(2,1)S(1)} %constant_dynamic-update-slice_fusion.refs_0_), channel_id=1, source_target_pairs={{0,8},{2,10},{4,12},{6,14},{8,0},{10,2},{12,4},{14,6},{16,24},{18,... | collective-permute-start | bytes 147464 | tf_op jit(solution)/shard_map/ppermute | solution.py:287
  9.7 4.0 %collective-permute-start.4 = (bf16[16,1536]{1,0:T(8,128)(2,1)S(1)}, bf16[16,1536]{1,0:T(8,128)(2,1)S(1)}, u32[]{:S(2)}, u32[]{:S(2)}) collective-permute-start(bf16[16,1536]{1,0:T(8,128)(2,1)S(1)} %constant_dynamic-update-slice_fusion.refs_0_), channel_id=1, source_target_pairs={{0,2},{2,0},{4,6},{6,4},{8,10},{10,8},{12,14},{14,12},{16,18},{18,... | collective-permute-start | bytes 147464 | tf_op jit(solution)/shard_map/ppermute | solution.py:287
  11.3 2.4 %collective-permute-start.7 = (bf16[16,1536]{1,0:T(8,128)(2,1)S(1)}, bf16[16,1536]{1,0:T(8,128)(2,1)S(1)}, u32[]{:S(2)}, u32[]{:S(2)}) collective-permute-start(bf16[16,1536]{1,0:T(8,128)(2,1)S(1)} %collective-permute-done.3.refs_3_), channel_id=1, source_target_pairs={{0,2},{2,0},{4,6},{6,4},{8,10},{10,8},{12,14},{14,12},{16,18},{18,... | collective-permute-start | bytes 147464 | tf_op jit(solution)/shard_map/ppermute | solution.py:287
  13.1 1.2 %collective-permute-start.6 = (bf16[16,1536]{1,0:T(8,128)(2,1)S(1)}, bf16[16,1536]{1,0:T(8,128)(2,1)S(1)}, u32[]{:S(2)}, u32[]{:S(2)}) collective-permute-start(bf16[16,1536]{1,0:T(8,128)(2,1)S(1)} %collective-permute-done.2.refs_2_), channel_id=1, source_target_pairs={{0,2},{2,0},{4,6},{6,4},{8,10},{10,8},{12,14},{14,12},{16,18},{18,... | collective-permute-start | bytes 147464 | tf_op jit(solution)/shard_map/ppermute | solution.py:287
  13.7 1.2 %collective-permute-start.5 = (bf16[16,1536]{1,0:T(8,128)(2,1)S(1)}, bf16[16,1536]{1,0:T(8,128)(2,1)S(1)}, u32[]{:S(2)}, u32[]{:S(2)}) collective-permute-start(bf16[16,1536]{1,0:T(8,128)(2,1)S(1)} %collective-permute-done.1.refs_1_), channel_id=1, source_target_pairs={{0,2},{2,0},{4,6},{6,4},{8,10},{10,8},{12,14},{14,12},{16,18},{18,... | collective-permute-start | bytes 147464 | tf_op jit(solution)/shard_map/ppermute | solution.py:287
  38.0 20.2 %copy-start.1 = (bf16[4,512,128]{2,1,0:T(8,128)(2,1)S(1)}, bf16[4,512,128]{2,1,0:T(8,128)(2,1)}, u32[]{:S(2)}) copy-start(bf16[4,512,128]{2,1,0:T(8,128)(2,1)} %uv_ref.1) | copy-start | bytes 1572868
  38.0 20.2 %collective-permute-start.8 = (bf16[512,3584]{1,0:T(8,128)(2,1)S(1)}, bf16[512,3584]{1,0:T(8,128)(2,1)S(1)}, u32[]{:S(2)}, u32[]{:S(2)}) collective-permute-start(bf16[512,3584]{1,0:T(8,128)(2,1)S(1)} %copy-done.5), channel_id=1, source_target_pairs={{0,2},{2,0},{4,6},{6,4},{8,10},{10,8},{12,14},{14,12},{16,18},{18,... | collective-permute-start | bytes 11010056 | tf_op jit(solution)/shard_map/ppermute | solution.py:287
  58.1 6.0 %copy-start.6 = (bf16[512,3584]{1,0:T(8,128)(2,1)}, bf16[512,3584]{1,0:T(8,128)(2,1)S(1)}, u32[]{:S(2)}) copy-start(bf16[512,3584]{1,0:T(8,128)(2,1)S(1)} %collective-permute-done.8.refs_1_) | copy-start | bytes 11010052
  58.5 5.6 %collective-permute-start.9 = (bf16[128,512]{1,0:T(8,128)(2,1)S(1)}, bf16[128,512]{1,0:T(8,128)(2,1)S(1)}, u32[]{:S(2)}, u32[]{:S(2)}) collective-permute-start(bf16[128,512]{1,0:T(8,128)(2,1)S(1)} %values.1.refs_1_), channel_id=1, source_target_pairs={{0,1},{1,0},{2,3},{3,2},{4,5},{5,4},{6,7},{7,6},{8,9},{9,8},{10,11... | collective-permute-start | bytes 393224 | tf_op jit(solution)/shard_map/ppermute | solution.py:287
  60.1 7.0 %collective-permute-start.10 = (bf16[128,512]{1,0:T(8,128)(2,1)S(1)}, bf16[128,512]{1,0:T(8,128)(2,1)S(1)}, u32[]{:S(2)}, u32[]{:S(2)}) collective-permute-start(bf16[128,512]{1,0:T(8,128)(2,1)S(1)} %values.1.refs_1_), channel_id=1, source_target_pairs={{0,2},{2,0},{4,6},{6,4},{8,10},{10,8},{12,14},{14,12},{16,18},{18,... | collective-permute-start | bytes 393224 | tf_op jit(solution)/shard_map/ppermute | solution.py:287
  64.1 3.3 %collective-permute-start.11 = (bf16[128,512]{1,0:T(8,128)(2,1)S(1)}, bf16[128,512]{1,0:T(8,128)(2,1)S(1)}, u32[]{:S(2)}, u32[]{:S(2)}) collective-permute-start(bf16[128,512]{1,0:T(8,128)(2,1)S(1)} %collective-permute-done.9.refs_1_), channel_id=1, source_target_pairs={{0,2},{2,0},{4,6},{6,4},{8,10},{10,8},{12,14},{14,12},{16,18},{18,... | collective-permute-start | bytes 393224 | tf_op jit(solution)/shard_map/ppermute | solution.py:287
